TPU v7x, 32 devices: a whole 2x2x4 slice. The times are simulated.
32 devices in a mesh: head: 4 (over x, core), blk: 8 (over z, y).
Axes of the slice: x: 2, y: 2, z: 4, core: 2. Of those that a mesh axis runs over, the one named last changes fastest.
Arguments:
- inputs: bfloat16 [4096, 512], P(('blk', 'head')), may hold values from -6 to 6
- ln1_gain: bfloat16 [512], P('blk'), may hold values from 0.5 to 1.5
- w_qkv: bfloat16 [512, 1536], P('blk'), may hold values from -0.25 to 0.25
- w_out: bfloat16 [512, 512], P('blk'), may hold values from -2 to 2
- ln2_gain: bfloat16 [512], P('blk'), may hold values from 0.5 to 1.5
- w_router: bfloat16 [512, 8], P('blk'), may hold values from -0.25 to 0.25
- expert_in: bfloat16 [8, 512, 2048], P('blk'), may hold values from -0.25 to 0.25
- expert_out: bfloat16 [8, 2048, 512], P('blk'), may hold values from -2 to 2
- routes: int32 [4096, 2], P(('blk', 'head')), may hold values from 0 to 7, all different within a row
- priority: int32 [32, 128], P(('blk', 'head')), may hold values from 0 to 127, each once within a row
- doc_lengths: int32 [16], replicated, may hold values from 1 to 2048, 4096 in all
- d_out: float32 [4096, 512], P(('blk', 'head')), may hold values from -6 to 6
Outputs:
- output: bfloat16 [4096, 512], P(('blk', 'head'))
- d_inputs: float32 [4096, 512], P(('blk', 'head'))
- d_ln1_gain: float32 [512], P('blk')
- d_w_qkv: float32 [512, 1536], P('blk')
- d_w_out: float32 [512, 512], P('blk')
- d_ln2_gain: float32 [512], P('blk')
- d_w_router: float32 [512, 8], P('blk')
- d_expert_in: float32 [8, 512, 2048], P('blk')
- d_expert_out: float32 [8, 2048, 512], P('blk')
Inputs may be any that keep to these rules, and one draw needn't show every extreme that they name: `routes`: each token names two different experts. `priority`: each row holds every rank from 0 to 127 once. `doc_lengths`: the documents' lengths sum to 4096; the longest has exactly 2048 tokens.
All inputs are finite; a program needn't handle non-finite values.
Results may differ from a plain program's by a relative error of at most 0.022.
Values may be sent and summed in bfloat16 or wider, within the bound.
A program may use at most 128 MiB of HBM per device.

v0:
```python
import jax
import jax.numpy as jnp
from jax import lax
from jax.sharding import PartitionSpec as P

HS = 64
KEY_BLOCK = 2048


PRECISE = lax.Precision.HIGHEST
MASKED = -1e30
EPSILON = 1e-06


def layer_norm(values, gain):
    average = jnp.mean(values, axis=-1, keepdims=True)
    centred = values - average
    spread = jnp.mean(centred * centred, axis=-1, keepdims=True)
    return centred * lax.rsqrt(spread + EPSILON) * gain


def gelu_exact(values):
    return jax.nn.gelu(values, approximate=False)


def router(row_block, weight):
    return jax.nn.softmax(jnp.dot(row_block, weight, precision=PRECISE), axis=-1)


def doc_index(positions, doc_lengths):
    starts = jnp.cumsum(doc_lengths) - doc_lengths
    at_most = (starts[None, :] <= positions[:, None]).astype(jnp.int32)
    return jnp.sum(at_most, axis=1) - 1


def slot_table(route_rows, ranking, capacity):
    token_count = route_rows.shape[0]
    expert = jnp.transpose(route_rows).reshape(-1)
    pair_order = (jnp.arange(2, dtype=jnp.int32)[:, None] * token_count + ranking[None, :]).reshape(
        -1
    )
    before = (expert[:, None] == expert[None, :]) & (pair_order[None, :] < pair_order[:, None])
    position = jnp.sum(before.astype(jnp.int32), axis=1)
    slot_ids = jnp.where(position < capacity, expert * capacity + position, -1)
    return slot_ids.reshape(2, token_count)


def keep_state(current):
    return current


def local(
    inputs,
    ln1_gain,
    w_qkv,
    w_out,
    ln2_gain,
    w_router,
    expert_in,
    expert_out,
    routes,
    priority,
    doc_lengths,
    d_out,
):
    blk_size = lax.axis_size("blk")
    tok_rows = inputs.shape[0]
    model_width = inputs.shape[1]
    capacity = 2 * tok_rows // blk_size
    slot_total = blk_size * capacity
    gain_one, qkv_weight, out_weight, gain_two, router_weight = (
        lax.all_gather(ln1_gain, "blk", axis=0, tiled=True),
        lax.all_gather(w_qkv, "blk", axis=0, tiled=True),
        lax.all_gather(w_out, "blk", axis=0, tiled=True),
        lax.all_gather(ln2_gain, "blk", axis=0, tiled=True),
        lax.all_gather(w_router, "blk", axis=0, tiled=True),
    )
    input_rows = inputs.astype(jnp.float32)
    normed_one, norm_one_pull = jax.vjp(layer_norm, input_rows, gain_one.astype(jnp.float32))
    normed_low = normed_one.astype(jnp.bfloat16)
    qkv_rows = jnp.dot(normed_low, qkv_weight, preferred_element_type=jnp.float32).astype(
        jnp.bfloat16
    )
    query_heads, key_heads, value_heads = (
        lax.all_to_all(qkv_rows[:, :model_width], "head", split_axis=1, concat_axis=0, tiled=True),
        lax.all_to_all(
            qkv_rows[:, model_width : 2 * model_width],
            "head",
            split_axis=1,
            concat_axis=0,
            tiled=True,
        ),
        lax.all_to_all(
            qkv_rows[:, 2 * model_width :], "head", split_axis=1, concat_axis=0, tiled=True
        ),
    )
    span_rows = query_heads.shape[0]
    head_count = query_heads.shape[1] // HS
    key_all, value_all = (
        lax.all_gather(key_heads, "blk", axis=0, tiled=True),
        lax.all_gather(value_heads, "blk", axis=0, tiled=True),
    )
    total_rows = key_all.shape[0]
    block_count = total_rows // KEY_BLOCK
    scale_factor = HS ** (-0.5)
    query_pos = lax.axis_index("blk") * span_rows + jnp.arange(span_rows, dtype=jnp.int32)
    query_docs = doc_index(query_pos, doc_lengths)
    queries = query_heads.reshape(span_rows, head_count, HS)

    def block_parts(block_index, key_source, value_source):
        first_key = block_index * KEY_BLOCK
        key_rows = lax.dynamic_slice_in_dim(key_source, first_key, KEY_BLOCK, 0).reshape(
            KEY_BLOCK, head_count, HS
        )
        value_rows = lax.dynamic_slice_in_dim(value_source, first_key, KEY_BLOCK, 0).reshape(
            KEY_BLOCK, head_count, HS
        )
        key_docs = doc_index(first_key + jnp.arange(KEY_BLOCK, dtype=jnp.int32), doc_lengths)
        is_live = (key_docs[0] <= query_docs[-1]) & (key_docs[-1] >= query_docs[0])
        same_doc = query_docs[:, None] == key_docs[None, :]
        return (first_key, key_rows, value_rows, same_doc, is_live)

    def block_scores(key_rows, same_doc):
        raw_scores = (
            jnp.einsum("qhd,khd->hqk", queries, key_rows, preferred_element_type=jnp.float32)
            * scale_factor
        )
        return jnp.where(same_doc[None], raw_scores, MASKED)

    def stat_step(block_index, loop_state):
        first_key, key_rows, value_rows, same_doc, is_live = block_parts(
            block_index, key_all, value_all
        )

        def stat_update(current):
            running_max, running_sum = current
            scores = block_scores(key_rows, same_doc)
            new_max = jnp.maximum(running_max, jnp.max(scores, axis=2))
            exp_terms = jnp.where(same_doc[None], jnp.exp(scores - new_max[:, :, None]), 0.0)
            return (
                new_max,
                running_sum * jnp.exp(running_max - new_max) + jnp.sum(exp_terms, axis=2),
            )

        return lax.cond(is_live, stat_update, keep_state, loop_state)

    start_state = (
        jnp.full((head_count, span_rows), MASKED, jnp.float32),
        jnp.zeros((head_count, span_rows), jnp.float32),
    )
    running_max, running_sum = lax.fori_loop(0, block_count, stat_step, start_state)
    log_total = running_max + jnp.log(running_sum)

    def out_step(block_index, loop_state):
        first_key, key_rows, value_rows, same_doc, is_live = block_parts(
            block_index, key_all, value_all
        )

        def out_update(current):
            scores = block_scores(key_rows, same_doc)
            weights = jnp.where(
                same_doc[None], jnp.exp(scores - log_total[:, :, None]), 0.0
            ).astype(jnp.bfloat16)
            return current + jnp.einsum(
                "hqk,khd->qhd", weights, value_rows, preferred_element_type=jnp.float32
            )

        return lax.cond(is_live, out_update, keep_state, loop_state)

    mixed_full = lax.fori_loop(
        0, block_count, out_step, jnp.zeros((span_rows, head_count, HS), jnp.float32)
    )
    mixed_low = mixed_full.reshape(span_rows, head_count * HS).astype(jnp.bfloat16)
    mixed_tokens = lax.all_to_all(mixed_low, "head", split_axis=0, concat_axis=1, tiled=True)
    attended = jnp.dot(mixed_tokens, out_weight, preferred_element_type=jnp.float32)
    hidden_one = input_rows + attended
    normed_two, norm_two_pull = jax.vjp(layer_norm, hidden_one, gain_two.astype(jnp.float32))
    routed_low = normed_two.astype(jnp.bfloat16)
    router_probs, router_pull = jax.vjp(
        router, routed_low.astype(jnp.float32), router_weight.astype(jnp.float32)
    )
    slot_ids = slot_table(routes, priority[0], capacity)
    select = (
        slot_ids[:, :, None] == jnp.arange(slot_total, dtype=jnp.int32)[None, None, :]
    ).astype(jnp.bfloat16)
    send_rows = jnp.einsum(
        "kts,td->sd", select, routed_low, preferred_element_type=jnp.float32
    ).astype(jnp.bfloat16)
    expert_rows = lax.all_to_all(
        send_rows.reshape(blk_size, capacity, model_width),
        "blk",
        split_axis=0,
        concat_axis=0,
        tiled=True,
    ).reshape(slot_total, model_width)
    weight_in = expert_in[0]
    weight_out = expert_out[0]
    pre_act = jnp.dot(expert_rows, weight_in, preferred_element_type=jnp.float32)
    hidden_act, gelu_pull = jax.vjp(gelu_exact, pre_act)
    hidden_low = hidden_act.astype(jnp.bfloat16)
    expert_result = jnp.dot(hidden_low, weight_out, preferred_element_type=jnp.float32).astype(
        jnp.bfloat16
    )
    slot_result = lax.all_to_all(
        expert_result.reshape(blk_size, capacity, model_width),
        "blk",
        split_axis=0,
        concat_axis=0,
        tiled=True,
    ).reshape(slot_total, model_width)
    pair_result = jnp.einsum("kts,sd->ktd", select, slot_result, preferred_element_type=jnp.float32)
    route_hot = (routes[:, :, None] == jnp.arange(blk_size, dtype=jnp.int32)[None, None, :]).astype(
        jnp.float32
    )
    gate_vals = jnp.sum(router_probs[:, None, :] * route_hot, axis=2)
    mixture = gate_vals[:, 0, None] * pair_result[0] + gate_vals[:, 1, None] * pair_result[1]
    output = (hidden_one + mixture).astype(jnp.bfloat16)
    d_gates = jnp.transpose(jnp.sum(d_out[None] * pair_result, axis=2))
    d_probs = jnp.sum(d_gates[:, :, None] * route_hot, axis=1)
    pair_grads = (jnp.transpose(gate_vals)[:, :, None] * d_out[None]).astype(jnp.bfloat16)
    slot_grads = jnp.einsum(
        "kts,ktd->sd", select, pair_grads, preferred_element_type=jnp.float32
    ).astype(jnp.bfloat16)
    result_grads = lax.all_to_all(
        slot_grads.reshape(blk_size, capacity, model_width),
        "blk",
        split_axis=0,
        concat_axis=0,
        tiled=True,
    ).reshape(slot_total, model_width)
    d_hidden_act = jnp.dot(result_grads, weight_out.T, preferred_element_type=jnp.float32)
    d_weight_out = jnp.dot(hidden_low.T, result_grads, preferred_element_type=jnp.float32)
    d_preact = gelu_pull(d_hidden_act)[0].astype(jnp.bfloat16)
    d_weight_in = jnp.dot(expert_rows.T, d_preact, preferred_element_type=jnp.float32)
    row_grads = jnp.dot(d_preact, weight_in.T, preferred_element_type=jnp.float32).astype(
        jnp.bfloat16
    )
    slot_back = lax.all_to_all(
        row_grads.reshape(blk_size, capacity, model_width),
        "blk",
        split_axis=0,
        concat_axis=0,
        tiled=True,
    ).reshape(slot_total, model_width)
    d_routed = jnp.einsum("kts,sd->td", select, slot_back, preferred_element_type=jnp.float32)
    d_routed_router, d_router = router_pull(d_probs)
    d_hidden_norm, d_gain_two = norm_two_pull(d_routed + d_routed_router)
    d_hidden_one = d_out + d_hidden_norm
    attn_grads = d_hidden_one.astype(jnp.bfloat16)
    d_out_weight = jnp.dot(mixed_tokens.T, attn_grads, preferred_element_type=jnp.float32)
    mixed_grads = jnp.dot(attn_grads, out_weight.T, preferred_element_type=jnp.float32).astype(
        jnp.bfloat16
    )
    head_grads = lax.all_to_all(mixed_grads, "head", split_axis=1, concat_axis=0, tiled=True)
    out_grads = head_grads.reshape(span_rows, head_count, HS)
    row_delta = jnp.transpose(jnp.sum(out_grads.astype(jnp.float32) * mixed_full, axis=2))
    key_back, value_back = (
        lax.all_gather(key_heads, "blk", axis=0, tiled=True),
        lax.all_gather(value_heads, "blk", axis=0, tiled=True),
    )

    def grad_step(block_index, loop_state):
        first_key, key_rows, value_rows, same_doc, is_live = block_parts(
            block_index, key_back, value_back
        )

        def grad_update(current):
            query_grad, key_grad, value_grad = current
            scores = block_scores(key_rows, same_doc)
            weights = jnp.where(same_doc[None], jnp.exp(scores - log_total[:, :, None]), 0.0)
            value_part = jnp.einsum(
                "hqk,qhd->khd",
                weights.astype(jnp.bfloat16),
                out_grads,
                preferred_element_type=jnp.float32,
            )
            weight_grads = jnp.einsum(
                "qhd,khd->hqk", out_grads, value_rows, preferred_element_type=jnp.float32
            )
            score_grads = (weights * (weight_grads - row_delta[:, :, None])).astype(jnp.bfloat16)
            query_grad = (
                query_grad
                + jnp.einsum(
                    "hqk,khd->qhd", score_grads, key_rows, preferred_element_type=jnp.float32
                )
                * scale_factor
            )
            key_part = (
                jnp.einsum("hqk,qhd->khd", score_grads, queries, preferred_element_type=jnp.float32)
                * scale_factor
            )
            key_grad = lax.dynamic_update_slice_in_dim(
                key_grad, key_part.reshape(KEY_BLOCK, head_count * HS), first_key, 0
            )
            value_grad = lax.dynamic_update_slice_in_dim(
                value_grad, value_part.reshape(KEY_BLOCK, head_count * HS), first_key, 0
            )
            return (query_grad, key_grad, value_grad)

        return lax.cond(is_live, grad_update, keep_state, loop_state)

    start_grads = (
        jnp.zeros((span_rows, head_count, HS), jnp.float32),
        jnp.zeros((total_rows, head_count * HS), jnp.float32),
        jnp.zeros((total_rows, head_count * HS), jnp.float32),
    )
    query_grad, key_grad, value_grad = lax.fori_loop(0, block_count, grad_step, start_grads)
    key_own, value_own = (
        lax.psum_scatter(
            key_grad.astype(jnp.bfloat16), "blk", scatter_dimension=0, tiled=True
        ).astype(jnp.float32),
        lax.psum_scatter(
            value_grad.astype(jnp.bfloat16), "blk", scatter_dimension=0, tiled=True
        ).astype(jnp.float32),
    )
    query_tokens_grad, key_tokens_grad, value_tokens_grad = (
        lax.all_to_all(
            query_grad.reshape(span_rows, head_count * HS).astype(jnp.bfloat16),
            "head",
            split_axis=0,
            concat_axis=1,
            tiled=True,
        ),
        lax.all_to_all(
            key_own.astype(jnp.bfloat16), "head", split_axis=0, concat_axis=1, tiled=True
        ),
        lax.all_to_all(
            value_own.astype(jnp.bfloat16), "head", split_axis=0, concat_axis=1, tiled=True
        ),
    )
    qkv_grads = jnp.concatenate([query_tokens_grad, key_tokens_grad, value_tokens_grad], axis=1)
    d_qkv_weight = jnp.dot(normed_low.T, qkv_grads, preferred_element_type=jnp.float32)
    normed_grads = jnp.dot(qkv_grads, qkv_weight.T, preferred_element_type=jnp.float32)
    d_inputs_norm, d_gain_one = norm_one_pull(normed_grads)
    d_inputs = d_hidden_one + d_inputs_norm
    gain_one_sum, qkv_sum, out_sum, gain_two_sum, router_sum = (
        lax.psum_scatter(
            d_gain_one.astype(jnp.bfloat16), "blk", scatter_dimension=0, tiled=True
        ).astype(jnp.float32),
        lax.psum_scatter(
            d_qkv_weight.astype(jnp.bfloat16), "blk", scatter_dimension=0, tiled=True
        ).astype(jnp.float32),
        lax.psum_scatter(
            d_out_weight.astype(jnp.bfloat16), "blk", scatter_dimension=0, tiled=True
        ).astype(jnp.float32),
        lax.psum_scatter(
            d_gain_two.astype(jnp.bfloat16), "blk", scatter_dimension=0, tiled=True
        ).astype(jnp.float32),
        lax.psum_scatter(
            d_router.astype(jnp.bfloat16), "blk", scatter_dimension=0, tiled=True
        ).astype(jnp.float32),
    )
    gain_one_all, qkv_all, out_all, gain_two_all, router_all, expert_in_all, expert_out_all = (
        lax.psum(gain_one_sum.astype(jnp.bfloat16), "head").astype(jnp.float32),
        lax.psum(qkv_sum.astype(jnp.bfloat16), "head").astype(jnp.float32),
        lax.psum(out_sum.astype(jnp.bfloat16), "head").astype(jnp.float32),
        lax.psum(gain_two_sum.astype(jnp.bfloat16), "head").astype(jnp.float32),
        lax.psum(router_sum.astype(jnp.bfloat16), "head").astype(jnp.float32),
        lax.psum(d_weight_in[None].astype(jnp.bfloat16), "head").astype(jnp.float32),
        lax.psum(d_weight_out[None].astype(jnp.bfloat16), "head").astype(jnp.float32),
    )
    return (
        output,
        d_inputs,
        gain_one_all,
        qkv_all,
        out_all,
        gain_two_all,
        router_all,
        expert_in_all,
        expert_out_all,
    )


def solution(mesh):
    in_specs = (
        P(("blk", "head"), None),
        P("blk"),
        P("blk", None),
        P("blk", None),
        P("blk"),
        P("blk", None),
        P("blk", None, None),
        P("blk", None, None),
        P(("blk", "head"), None),
        P(("blk", "head"), None),
        P(),
        P(("blk", "head"), None),
    )
    out_specs = (
        P(("blk", "head"), None),
        P(("blk", "head"), None),
        P("blk"),
        P("blk", None),
        P("blk", None),
        P("blk"),
        P("blk", None),
        P("blk", None, None),
        P("blk", None, None),
    )
    return jax.shard_map(local, mesh=mesh, in_specs=in_specs, out_specs=out_specs, check_vma=False)
```

profile of v0, /device:TPU:0, one launch (start us, length us, event | category | flops | bytes accessed | tf_op | source)
XLA Modules:
  0.0 760.1 jit_solution(12568574816553132908)
XLA Ops:
  11.8 23.2 %all-reduce.5 = (bf16[512]{0:T(512)(128)(2,1)S(1)}, bf16[512]{0:T(512)(128)(2,1)S(1)}) all-reduce(bf16[512]{0:T(512)(128)(2,1)S(1)} %dynamic-update-slice, bf16[512]{0:T(512)(128)(2,1)S(1)} %dynamic-update-slice.1), channel_id=1, replica_groups=mesh['head'=4,'blk'=8] {'blk'}, use_global_device_ids=true, to_apply=%add | all-reduce | flops 1024 | bytes 4096
  37.1 19.9 %all-gather.5.cloned.1.call-done = bf16[512,1536]{1,0:T(8,128)(2,1)} async-done(((bf16[64,1536]{1,0:T(8,128)(2,1)}), bf16[512,1536]{1,0:T(8,128)(2,1)}) %all-gather.5.cloned.1.call-update) | async-done | bytes 1572880 | tf_op jit(solution)/shard_map/all_gather | solution.py:73
  59.0 7.2 all_to_all.160
  69.2 3.3 all-to-all-start.2
  72.6 4.5 all-to-all-done.2
  78.1 33.9 %all_gather.27 = bf16[512,512]{1,0:T(8,128)(2,1)} all-gather(bf16[64,512]{1,0:T(8,128)(2,1)S(1)} %copy-done.31), channel_id=1, replica_groups=mesh['head'=4,'blk'=8] {'blk'}, dimensions={0}, use_global_device_ids=true | all-gather | bytes 589824 | tf_op jit(solution)/shard_map/all_gather | solution.py:74
  112.7 3.3 all-to-all-start.1
  116.1 4.6 all-to-all-done.1
  120.9 14.1 %while.54 = (s32[]{:T(128)}, f32[2,512]{1,0:T(2,128)S(1)}, f32[2,512]{1,0:T(2,128)S(1)}, s32[1,16]{1,0:T(1,128)}, s32[512]{0:T(512)S(1)}, /*index=5*/bf16[4096,1...) while((s32[]{:T(128)}, f32[2,512]{1,0:T(2,128)S(1)}, f32[2,512]{1,0:T(2,128)S(1)}, ...), condition=%wide.region_10.11_spmd, body=%wide.region_4.10_spmd.sunk | while | flops 286365696 | bytes 21748084 | solution.py:151
  124.8 6.1 conditional.6
  135.0 14.0 %all-gather.9.cloned.1.call-done = bf16[4096,128]{0,1:T(8,128)(2,1)} async-done(((bf16[512,128]{0,1:T(8,128)(2,1)}), bf16[4096,128]{0,1:T(8,128)(2,1)}) %all-gather.9.cloned.1.call-update) | async-done | bytes 1048592 | tf_op jit(solution)/shard_map/all_gather | solution.py:101
  149.8 16.6 %while.55 = (s32[]{:T(128)}, f32[512,2,64]{0,2,1:T(8,128)}, s32[1,16]{1,0:T(1,128)}, s32[512]{0:T(512)S(1)}, bf16[4096,128]{0,1:T(8,128)(2,1)}, /*index=5*/bf16[...) while((s32[]{:T(128)}, f32[512,2,64]{0,2,1:T(8,128)}, ...), condition=%wide.region_15.16_spmd, body=%wide.region_11.15_spmd.sunk | while | flops 548573184 | bytes 5970277 | solution.py:170
  153.7 8.6 %conditional.7 = (f32[512,2,64]{0,2,1:T(8,128)}) conditional(s32[]{:T(128)} %bitcast.239, f32[512,2,64]{0,2,1:T(8,128)} %get-tuple-element.1472, (s32[512]{0:T(512)S(1)}, s32[2048]{0:T(1024)S(1)}, s32[]{:T(128)}, bf16[4096,128]{0,1:T(8,128)(2,1)}, bf16[512,2,64]{0,2,1:T(8,128)(2,1)S(1)}, /*index=5*/f32[2,512]{1,0:T(2,128)S(1)}, ...), branch_computations={%region_13.13_spmd, %region_14.14_spmd} | conditional | flops 548472832 | bytes 5929006 | solution.py:168
  156.8 5.6 fusion.7
  168.0 3.3 all-to-all-start.3
  171.4 4.5 all-to-all-done.3
  178.7 12.1 %all-to-all-start.4 = ((bf16[8,32,512]{2,1,0:T(8,128)(2,1)}), bf16[8,32,512]{2,1,0:T(8,128)(2,1)S(1)}, u32[]{:S(2)}, u32[]{:S(2)}) async-start(bf16[8,32,512]{2,1,0:T(8,128)(2,1)} %bitcast.39), calls=%async_computation.4 | async-start | bytes 524288 | tf_op jit(solution)/shard_map/all_to_all | solution.py:189
  190.8 28.0 %all-gather = bf16[8,64,8]{1,2,0:T(8,128)(2,1)S(1)} all-gather(bf16[1,64,8]{1,2,0:T(8,128)(2,1)S(1)} %bitcast.278), channel_id=1, replica_groups=mesh['head'=4,'blk'=8] {'blk'}, dimensions={0}, use_global_device_ids=true | all-gather | bytes 9216 | tf_op jit(solution)/shard_map/all_gather | solution.py:76
  218.9 6.2 multiply_convert_fusion
  227.5 3.4 all-to-all-start.5
  231.8 7.4 all-to-all-done.5
  244.7 4.1 all-to-all-start.6
  250.0 7.0 all-to-all-done.6
  257.0 4.1 add_convert_fusion
  263.7 3.5 all-to-all-start.7
  269.8 5.6 all-to-all-done.7
  279.8 7.2 all_to_all.161
  291.0 21.3 %while.56 = (s32[]{:T(128)}, f32[512,2,64]{0,2,1:T(8,128)S(1)}, bf16[4096,128]{0,1:T(8,128)(2,1)}, bf16[4096,128]{0,1:T(8,128)(2,1)}, s32[1,16]{1,0:T(1,128)}, /...) while((s32[]{:T(128)}, f32[512,2,64]{0,2,1:T(8,128)S(1)}, ...), condition=%wide.region_33.34_spmd, body=%wide.region_29.33_spmd.sunk | while | flops 1369149440 | bytes 66173600 | solution.py:307
  295.0 13.3 %conditional.8 = ((f32[512,2,64]{0,2,1:T(8,128)S(1)}, bf16[4096,128]{0,1:T(8,128)(2,1)}, bf16[4096,128]{0,1:T(8,128)(2,1)})) conditional(s32[]{:T(128)} %bitcast.241, (f32[512,2,64]{0,2,1:T(8,128)S(1)}, bf16[4096,128]{0,1:T(8,128)(2,1)}, bf16[4096,128]{0,1:T(8,128)(2,1)}) %tuple.204, (s32[512]{0:T(512)S(1)}, s32[2048]{0:T(1024)S(1)}, s32[]{:T(128)}, ...), branch_computations={%region_31.31_spmd, %region_32.32_spmd} | conditional | flops 1369049088 | bytes 66132240 | solution.py:300
  297.3 3.5 fusion.11
  303.1 3.1 fusion.16
  312.3 2.4 copy.136
  317.3 70.8 %reduce-scatter.10.cloned.1.call-done = bf16[512,128]{1,0:T(8,128)(2,1)} async-done(((bf16[4096,128]{1,0:T(8,128)(2,1)}), bf16[512,128]{1,0:T(8,128)(2,1)}) %reduce-scatter.10.cloned.1.call-update) | async-done | bytes 131088 | tf_op jit(solution)/shard_map/reduce_scatter | solution.py:312
  388.1 3.3 all-to-all-start.11
  391.4 63.3 %reduce-scatter.8.cloned.1.call-done = bf16[512,128]{1,0:T(8,128)(2,1)} async-done(((bf16[4096,128]{1,0:T(8,128)(2,1)}), bf16[512,128]{1,0:T(8,128)(2,1)}) %reduce-scatter.8.cloned.1.call-update) | async-done | bytes 131088 | tf_op jit(solution)/shard_map/reduce_scatter | solution.py:309
  454.7 3.3 all-to-all-start.10
  458.8 3.9 all-to-all-done.10
  462.6 3.3 all-to-all-start.9
  466.3 4.2 all-to-all-done.9
  473.6 3.1 fusion.25
  478.8 40.1 %reduce-scatter.14.cloned.1.call-done = bf16[64,512]{1,0:T(8,128)(2,1)} async-done(((bf16[512,512]{1,0:T(8,128)(2,1)}), bf16[64,512]{1,0:T(8,128)(2,1)}) %reduce-scatter.14.cloned.1.call-update) | async-done | bytes 65552 | tf_op jit(solution)/shard_map/reduce_scatter | solution.py:343
  518.9 67.7 %reduce-scatter.12.cloned.1.call-done = bf16[64,1536]{1,0:T(8,128)(2,1)} async-done(((bf16[512,1536]{1,0:T(8,128)(2,1)}), bf16[64,1536]{1,0:T(8,128)(2,1)}) %reduce-scatter.12.cloned.1.call-update) | async-done | bytes 196624 | tf_op jit(solution)/shard_map/reduce_scatter | solution.py:340
  587.4 62.8 %reduce-scatter.16.cloned.1.call-done = bf16[64,8]{1,0:T(8,128)(2,1)} async-done(((bf16[512,8]{1,0:T(8,128)(2,1)}), bf16[64,8]{1,0:T(8,128)(2,1)}) %reduce-scatter.16.cloned.1.call-update) | async-done | bytes 1040
  652.0 19.5 %all-reduce.4 = (bf16[512]{0:T(512)(128)(2,1)S(1)}, bf16[512]{0:T(512)(128)(2,1)S(1)}) all-reduce(bf16[512]{0:T(512)(128)(2,1)S(1)} %get-tuple-element.1110, bf16[512]{0:T(512)(128)(2,1)S(1)} %copy-done.53), channel_id=4, replica_groups=mesh['head'=4,'blk'=8] {'blk'}, use_global_device_ids=true, to_apply=%region_39.40.clone | all-reduce | flops 1024 | bytes 4096
  671.7 6.5 all-reduce.6
  680.7 62.7 %all-reduce.10.cloned.1.call-done = (bf16[64,1536]{1,0:T(8,128)(2,1)}, bf16[64,512]{1,0:T(8,128)(2,1)}, bf16[1,512,2048]{2,1,0:T(8,128)(2,1)}, bf16[1,2048,512]{2,1,0:T(8,128)(2,1)}) async-done(((bf16[64,1536]{1,0:T(8,128)(2,1)}, bf16[64,512]{1,0:T(8,128)(2,1)}, bf16[1,512,2048]{2,1,0:T(8,128)(2,1)}, bf16[1,2048,512]{2,1,0:T(8,128)(2,1)}), (bf16[64,1536]{1,0:T(8,128)(2,1)}, bf16[64,512]{1,0:T(8,128)(2,1)}, ...) | async-done | bytes 4456464 | tf_op jit(solution)/shard_map/psum | solution.py:355
  746.7 4.3 convert_element_type.275
  750.9 2.6 convert_element_type.278
  (290 shorter events, 81.7 us)
Async XLA Ops:
  7.2 211.7 %copy-start = (bf16[1,512,2048]{2,1,0:T(8,128)(2,1)S(1)}, bf16[1,512,2048]{2,1,0:T(8,128)(2,1)}, u32[]{:S(2)}) copy-start(bf16[1,512,2048]{2,1,0:T(8,128)(2,1)} %param.30) | copy-start | bytes 6291460
  7.2 49.8 %all-gather.5.cloned.1.call-start = ((), (), s32[]{:S(2)}) async-start(), calls=%async_computation.17 | async-start | bytes 1769472 | tf_op jit(solution)/shard_map/all_gather | solution.py:73
  7.9 59.1 %copy-start.60 = (s32[16]{0:T(128)S(1)}, s32[16]{0:T(128)}, u32[]{:S(2)}) copy-start(s32[16]{0:T(128)} %param.34) | copy-start | bytes 196
  7.9 112.9 %all-gather.7.cloned.1.call-start = ((), (), s32[]{:S(2)}) async-start(), calls=%async_computation.18 | async-start | bytes 1179648 | tf_op jit(solution)/shard_map/all_gather | solution.py:100
  34.9 24.0 %copy-start.32 = (f32[512]{0:T(512)}, f32[512]{0:T(512)S(1)}, u32[]{:S(2)}) copy-start(f32[512]{0:T(512)S(1)} %convert_element_type.238) | copy-start | bytes 6148
  36.0 23.0 %copy-start.39 = (f32[128]{0:T(128)}, f32[128]{0:T(128)S(1)}, u32[]{:S(2)}) copy-start(f32[128]{0:T(128)S(1)} %broadcast_multiply_fusion.1) | copy-start | bytes 1540
  37.1 21.9 %copy-start.57 = (f32[128]{0:T(128)}, f32[128]{0:T(128)S(1)}, u32[]{:S(2)}) copy-start(f32[128]{0:T(128)S(1)} %fusion.58) | copy-start | bytes 1540
  37.1 21.9 %copy-start.43 = (f32[128]{0:T(128)}, f32[128]{0:T(128)S(1)}, u32[]{:S(2)}) copy-start(f32[128]{0:T(128)S(1)} %fusion.76) | copy-start | bytes 1540
  37.1 35.5 %copy-start.61 = (s32[1,128]{1,0:T(1,128)S(1)}, s32[1,128]{1,0:T(1,128)}, u32[]{:S(2)}) copy-start(s32[1,128]{1,0:T(1,128)} %param.33) | copy-start | bytes 1540
  37.1 40.8 %copy-start.37 = (s32[128,2]{0,1:T(2,128)S(1)}, s32[128,2]{0,1:T(2,128)}, u32[]{:S(2)}) copy-start(s32[128,2]{0,1:T(2,128)} %param.32) | copy-start | bytes 3076
  37.1 41.0 %copy-start.31 = (bf16[64,512]{1,0:T(8,128)(2,1)S(1)}, bf16[64,512]{1,0:T(8,128)(2,1)}, u32[]{:S(2)}) copy-start(bf16[64,512]{1,0:T(8,128)(2,1)} %param.27) | copy-start | bytes 196612
  69.2 7.9 %all-to-all-start.2 = ((bf16[128,4,128]{2,0,1:T(8,128)(2,1)}), bf16[128,4,128]{2,0,1:T(8,128)(2,1)S(1)}, u32[]{:S(2)}, u32[]{:S(2)}) async-start(bf16[128,4,128]{2,0,1:T(8,128)(2,1)} %bitcast.227), calls=%async_computation.2 | async-start | bytes 262144 | tf_op jit(solution)/shard_map/all_to_all | solution.py:93
  72.5 76.5 %all-gather.9.cloned.1.call-start = ((), (), s32[]{:S(2)}) async-start(), calls=%async_computation.19 | async-start | bytes 1179648 | tf_op jit(solution)/shard_map/all_gather | solution.py:101
  112.7 7.9 %all-to-all-start.1 = ((bf16[128,4,128]{2,0,1:T(8,128)(2,1)}), bf16[128,4,128]{2,0,1:T(8,128)(2,1)S(1)}, u32[]{:S(2)}, u32[]{:S(2)}) async-start(bf16[128,4,128]{2,0,1:T(8,128)(2,1)} %bitcast.228), calls=%async_computation.1 | async-start | bytes 262144 | tf_op jit(solution)/shard_map/all_to_all | solution.py:85
  116.0 55.3 %copy-start.38 = (s32[2,128]{1,0:T(2,128)}, s32[2,128]{1,0:T(2,128)S(1)}, u32[]{:S(2)}) copy-start(s32[2,128]{1,0:T(2,128)S(1)} %compare_select_fusion) | copy-start | bytes 3076
  116.1 61.6 %copy-start.34 = (f32[512]{0:T(512)}, f32[512]{0:T(512)S(1)}, u32[]{:S(2)}) copy-start(f32[512]{0:T(512)S(1)} %convert_element_type.243) | copy-start | bytes 6148
  149.8 26.2 %copy-start.4 = (bf16[128,512]{1,0:T(8,128)(2,1)S(1)}, bf16[128,512]{1,0:T(8,128)(2,1)}, u32[]{:S(2)}) copy-start(bf16[128,512]{1,0:T(8,128)(2,1)} %param.24) | copy-start | bytes 393220
  166.3 11.3 %copy-start.51 = (f32[2,512]{1,0:T(2,128)}, f32[2,512]{1,0:T(2,128)S(1)}, u32[]{:S(2)}) copy-start(f32[2,512]{1,0:T(2,128)S(1)} %get-tuple-element.1615) | copy-start | bytes 12292
  166.3 24.5 %copy-start.56 = (bf16[64,8]{0,1:T(8,128)(2,1)S(1)}, bf16[64,8]{0,1:T(8,128)(2,1)}, u32[]{:S(2)}) copy-start(bf16[64,8]{0,1:T(8,128)(2,1)} %param.29) | copy-start | bytes 3076
  168.0 7.9 %all-to-all-start.3 = ((bf16[4,128,128]{1,2,0:T(8,128)(2,1)}), bf16[4,128,128]{1,2,0:T(8,128)(2,1)S(1)}, u32[]{:S(2)}, u32[]{:S(2)}) async-start(bf16[4,128,128]{1,2,0:T(8,128)(2,1)} %copy.128), calls=%async_computation.3 | async-start | bytes 262144 | tf_op jit(solution)/shard_map/all_to_all | solution.py:174
  177.4 41.4 %copy-start.46 = (f32[128]{0:T(128)}, f32[128]{0:T(128)S(1)}, u32[]{:S(2)}) copy-start(f32[128]{0:T(128)S(1)} %broadcast_multiply_fusion) | copy-start | bytes 1540
  178.7 40.2 %all-to-all-start.4 = ((bf16[8,32,512]{2,1,0:T(8,128)(2,1)}), bf16[8,32,512]{2,1,0:T(8,128)(2,1)S(1)}, u32[]{:S(2)}, u32[]{:S(2)}) async-start(bf16[8,32,512]{2,1,0:T(8,128)(2,1)} %bitcast.39), calls=%async_computation.4 | async-start | bytes 524288 | tf_op jit(solution)/shard_map/all_to_all | solution.py:189
  226.1 13.7 %copy-start.13 = (f32[128,512]{1,0:T(8,128)S(1)}, f32[128,512]{1,0:T(8,128)}, u32[]{:S(2)}) copy-start(f32[128,512]{1,0:T(8,128)} %param.35) | copy-start | bytes 786436
  227.5 11.6 %all-to-all-start.5 = ((bf16[8,32,512]{2,1,0:T(8,128)(2,1)}), bf16[8,32,512]{2,1,0:T(8,128)(2,1)S(1)}, u32[]{:S(2)}, u32[]{:S(2)}) async-start(bf16[8,32,512]{2,1,0:T(8,128)(2,1)} %bitcast.43), calls=%async_computation.5 | async-start | bytes 524288 | tf_op jit(solution)/shard_map/all_to_all | solution.py:204
  244.7 12.3 %all-to-all-start.6 = ((bf16[8,32,512]{2,1,0:T(8,128)(2,1)}), bf16[8,32,512]{2,1,0:T(8,128)(2,1)}, u32[]{:S(2)}, u32[]{:S(2)}) async-start(bf16[8,32,512]{2,1,0:T(8,128)(2,1)} %bitcast.254), calls=%async_computation.6 | async-start | bytes 524288 | tf_op jit(solution)/shard_map/all_to_all | solution.py:224
  263.7 15.7 %copy-start.5 = (bf16[512,512]{1,0:T(8,128)(2,1)S(1)}, bf16[512,512]{1,0:T(8,128)(2,1)}, u32[]{:S(2)}) copy-start(bf16[512,512]{1,0:T(8,128)(2,1)} %all_gather.27) | copy-start | bytes 1572868
  263.7 11.7 %all-to-all-start.7 = ((bf16[8,32,512]{2,1,0:T(8,128)(2,1)}), bf16[8,32,512]{2,1,0:T(8,128)(2,1)S(1)}, u32[]{:S(2)}, u32[]{:S(2)}) async-start(bf16[8,32,512]{2,1,0:T(8,128)(2,1)} %bitcast.271), calls=%async_computation.7 | async-start | bytes 524288 | tf_op jit(solution)/shard_map/all_to_all | solution.py:238
  267.2 120.8 %reduce-scatter.10.cloned.1.call-start = ((), (), s32[]{:S(2)}) async-start(), calls=%async_computation.21 | async-start | bytes 1179648 | tf_op jit(solution)/shard_map/reduce_scatter | solution.py:312
  279.7 11.2 %copy-start.2 = (bf16[4096,128]{0,1:T(8,128)(2,1)S(1)}, bf16[4096,128]{0,1:T(8,128)(2,1)}, u32[]{:S(2)}) copy-start(bf16[4096,128]{0,1:T(8,128)(2,1)} %get-tuple-element.1554) | copy-start | bytes 3145732
  279.7 11.2 %copy-start.3 = (bf16[4096,128]{0,1:T(8,128)(2,1)S(1)}, bf16[4096,128]{0,1:T(8,128)(2,1)}, u32[]{:S(2)}) copy-start(bf16[4096,128]{0,1:T(8,128)(2,1)} %get-tuple-element.1557) | copy-start | bytes 3145732
  314.7 140.0 %reduce-scatter.8.cloned.1.call-start = ((), (), s32[]{:S(2)}) async-start(), calls=%async_computation.20 | async-start | bytes 1179648 | tf_op jit(solution)/shard_map/reduce_scatter | solution.py:309
  316.1 154.5 %copy-start.33 = (f32[512]{0:T(512)S(1)}, f32[512]{0:T(512)}, u32[]{:S(2)}) copy-start(f32[512]{0:T(512)} %copy-done.32) | copy-start | bytes 6148
  316.1 154.5 %copy-start.40 = (f32[128]{0:T(128)S(1)}, f32[128]{0:T(128)}, u32[]{:S(2)}) copy-start(f32[128]{0:T(128)} %copy-done.39) | copy-start | bytes 1540
  316.1 154.5 %copy-start.44 = (f32[128]{0:T(128)S(1)}, f32[128]{0:T(128)}, u32[]{:S(2)}) copy-start(f32[128]{0:T(128)} %copy-done.43) | copy-start | bytes 1540
  316.1 202.8 %reduce-scatter.14.cloned.1.call-start = ((), (), s32[]{:S(2)}) async-start(), calls=%async_computation.23 | async-start | bytes 589824 | tf_op jit(solution)/shard_map/reduce_scatter | solution.py:343
  388.1 66.6 %all-to-all-start.11 = ((bf16[4,128,128]{2,1,0:T(8,128)(2,1)}), bf16[4,128,128]{2,1,0:T(8,128)(2,1)S(1)}, u32[]{:S(2)}, u32[]{:S(2)}) async-start(bf16[4,128,128]{2,1,0:T(8,128)(2,1)} %bitcast.273), calls=%async_computation.13 | async-start | bytes 262144 | tf_op jit(solution)/shard_map/all_to_all | solution.py:327
  454.7 7.9 %all-to-all-start.10 = ((bf16[4,128,128]{2,1,0:T(8,128)(2,1)}), bf16[4,128,128]{2,1,0:T(8,128)(2,1)S(1)}, u32[]{:S(2)}, u32[]{:S(2)}) async-start(bf16[4,128,128]{2,1,0:T(8,128)(2,1)} %bitcast.272), calls=%async_computation.11 | async-start | bytes 262144 | tf_op jit(solution)/shard_map/all_to_all | solution.py:324
  462.6 7.9 %all-to-all-start.9 = ((bf16[4,128,128]{1,2,0:T(8,128)(2,1)}), bf16[4,128,128]{1,2,0:T(8,128)(2,1)S(1)}, u32[]{:S(2)}, u32[]{:S(2)}) async-start(bf16[4,128,128]{1,2,0:T(8,128)(2,1)} %copy.133), calls=%async_computation.9 | async-start | bytes 262144 | tf_op jit(solution)/shard_map/all_to_all | solution.py:317
  466.0 120.6 %reduce-scatter.12.cloned.1.call-start = ((), (), s32[]{:S(2)}) async-start(), calls=%async_computation.22 | async-start | bytes 1769472 | tf_op jit(solution)/shard_map/reduce_scatter | solution.py:340
  472.5 177.7 %reduce-scatter.16.cloned.1.call-start = ((), (), s32[]{:S(2)}) async-start(), calls=%async_computation.24 | async-start | bytes 147456
  473.6 269.9 %all-reduce.10.cloned.1.call-start = ((), (), s32[]{:S(2)}) async-start(), calls=%async_computation.25 | async-start | bytes 8912896 | tf_op jit(solution)/shard_map/psum | solution.py:355
  586.6 64.4 %copy-start.17 = (bf16[512,1536]{1,0:T(8,128)(2,1)S(1)}, bf16[512,1536]{1,0:T(8,128)(2,1)}, u32[]{:S(2)}) copy-start(bf16[512,1536]{1,0:T(8,128)(2,1)} %all-gather.5.cloned.1.call-done) | copy-start | bytes 4718596
  586.6 64.4 %copy-start.27 = (bf16[128,4,128]{0,2,1:T(8,128)(2,1)S(1)}, bf16[128,4,128]{0,2,1:T(8,128)(2,1)}, u32[]{:S(2)}) copy-start(bf16[128,4,128]{0,2,1:T(8,128)(2,1)} %copy-done.26) | copy-start | bytes 393220
  586.6 64.4 %copy-start.29 = (bf16[128,4,128]{0,2,1:T(8,128)(2,1)S(1)}, bf16[128,4,128]{0,2,1:T(8,128)(2,1)}, u32[]{:S(2)}) copy-start(bf16[128,4,128]{0,2,1:T(8,128)(2,1)} %copy-done.28) | copy-start | bytes 393220
  586.6 64.4 %copy-start.41 = (f32[128]{0:T(128)S(1)}, f32[128]{0:T(128)}, u32[]{:S(2)}) copy-start(f32[128]{0:T(128)} %copy-done.39) | copy-start | bytes 1540
  586.6 65.2 %copy-start.58 = (f32[128]{0:T(128)S(1)}, f32[128]{0:T(128)}, u32[]{:S(2)}) copy-start(f32[128]{0:T(128)} %copy-done.57) | copy-start | bytes 1540
  586.6 65.2 %copy-start.45 = (f32[128]{0:T(128)S(1)}, f32[128]{0:T(128)}, u32[]{:S(2)}) copy-start(f32[128]{0:T(128)} %copy-done.43) | copy-start | bytes 1540
  586.6 65.4 %copy-start.53 = (bf16[512]{0:T(512)(128)(2,1)S(1)}, bf16[512]{0:T(512)(128)(2,1)}, u32[]{:S(2)}) copy-start(bf16[512]{0:T(512)(128)(2,1)} %get-tuple-element.1108) | copy-start | bytes 3076
  (34 other events, 129.8 us)
Sparse Core Ops, SparseCore 0:
  10.2 46.7 all-gather.4
  67.1 41.6 all-gather.6
  111.5 37.5 all-gather.8
  314.8 73.2 reduce-scatter.9
  392.3 62.3 reduce-scatter.7
  457.9 60.9 reduce-scatter.13
  522.7 63.8 reduce-scatter.11
  590.4 59.7 reduce-scatter.15
  653.9 89.4 all-reduce.9
where the time goes:
time: 763 us; the launch traced here: 760 us
  waiting for transfers between devices  444 us (58%)
  blocking collectives  125 us (16%)
  matrix products  50.5 us (7%)
  starting transfers between devices  43.4 us (6%)
  other arithmetic  34.8 us (5%)
  local copies, waits for them, and re-layouts  30.1 us (4%)
  between operations  16.2 us (2%)
  loops' own time  16 us (2%)
    reduce_scatter x1, waiting for transfers between devices, local(): lax.psum_scatter(value_grad.astype(jnp.bfloat16), 'blk', scatter_dimensio...  70.8 us
    reduce_scatter x1, waiting for transfers between devices, local(): lax.psum_scatter(d_qkv_weight.astype(jnp.bfloat16), 'blk', scatter_dimens...  67.7 us
    unnamed x10, waiting for transfers between devices  63.6 us
    reduce_scatter x1, waiting for transfers between devices, local(): lax.psum_scatter(key_grad.astype(jnp.bfloat16), 'blk', scatter_dimension=...  63.3 us
    psum x1, waiting for transfers between devices, local(): lax.psum(qkv_sum.astype(jnp.bfloat16), 'head').astype(jnp.float32)  62.7 us
    unnamed x2, blocking collectives  42.7 us
    reduce_scatter x1, waiting for transfers between devices, local(): lax.psum_scatter(d_out_weight.astype(jnp.bfloat16), 'blk', scatter_dimens...  40.1 us
    all_gather x1, blocking collectives, local(): lax.all_gather(w_out, 'blk', axis=0, tiled=True)  33.9 us
  transfers between devices with their start and end apart: 19, of which 16 were waited for; matrix products, arithmetic and copies ran while one was open for 5% of the time, Pallas kernels for 0%

commit v1 on v0

--- a/solution.py
+++ b/solution.py
@@ -1,6 +1,11 @@
+import functools
+import math
+
 import jax
 import jax.numpy as jnp
 from jax import lax
+from jax.experimental import pallas as pl
+from jax.experimental.pallas import tpu as pltpu
 from jax.sharding import PartitionSpec as P
 
 HS = 64
@@ -28,7 +33,8 @@
 
 
 def doc_index(positions, doc_lengths):
-    starts = jnp.cumsum(doc_lengths) - doc_lengths
+    places = jnp.arange(doc_lengths.shape[0], dtype=jnp.int32)
+    starts = jnp.sum(jnp.where(places[None, :] < places[:, None], doc_lengths[None, :], 0), axis=1)
     at_most = (starts[None, :] <= positions[:, None]).astype(jnp.int32)
     return jnp.sum(at_most, axis=1) - 1
 
@@ -372,6 +378,1066 @@
     )
 
 
+MESH = pl.DeviceIdType.MESH
+LANES = 128
+HALF = LANES // 2
+VMEM_LIMIT = 50 * 2**20
+F32 = jnp.float32
+BF16 = jnp.bfloat16
+
+
+def dot(left, right, dims=(1, 0)):
+    return lax.dot_general(
+        left, right, (((dims[0],), (dims[1],)), ((), ())), preferred_element_type=F32
+    )
+
+
+def remote(src, dst, send_sem, recv_sem, head, blk):
+    return pltpu.make_async_remote_copy(
+        src_ref=src,
+        dst_ref=dst,
+        send_sem=send_sem,
+        recv_sem=recv_sem,
+        device_id={"head": head, "blk": blk},
+        device_id_type=MESH,
+    )
+
+
+def arrived(ref, sem):
+    pltpu.make_async_copy(ref, ref, sem).wait()
+
+
+def greet(peers):
+    barrier = pltpu.get_barrier_semaphore()
+    for head, blk in peers:
+        pl.semaphore_signal(
+            barrier, inc=1, device_id={"head": head, "blk": blk}, device_id_type=MESH
+        )
+    pl.semaphore_wait(barrier, len(peers))
+
+
+def lane_ids(shape):
+    return lax.broadcasted_iota(jnp.int32, shape, len(shape) - 1)
+
+
+def centre(values):
+    average = jnp.mean(values, axis=-1, keepdims=True)
+    centred = values - average
+    spread = jnp.mean(centred * centred, axis=-1, keepdims=True)
+    scale = lax.rsqrt(spread + EPSILON)
+    return centred * scale, scale
+
+
+def centre_back(grad, xhat, scale):
+    middle = jnp.mean(grad, axis=-1, keepdims=True)
+    along = jnp.mean(grad * xhat, axis=-1, keepdims=True)
+    return (grad - middle - xhat * along) * scale
+
+
+def split_high_low(column, lanes):
+    high = column.astype(BF16)
+    low = (column - high.astype(F32)).astype(BF16)
+    return jnp.where(lanes < HALF, high.astype(F32), low.astype(F32)).astype(BF16)
+
+
+def join_high_low(matrix, start):
+    return matrix[:, start : start + 1].astype(F32) + matrix[
+        :, start + HALF : start + HALF + 1
+    ].astype(F32)
+
+
+def place():
+    head, blk = lax.axis_index("head"), lax.axis_index("blk")
+    return head, blk, blk // 2, lax.rem(blk, 2)
+
+
+def around(index, step, size):
+    return lax.rem(index + step, size)
+
+
+def qkv_kernel(
+    heads, blks,
+    x_ref, w_ref, g1_ref, wo_ref, wr_ref, g2_ref,
+    q_out, kv_out, xa_out, wa_out, wo_out,
+    gain_tile, xall, wall, wo_own, wo_all, kvall, kv_other, qall,
+    x_send, x_recv, w_send, w_recv, o_send, o_recv, p_send, p_recv,
+    k_send, k_recv, q_recv, out_sem,
+):
+    head, blk, z, y = place()
+    planes = blks // 2
+    model = x_ref.shape[1]
+    rows = w_ref.shape[0]
+    part = rows // heads
+    greet(
+        [(around(head, k, heads), blk) for k in range(1, heads)]
+        + [(head, around(blk, k, blks)) for k in range(1, blks)]
+    )
+    lanes = lane_ids((rows, LANES))
+    gain_tile[...] = jnp.zeros_like(gain_tile)
+    gain_tile[0:1, 0:rows] = g1_ref[...].astype(F32)
+    gain = jnp.transpose(jnp.broadcast_to(gain_tile[0:1, :], (LANES, LANES)))[:rows]
+
+    def columns(which):
+        start = pl.multiple_of(which * model + head * LANES, LANES)
+        return w_ref[:, pl.ds(start, LANES)].astype(F32) * gain
+
+    key_cols = columns(1)
+    value_cols = pltpu.roll(columns(2), HALF, 1)
+    wall[blk, :, 0:LANES] = jnp.where(lanes < HALF, key_cols, value_cols).astype(BF16)
+    wall[blk, :, LANES : 2 * LANES] = jnp.where(lanes < HALF, value_cols, key_cols).astype(BF16)
+    wall[blk, :, 2 * LANES : 3 * LANES] = (columns(0) * HS ** (-0.5)).astype(BF16)
+    w_copies = [
+        remote(wall.at[blk], wall.at[blk], w_send.at[k], w_recv.at[k], head, around(blk, k, blks))
+        for k in range(1, blks)
+    ]
+    for copy in w_copies:
+        copy.start()
+    xhat, _ = centre(x_ref[...].astype(F32))
+    xall[head] = xhat.astype(BF16)
+    x_copies = [
+        remote(xall.at[head], xall.at[head], x_send.at[k], x_recv.at[k], around(head, k, heads), blk)
+        for k in range(1, heads)
+    ]
+    for copy in x_copies:
+        copy.start()
+    wo_own[...] = jnp.zeros_like(wo_own)
+    wo_own[:, 0:model] = wo_ref[...]
+    wo_own[:, model : model + wr_ref.shape[1]] = wr_ref[...]
+    wo_own[:, model + wr_ref.shape[1] : model + wr_ref.shape[1] + 1] = g2_ref[...]
+    wo_all[blk, head] = wo_own[pl.ds(pl.multiple_of(head * part, part), part), :]
+    o_copies = [
+        remote(
+            wo_all.at[blk, head], wo_all.at[blk, head],
+            o_send.at[k], o_recv.at[k], head, around(blk, k, blks),
+        )
+        for k in range(1, blks)
+    ]
+    for copy in o_copies:
+        copy.start()
+    for copy in x_copies:
+        copy.wait()
+    for copy in w_copies:
+        copy.wait()
+    weight = wall[...].reshape(model, 3 * LANES)
+    tokens = x_ref.shape[0]
+    even = y == 0
+    for piece in range(heads):
+        made = dot(xall[piece], weight).astype(BF16)
+        first, second = made[:, 0:LANES], made[:, LANES : 2 * LANES]
+        span = slice(piece * tokens, (piece + 1) * tokens)
+        kvall[blk, span, :] = jnp.where(even, first, second)
+        kv_other[span, :] = jnp.where(even, second, first)
+        qall[y, span, :] = made[:, 2 * LANES : 3 * LANES]
+    above, below = z < planes - 1, z > 0
+    own = kvall.at[blk]
+
+    def outward(slot, step, across):
+        target = 2 * (z + step) + around(y, across, 2)
+        return remote(kv_other if across else own, own, k_send.at[slot], k_recv.at[blk], head, target)
+
+    def onward(slot, step, side):
+        from_span = 2 * (z - step) + side
+        ref = kvall.at[from_span]
+        return remote(ref, ref, k_send.at[slot], k_recv.at[from_span], head, 2 * (z + step) + y)
+
+    sides = ((1, above, below, 0), (-1, below, above, 2))
+    for step, there, _, slot in sides:
+
+        @pl.when(there)
+        def _():
+            outward(slot, step, 0).start()
+            outward(slot + 1, step, 1).start()
+
+    to_pair = outward(4, 0, 1)
+    to_pair.start()
+    q_pair = remote(qall.at[y], qall.at[y], k_send.at[5], q_recv, head, 2 * z + around(y, 1, 2))
+    q_pair.start()
+    for copy in o_copies:
+        copy.wait()
+    p_copies = [
+        remote(
+            wo_all.at[:, head], wo_all.at[:, head],
+            p_send.at[k], p_recv.at[k], around(head, k, heads), blk,
+        )
+        for k in range(1, heads)
+    ]
+    for copy in p_copies:
+        copy.start()
+    for step, there, back, slot in sides:
+
+        @pl.when(back)
+        def _():
+            for side in range(2):
+                span = 2 * (z - step) + side
+                arrived(kvall.at[span], k_recv.at[span])
+
+        @pl.when(jnp.logical_and(there, back))
+        def _():
+            for side in range(2):
+                onward(6 + slot + side, step, side).start()
+
+    far = jnp.zeros(kv_other.shape, BF16)
+    for other in range(planes):
+        for side in range(2):
+            span = 2 * other + side
+
+            @pl.when(jnp.logical_or(z - other > 2, other - z > 2))
+            def _():
+                kvall[span] = far
+
+            @pl.when(jnp.logical_or(z - other == 2, other - z == 2))
+            def _():
+                arrived(kvall.at[span], k_recv.at[span])
+
+    pair = 2 * z + around(y, 1, 2)
+    arrived(kvall.at[pair], k_recv.at[pair])
+    q_pair.wait()
+    for copy in p_copies:
+        copy.wait()
+    outs = [
+        pltpu.make_async_copy(src, dst, out_sem.at[i])
+        for i, (src, dst) in enumerate(
+            ((qall, q_out), (kvall, kv_out), (xall, xa_out), (wall, wa_out), (wo_all, wo_out))
+        )
+    ]
+    for copy in outs:
+        copy.start()
+    to_pair.wait_send()
+    for step, there, back, slot in sides:
+
+        @pl.when(there)
+        def _():
+            outward(slot, step, 0).wait_send()
+            outward(slot + 1, step, 1).wait_send()
+
+        @pl.when(jnp.logical_and(there, back))
+        def _():
+            for side in range(2):
+                onward(6 + slot + side, step, side).wait_send()
+
+    for copy in outs:
+        copy.wait()
+
+
+def vmem_specs(count):
+    return [pl.BlockSpec(memory_space=pltpu.VMEM)] * count
+
+
+def any_specs(count):
+    return [pl.BlockSpec(memory_space=pl.ANY)] * count
+
+
+def dma(*shape):
+    return pltpu.SemaphoreType.DMA(shape)
+
+
+def call_qkv(x, w_qkv, g1, w_out, w_router, g2, heads, blks):
+    tokens, model = x.shape
+    rows = w_qkv.shape[0]
+    span = tokens * heads
+    wide = model + LANES
+    part = rows // heads
+    return pl.pallas_call(
+        functools.partial(qkv_kernel, heads, blks),
+        out_shape=(
+            jax.ShapeDtypeStruct((2, span, LANES), BF16),
+            jax.ShapeDtypeStruct((blks, span, LANES), BF16),
+            jax.ShapeDtypeStruct((heads, tokens, model), BF16),
+            jax.ShapeDtypeStruct((blks, rows, 3 * LANES), BF16),
+            jax.ShapeDtypeStruct((blks, heads, part, wide), BF16),
+        ),
+        in_specs=vmem_specs(6),
+        out_specs=tuple(any_specs(5)),
+        scratch_shapes=[
+            pltpu.VMEM((8, LANES), F32),
+            pltpu.VMEM((heads, tokens, model), BF16),
+            pltpu.VMEM((blks, rows, 3 * LANES), BF16),
+            pltpu.VMEM((rows, wide), BF16),
+            pltpu.VMEM((blks, heads, part, wide), BF16),
+            pltpu.VMEM((blks, span, LANES), BF16),
+            pltpu.VMEM((span, LANES), BF16),
+            pltpu.VMEM((2, span, LANES), BF16),
+            dma(heads), dma(heads), dma(blks), dma(blks), dma(blks), dma(blks), dma(heads), dma(heads),
+            dma(10), dma(blks), pltpu.SemaphoreType.DMA, dma(5),
+        ],
+        compiler_params=pltpu.CompilerParams(
+            collective_id=1, has_side_effects=True, vmem_limit_bytes=VMEM_LIMIT
+        ),
+        name="qkv",
+    )(x, w_qkv, g1.reshape(1, rows), w_out, w_router, g2.reshape(rows, 1))
+
+
+QUERY_TILE = 256
+KEY_TILE = 512
+
+
+def tile_docs(doc_ref, first, size):
+    token = first + lane_ids((1, size))
+    last = first + size - 1
+    start = jnp.int32(0)
+    low_row, high_row = jnp.zeros((1, size), jnp.int32), jnp.zeros((1, size), jnp.int32)
+    low = low_last = high = jnp.int32(0)
+    for index in range(doc_ref.shape[0]):
+        end = start + doc_ref[index]
+        low_row = jnp.where(token >= start, start, low_row)
+        high_row = jnp.where(token >= start, end, high_row)
+        low = jnp.where(first >= start, start, low)
+        low_last = jnp.where(last >= start, start, low_last)
+        high = jnp.where(last >= start, end, high)
+        start = end
+    return low_row, high_row, low, high, low == low_last
+
+
+def key_columns(doc_ref, kv_ref, kvt, z, span):
+    _, _, low, _, _ = tile_docs(doc_ref, z * span, LANES)
+    _, _, _, high, _ = tile_docs(doc_ref, (z + 1) * span - LANES, LANES)
+    for block in range(kv_ref.shape[0]):
+        size = kv_ref.shape[1]
+
+        @pl.when(jnp.logical_and(block * size < high, (block + 1) * size > low))
+        def _():
+            kvt[:, block * size : (block + 1) * size] = jnp.transpose(kv_ref[block])
+
+
+def forward_kernel(doc_ref, q_ref, kv_ref, o_out, ob_out, lse_out, kvt):
+    _, _, z, y = place()
+    total = q_ref.shape[0] * q_ref.shape[1]
+    key_columns(doc_ref, kv_ref, kvt, z, total)
+    lanes = lane_ids((QUERY_TILE, LANES))
+    tiles_per_span = q_ref.shape[1] // QUERY_TILE
+    key_lanes = (lanes < HALF) == (y == 0)
+    for tile in range(total // QUERY_TILE):
+        inner = tile % tiles_per_span * QUERY_TILE
+        query = q_ref[tile // tiles_per_span, inner : inner + QUERY_TILE, :]
+        query = jnp.where(key_lanes, query, jnp.zeros_like(query))
+        low_row, high_row, low, high, single = tile_docs(
+            doc_ref, z * total + tile * QUERY_TILE, QUERY_TILE
+        )
+
+        def step(block, carry, query=query, low_row=low_row, high_row=high_row):
+            biggest, weight, mixed = carry
+            first = pl.multiple_of(block * KEY_TILE, KEY_TILE)
+            scores = dot(kv_ref[block], query, (1, 1))
+            key = first + lax.broadcasted_iota(jnp.int32, scores.shape, 0)
+            inside = jnp.logical_and(key >= low_row, key < high_row)
+            scores = jnp.where(inside, scores, MASKED)
+            bigger = jnp.maximum(biggest, jnp.max(scores, axis=0, keepdims=True))
+            fade = jnp.exp(biggest - bigger)
+            terms = jnp.where(inside, jnp.exp(scores - bigger), 0.0)
+            weight = weight * fade + jnp.sum(terms, axis=0, keepdims=True)
+            mixed = mixed * fade + dot(kvt[:, pl.ds(first, KEY_TILE)], terms.astype(BF16))
+            return bigger, weight, mixed
+
+        biggest, weight, mixed = lax.fori_loop(
+            low // KEY_TILE,
+            (high + KEY_TILE - 1) // KEY_TILE,
+            step,
+            (
+                jnp.full((1, QUERY_TILE), MASKED, F32),
+                jnp.zeros((1, QUERY_TILE), F32),
+                jnp.zeros((LANES, QUERY_TILE), F32),
+            ),
+        )
+        result = jnp.transpose(mixed / weight)
+        o_out[tile] = result
+        ob_out[tile] = result.astype(BF16)
+        lse_out[tile] = jnp.broadcast_to(biggest + jnp.log(weight), (8, QUERY_TILE))
+
+
+def call_forward(doc_lengths, q, kv):
+    blks, span, _ = kv.shape
+    tiles = 2 * span // QUERY_TILE
+    return pl.pallas_call(
+        forward_kernel,
+        out_shape=(
+            jax.ShapeDtypeStruct((tiles, QUERY_TILE, LANES), F32),
+            jax.ShapeDtypeStruct((tiles, QUERY_TILE, LANES), BF16),
+            jax.ShapeDtypeStruct((tiles, 8, QUERY_TILE), F32),
+        ),
+        in_specs=[pl.BlockSpec(memory_space=pltpu.SMEM)] + vmem_specs(2),
+        out_specs=tuple(vmem_specs(3)),
+        scratch_shapes=[pltpu.VMEM((LANES, blks * span), BF16)],
+        compiler_params=pltpu.CompilerParams(vmem_limit_bytes=VMEM_LIMIT),
+        name="attend",
+    )(doc_lengths, q, kv)
+
+
+def backward_kernel(doc_ref, q_ref, kv_ref, do_ref, o_ref, lse_ref, dq_out, dkv_out, kvt, dkv):
+    _, _, z, y = place()
+    total = q_ref.shape[0] * q_ref.shape[1]
+    key_columns(doc_ref, kv_ref, kvt, z, total)
+    dkv[...] = jnp.zeros_like(dkv)
+    lanes = lane_ids((QUERY_TILE, LANES))
+    tiles_per_span = q_ref.shape[1] // QUERY_TILE
+    key_lanes = (lanes < HALF) == (y == 0)
+    for tile in range(total // QUERY_TILE):
+        inner = tile % tiles_per_span * QUERY_TILE
+        query = q_ref[tile // tiles_per_span, inner : inner + QUERY_TILE, :]
+        query = jnp.where(key_lanes, query, jnp.zeros_like(query))
+        out_grad = do_ref[tile]
+        out_grad = jnp.where(key_lanes, jnp.zeros_like(out_grad), out_grad)
+        delta = jnp.sum(
+            jnp.transpose(out_grad.astype(F32) * o_ref[tile]), axis=0, keepdims=True
+        )
+        log_total = lse_ref[tile, 0:1, :]
+        low_row, high_row, low, high, single = tile_docs(
+            doc_ref, z * total + tile * QUERY_TILE, QUERY_TILE
+        )
+
+        def step(
+            block, mixed, query=query, out_grad=out_grad, delta=delta, log_total=log_total,
+            low_row=low_row, high_row=high_row,
+        ):
+            first = pl.multiple_of(block * KEY_TILE, KEY_TILE)
+            scores = dot(kv_ref[block], query, (1, 1))
+            key = first + lax.broadcasted_iota(jnp.int32, scores.shape, 0)
+            inside = jnp.logical_and(key >= low_row, key < high_row)
+            weights = jnp.where(inside, jnp.exp(scores - log_total), 0.0)
+            weight_grads = dot(kv_ref[block], out_grad, (1, 1))
+            score_grads = (weights * (weight_grads - delta)).astype(BF16)
+            dkv[block] += dot(score_grads, query) + dot(weights.astype(BF16), out_grad)
+            return mixed + dot(kvt[:, pl.ds(first, KEY_TILE)], score_grads)
+
+        mixed = lax.fori_loop(
+            low // KEY_TILE,
+            (high + KEY_TILE - 1) // KEY_TILE,
+            step,
+            jnp.zeros((LANES, QUERY_TILE), F32),
+        )
+        dq_out[tile] = jnp.transpose(mixed).astype(BF16)
+    for block in range(dkv.shape[0]):
+        dkv_out[block] = dkv[block].astype(BF16)
+
+
+def call_backward(doc_lengths, q, kv, d_o, o, lse):
+    blks, span, _ = kv.shape
+    tiles = 2 * span // QUERY_TILE
+    return pl.pallas_call(
+        backward_kernel,
+        out_shape=(
+            jax.ShapeDtypeStruct((tiles, QUERY_TILE, LANES), BF16),
+            jax.ShapeDtypeStruct((blks, span, LANES), BF16),
+        ),
+        in_specs=[pl.BlockSpec(memory_space=pltpu.SMEM)] + vmem_specs(5),
+        out_specs=tuple(vmem_specs(2)),
+        scratch_shapes=[
+            pltpu.VMEM((LANES, blks * span), BF16),
+            pltpu.VMEM((blks, span, LANES), F32),
+        ],
+        compiler_params=pltpu.CompilerParams(vmem_limit_bytes=VMEM_LIMIT),
+        name="attend_back",
+    )(doc_lengths, q, kv, d_o.reshape(tiles, QUERY_TILE, LANES), o, lse)
+
+
+def gelu_parts(values):
+    share = 0.5 * (1.0 + lax.erf(values * (2.0**-0.5)))
+    slope = share + values * jnp.exp(-0.5 * values * values) * (2.0 * math.pi) ** -0.5
+    return values * share, slope
+
+
+def positions(expert_rows, expert_cols, rank_row, rank_col):
+    def count(mask, axis):
+        return jnp.sum(mask.astype(F32), axis=axis, keepdims=True)
+
+    row = [None, None]
+    col = [None, None]
+    before = rank_col < rank_row
+    after = rank_row < rank_col
+    for choice in range(2):
+        row[choice] = count((expert_cols[choice] == expert_rows[choice]) & before, 0)
+        col[choice] = count((expert_rows[choice] == expert_cols[choice]) & after, 1)
+    row[1] = row[1] + count(expert_cols[0] == expert_rows[1], 0)
+    col[1] = col[1] + count(expert_rows[0] == expert_cols[1], 1)
+    return row, col
+
+
+def middle_kernel(
+    heads, blks,
+    x_ref, o_ref, wo_ref, routes_ref, rank_ref, d_out_ref, win_ref, wout_ref,
+    out_ref, dh_ref, do_out, grads_ref, rows_out,
+    o_all, dos, doa, rs, ra, po, pa, dr, da, dms, dma_all, rx, acc_out, acc_row, mix,
+    o_send, o_recv, dos_send, dos_recv, r_send, r_recv, po_send, po_recv,
+    dr_send, dr_recv, dm_send, dm_recv, rx_send, rx_recv, out_sem,
+):
+    head, blk, z, y = place()
+    tokens, model = x_ref.shape
+    capacity = 2 * tokens // blks
+    slots = capacity * blks
+    plane = [(k % heads, k // heads) for k in range(1, 2 * heads)]
+    greet(
+        [(around(head, kh, heads), 2 * z + around(y, ky, 2)) for kh, ky in plane]
+        + [(head, around(blk, k, blks)) for k in range(1, blks) if True]
+    )
+
+    def plane_copies(src_of, dst, send, recv):
+        copies = []
+        for k, (kh, ky) in enumerate(plane):
+            to_head, to_y = around(head, kh, heads), around(y, ky, 2)
+            copies.append(
+                remote(src_of(to_y, to_head), dst, send.at[k], recv.at[k], to_head, 2 * z + to_y)
+            )
+        return copies
+
+    def blk_copies(src, dst, send, recv):
+        return [
+            remote(
+                src.at[around(blk, k, blks)], dst.at[blk],
+                send.at[k], recv.at[k], head, around(blk, k, blks),
+            )
+            for k in range(1, blks)
+        ]
+
+    def start(copies):
+        for copy in copies:
+            copy.start()
+
+    def finish(copies):
+        for copy in copies:
+            copy.wait()
+
+    o_copies = plane_copies(lambda to_y, to_head: o_ref.at[to_y, to_head], o_all.at[y, head], o_send, o_recv)
+    start(o_copies)
+    o_all[y, head] = o_ref[y, head]
+
+    lanes = lane_ids((tokens, LANES))
+    routes = routes_ref[...].astype(F32)
+    e_cols = [routes[:, 0:1], routes[:, 1:2]]
+    e_mix = jnp.transpose(jnp.where(lanes == 0, e_cols[0], e_cols[1]))
+    e_rows = [e_mix[0:1, :], e_mix[1:2, :]]
+    rank_row = rank_ref[...].astype(F32)
+    rank_col = jnp.transpose(jnp.broadcast_to(rank_row, (tokens, tokens)))[:, 0:1]
+    pos_rows, pos_cols = positions(e_rows, e_cols, rank_row, rank_col)
+
+    def slot_of(expert, position):
+        return jnp.where(position < capacity, expert * capacity + position, -1.0).astype(jnp.int32)
+
+    slot_rows = [slot_of(e, p) for e, p in zip(e_rows, pos_rows)]
+    slot_cols = [slot_of(e, p) for e, p in zip(e_cols, pos_cols)]
+    slot_down = lax.broadcasted_iota(jnp.int32, (slots, tokens), 0)
+    slot_across = lane_ids((tokens, slots))
+    pick = [(slot_down == s).astype(BF16) for s in slot_rows]
+    put = [(slot_across == s).astype(BF16) for s in slot_cols]
+    pick_any = pick[0] + pick[1]
+    put_any = put[0] + put[1]
+
+    d_out = d_out_ref[...]
+    dos[...] = dot(pick_any, d_out.astype(BF16)).astype(BF16).reshape(dos.shape)
+    dos_copies = blk_copies(dos, doa, dos_send, dos_recv)
+    start(dos_copies)
+    doa[blk] = dos[blk]
+
+    weight_out = jnp.concatenate(
+        [wo_ref[(b ^ 1) * HALF : ((b ^ 1) + 1) * HALF, 0:model] for b in range(blks)], axis=0
+    )
+    small = wo_ref[:, model : model + LANES]
+    small_across = jnp.concatenate(
+        [
+            jnp.transpose(small[i * LANES : (i + 1) * LANES].astype(F32))
+            for i in range(model // LANES)
+        ],
+        axis=1,
+    )
+    gain = small_across[blks : blks + 1, :]
+
+    finish(o_copies)
+    for piece in range(heads):
+        mix[:, piece * LANES : (piece + 1) * LANES] = jnp.where(
+            lanes < HALF, o_all[1, piece], o_all[0, piece]
+        )
+    mixed = mix[...]
+    hidden = x_ref[...].astype(F32) + dot(mixed, weight_out)
+    xhat, scale = centre(hidden)
+    routed = (xhat * gain).astype(BF16)
+    logits = jnp.where(lanes < blks, dot(routed, small), MASKED)
+    powers = jnp.exp(logits - jnp.max(logits, axis=1, keepdims=True))
+    probs = powers / jnp.sum(powers, axis=1, keepdims=True)
+    lanes_f = lanes.astype(F32)
+    hots = [lanes_f == e for e in e_cols]
+    gates = [jnp.sum(jnp.where(hot, probs, 0.0), axis=1, keepdims=True) for hot in hots]
+    gate_mats = [split_high_low(g, lanes) for g in gates]
+
+    rs[:, :, 0:model] = dot(pick_any, routed).astype(BF16).reshape(blks, capacity, model)
+    rs[:, :, model : model + LANES] = (
+        (dot(pick[0], gate_mats[0]) + dot(pick[1], gate_mats[1]))
+        .astype(BF16)
+        .reshape(blks, capacity, LANES)
+    )
+    r_copies = blk_copies(rs, ra, r_send, r_recv)
+    start(r_copies)
+    ra[blk] = rs[blk]
+    acc_out[...] = jnp.zeros_like(acc_out)
+    acc_row[...] = jnp.zeros_like(acc_row)
+    finish(dos_copies)
+    finish(r_copies)
+
+    arrived_rows = ra[...].reshape(slots, model + LANES)
+    out_rows = doa[...].reshape(slots, model)
+    gate_col = join_high_low(arrived_rows, model)
+    rx[head, :, 0:model] = arrived_rows[:, 0:model]
+    rx[head, :, model : 2 * model] = (out_rows.astype(F32) * gate_col).astype(BF16)
+    half_ff = wout_ref.shape[0] // 4
+
+    @pl.loop(0, 4)
+    def _(chunk):
+        first = pl.multiple_of(chunk * half_ff, half_ff)
+        into = win_ref[:, pl.ds(first, half_ff)]
+        outof = wout_ref[pl.ds(first, half_ff), :]
+        act, slope = gelu_parts(dot(rx[head, :, 0:model], into))
+        acc_out[...] += dot(act.astype(BF16), outof)
+        d_act = dot(rx[head, :, model : 2 * model], outof, (1, 1))
+        acc_row[...] += dot((slope * d_act).astype(BF16), into, (1, 1))
+
+    result = acc_out[...].astype(BF16)
+    d_gate = jnp.sum(out_rows.astype(F32) * result.astype(F32), axis=1, keepdims=True)
+    dr[:, :, 0:model] = acc_row[...].astype(BF16).reshape(blks, capacity, model)
+    dr[:, :, model : model + LANES] = split_high_low(d_gate, lane_ids((slots, LANES))).reshape(
+        blks, capacity, LANES
+    )
+    dr_copies = blk_copies(dr, da, dr_send, dr_recv)
+    start(dr_copies)
+    da[blk] = dr[blk]
+    po[...] = result.reshape(blks, capacity, model)
+    po_copies = blk_copies(po, pa, po_send, po_recv)
+    start(po_copies)
+    pa[blk] = po[blk]
+    core = lax.rem(head, 2)
+    sibling, across = head - core + 1 - core, around(head, 2, heads)
+    to_sibling = remote(rx.at[head], rx.at[head], rx_send.at[0], rx_recv.at[0], sibling, blk)
+    to_across = remote(rx.at[head], rx.at[head], rx_send.at[1], rx_recv.at[1], across, blk)
+    to_across.start()
+    to_sibling.start()
+
+    finish(dr_copies)
+    back = da[...].reshape(slots, model + LANES)
+    d_routed = dot(put_any, back[:, 0:model])
+    back_gate = back[:, model : model + LANES]
+    d_gates = [join_high_low(dot(p, back_gate), 0) for p in put]
+    d_probs = jnp.where(hots[0], d_gates[0], 0.0) + jnp.where(hots[1], d_gates[1], 0.0)
+    d_logits = probs * (d_probs - jnp.sum(probs * d_probs, axis=1, keepdims=True))
+    d_high = d_logits.astype(BF16)
+    d_low = (d_logits - d_high.astype(F32)).astype(BF16)
+    d_routed = d_routed + dot(d_high, small, (1, 1)) + dot(d_low, small, (1, 1))
+    d_hidden = d_out + centre_back(d_routed * gain, xhat, scale)
+    dh_ref[...] = d_hidden
+    d_attn = d_hidden.astype(BF16)
+    d_mixed = dot(d_attn, weight_out, (1, 1)).astype(BF16)
+    for piece in range(heads):
+        dms[piece] = d_mixed[:, piece * LANES : (piece + 1) * LANES]
+    dm_copies = plane_copies(lambda to_y, to_head: dms.at[to_head], dma_all.at[y, head], dm_send, dm_recv)
+    start(dm_copies)
+    dma_all[y, head] = dms[head]
+
+    d_weight = dot(mixed, d_attn, (0, 0)).astype(BF16)
+    for b in range(blks):
+        grads_ref[b, :, 0:model] = d_weight[(b ^ 1) * HALF : ((b ^ 1) + 1) * HALF, :]
+    last = (lanes == blks).astype(BF16)
+    d_small = dot(routed, d_high, (0, 0)) + dot((d_routed * xhat).astype(BF16), last, (0, 0))
+    grads_ref[:, :, model : model + LANES] = d_small.astype(BF16).reshape(blks, HALF, LANES)
+    finish(po_copies)
+    parts = pa[...].reshape(slots, model)
+    mixture = gates[0] * dot(put[0], parts) + gates[1] * dot(put[1], parts)
+    out_ref[...] = (hidden + mixture).astype(BF16)
+
+    arrived(rx.at[across], rx_recv.at[1])
+    forward = remote(rx.at[across], rx.at[across], rx_send.at[2], rx_recv.at[2], sibling, blk)
+    forward.start()
+    finish(dm_copies)
+    do_copy = pltpu.make_async_copy(dma_all, do_out, out_sem.at[0])
+    do_copy.start()
+    to_sibling.wait()
+    to_across.wait_send()
+    forward.wait()
+    rows_copy = pltpu.make_async_copy(rx, rows_out, out_sem.at[1])
+    rows_copy.start()
+    do_copy.wait()
+    rows_copy.wait()
+
+
+def call_middle(x, o, wo, routes, rank, d_out, win, wout, heads, blks):
+    tokens, model = x.shape
+    capacity = 2 * tokens // blks
+    slots = capacity * blks
+    wide = model + LANES
+
+    def rows(width):
+        return pltpu.VMEM((blks, capacity, width), BF16)
+
+    def block(*lead):
+        return pltpu.VMEM((*lead, tokens, LANES), BF16)
+
+    return pl.pallas_call(
+        functools.partial(middle_kernel, heads, blks),
+        out_shape=(
+            jax.ShapeDtypeStruct((tokens, model), BF16),
+            jax.ShapeDtypeStruct((tokens, model), F32),
+            jax.ShapeDtypeStruct((2, heads, tokens, LANES), BF16),
+            jax.ShapeDtypeStruct((blks, model // blks, wide), BF16),
+            jax.ShapeDtypeStruct((heads, slots, 2 * model), BF16),
+        ),
+        in_specs=vmem_specs(8),
+        out_specs=(*vmem_specs(2), *any_specs(1), *vmem_specs(1), *any_specs(1)),
+        scratch_shapes=[
+            block(2, heads), rows(model), rows(model), rows(wide), rows(wide), rows(model), rows(model),
+            rows(wide), rows(wide), block(heads), block(2, heads),
+            pltpu.VMEM((heads, slots, 2 * model), BF16),
+            pltpu.VMEM((slots, model), F32), pltpu.VMEM((slots, model), F32),
+            pltpu.VMEM((tokens, model), BF16),
+            dma(2 * heads), dma(2 * heads), dma(blks), dma(blks), dma(blks), dma(blks), dma(blks), dma(blks),
+            dma(blks), dma(blks), dma(2 * heads), dma(2 * heads), dma(3), dma(3), dma(2),
+        ],
+        compiler_params=pltpu.CompilerParams(
+            collective_id=2, has_side_effects=True, vmem_limit_bytes=VMEM_LIMIT
+        ),
+        name="experts",
+    )(x, o, wo, routes, rank, d_out, win, wout)
+
+
+def last_kernel(
+    heads, blks,
+    x_ref, dh_ref, dq_ref, dkv_ref, xa_ref, wa_ref, w_ref, g1_ref, grads_ref, rx_ref, win_ref, wout_ref,
+    dx_ref, dw_ref, shared_ref, din_out, dout_out,
+    gain_tile, far_all, near_send_buf, near_all, pair_all, dq_all, us, ua, gs, ga, gh, w1, w2s, w2, w3,
+    din_own, dout_own, din_other, dout_other,
+    q_send, q_recv, pair_send, pair_recv, far_send, far_recv, near_send, near_recv,
+    u_send, u_recv, g_send, g_recv, gh_send, gh_recv, w1_send, w1_recv, w2_send, w2_recv,
+    w3_send, w3_recv, e_send, e_recv, out_sem,
+):
+    head, blk, z, y = place()
+    planes = blks // 2
+    tokens, model = x_ref.shape
+    rows = w_ref.shape[0]
+    greet(
+        [(around(head, k, heads), blk) for k in range(1, heads)]
+        + [(head, around(blk, k, blks)) for k in range(1, blks)]
+    )
+
+    def start(copies):
+        for copy in copies:
+            copy.start()
+
+    def finish(copies):
+        for copy in copies:
+            copy.wait()
+
+    other_y = around(y, 1, 2)
+    pair = 2 * z + other_y
+    above, below = z < planes - 1, z > 0
+    directions = ((1, above, below, 0), (-1, below, above, 2))
+
+    def far_copy(step, slot, side):
+        span = 2 * (z + 2 * step) + side
+        return remote(
+            dkv_ref.at[span], far_all.at[slot + side],
+            far_send.at[slot + side], far_recv.at[slot + side], head, 2 * (z + step) + y,
+        )
+
+    def near_copy(step, slot, side):
+        return remote(
+            near_send_buf.at[slot + side], near_all.at[slot // 2, y],
+            near_send.at[slot + side], near_recv.at[slot // 2, y], head, 2 * (z + step) + side,
+        )
+
+    def two_away(step):
+        return z + 2 * step < planes if step > 0 else z + 2 * step >= 0
+
+    for step, there, back, slot in directions:
+
+        @pl.when(two_away(step))
+        def _():
+            for side in range(2):
+                far_copy(step, slot, side).start()
+
+    pair_copy = remote(dkv_ref.at[pair], pair_all, pair_send, pair_recv, head, pair)
+    pair_copy.start()
+    q_copy = remote(dq_ref.at[other_y], dq_all, q_send, q_recv, head, pair)
+    q_copy.start()
+    w1_copies = [
+        remote(
+            grads_ref.at[:, around(head, k, heads)], w1.at[head],
+            w1_send.at[k], w1_recv.at[k], around(head, k, heads), blk,
+        )
+        for k in range(1, heads)
+    ]
+    start(w1_copies)
+    w1[head] = grads_ref[:, head]
+
+    core = lax.rem(head, 2)
+    sibling = head - core + 1 - core
+    ff_half = wout_ref.shape[0] // 2
+    ff_step = ff_half // 4
+
+    def expert_chunk(chunk):
+        here = pl.multiple_of(core * ff_half + chunk * ff_step, ff_step)
+        there = pl.multiple_of(chunk * ff_step, ff_step)
+        into = win_ref[:, pl.ds(here, ff_step)]
+        outof = wout_ref[pl.ds(here, ff_step), :]
+        d_in = jnp.zeros((model, ff_step), F32)
+        d_out = jnp.zeros((ff_step, model), F32)
+        for source in range(heads):
+            rows_in = rx_ref[source, :, 0:model]
+            grads_out = rx_ref[source, :, model : 2 * model]
+            act, slope = gelu_parts(dot(rows_in, into))
+            d_act = dot(grads_out, outof, (1, 1))
+            d_in = d_in + dot(rows_in, (slope * d_act).astype(BF16), (0, 0))
+            d_out = d_out + dot(act.astype(BF16), grads_out, (0, 0))
+        din_own[:, pl.ds(there, ff_step)] = d_in.astype(BF16)
+        dout_own[pl.ds(there, ff_step), :] = d_out.astype(BF16)
+
+    @pl.loop(0, 2)
+    def _(chunk):
+        expert_chunk(chunk)
+
+    for step, there, back, slot in directions:
+
+        @pl.when(there)
+        def _():
+            for side in range(2):
+                near_send_buf[slot + side] = dkv_ref[2 * (z + step) + side]
+
+        @pl.when(jnp.logical_and(there, back))
+        def _():
+            for side in range(2):
+                arrived(far_all.at[slot + side], far_recv.at[slot + side])
+                near_send_buf[slot + side] = (
+                    near_send_buf[slot + side].astype(F32) + far_all[slot + side].astype(F32)
+                ).astype(BF16)
+
+        @pl.when(there)
+        def _():
+            for side in range(2):
+                near_copy(step, slot, side).start()
+
+    @pl.loop(2, 4)
+    def _(chunk):
+        expert_chunk(chunk)
+
+    e_copies = [
+        remote(din_own, din_other, e_send.at[0], e_recv.at[0], sibling, blk),
+        remote(dout_own, dout_other, e_send.at[1], e_recv.at[1], sibling, blk),
+    ]
+    start(e_copies)
+
+    pair_copy.wait()
+    q_copy.wait()
+    for step, there, back, slot in directions:
+
+        @pl.when(back)
+        def _():
+            for side in range(2):
+                arrived(near_all.at[slot // 2, side], near_recv.at[slot // 2, side])
+
+        @pl.when(jnp.logical_not(back))
+        def _():
+            near_all[slot // 2] = jnp.zeros(near_all.shape[1:], BF16)
+
+    lanes = lane_ids((tokens, LANES))
+    even = y == 0
+    weight = wa_ref[...].reshape(model, 3 * LANES)
+    g_sum = jnp.zeros((model, 3 * LANES), F32)
+    for piece in range(heads):
+        span = slice(piece * tokens, (piece + 1) * tokens)
+        own = dkv_ref[blk, span, :].astype(F32)
+        other = pair_all[span, :].astype(F32)
+        kv_grads = [
+            jnp.where(even, own, other) + near_all[0, 0, span, :].astype(F32) + near_all[1, 0, span, :].astype(F32),
+            jnp.where(even, other, own) + near_all[0, 1, span, :].astype(F32) + near_all[1, 1, span, :].astype(F32),
+        ]
+        q_own = dq_ref[y, span, :]
+        q_other = dq_all[span, :]
+        own_lanes = (lanes < HALF) == even
+        q_grads = jnp.where(own_lanes, q_own, q_other)
+        made = jnp.concatenate([kv_grads[0].astype(BF16), kv_grads[1].astype(BF16), q_grads], axis=1)
+        us[piece] = dot(made, weight, (1, 1)).astype(BF16)
+        g_sum = g_sum + dot(xa_ref[piece], made, (0, 0))
+    u_copies = [
+        remote(
+            us.at[around(head, k, heads)], ua.at[head],
+            u_send.at[k], u_recv.at[k], around(head, k, heads), blk,
+        )
+        for k in range(1, heads)
+    ]
+    start(u_copies)
+    ua[head] = us[head]
+    gs[...] = g_sum.astype(BF16).reshape(gs.shape)
+    g_copies = [
+        remote(
+            gs.at[around(blk, k, blks)], ga.at[blk],
+            g_send.at[k], g_recv.at[k], head, around(blk, k, blks),
+        )
+        for k in range(1, blks)
+    ]
+    start(g_copies)
+    ga[blk] = gs[blk]
+
+    finish(w1_copies)
+    summed = w1[0].astype(F32)
+    for source in range(1, heads):
+        summed = summed + w1[source].astype(F32)
+    w2s[...] = summed.astype(BF16)
+    w2_copies = [
+        remote(
+            w2s.at[around(blk, k, blks)], w2.at[blk],
+            w2_send.at[k], w2_recv.at[k], head, around(blk, k, blks),
+        )
+        for k in range(1, blks)
+    ]
+    start(w2_copies)
+    w2[blk] = w2s[blk]
+
+    finish(e_copies)
+    wide_out = [
+        pltpu.make_async_copy(din_own, din_out.at[core], out_sem.at[0]),
+        pltpu.make_async_copy(din_other, din_out.at[1 - core], out_sem.at[1]),
+        pltpu.make_async_copy(dout_own, dout_out.at[core], out_sem.at[2]),
+        pltpu.make_async_copy(dout_other, dout_out.at[1 - core], out_sem.at[3]),
+    ]
+    start(wide_out)
+
+    finish(u_copies)
+    grad = ua[0].astype(F32)
+    for source in range(1, heads):
+        grad = grad + ua[source].astype(F32)
+    xhat, scale = centre(x_ref[...].astype(F32))
+    dx_ref[...] = dh_ref[...] + centre_back(grad, xhat, scale)
+
+    finish(g_copies)
+    total = ga[0].astype(F32)
+    for source in range(1, blks):
+        total = total + ga[source].astype(F32)
+    gh[head] = total.astype(BF16)
+    gh_copies = [
+        remote(gh.at[head], gh.at[head], gh_send.at[k], gh_recv.at[k], around(head, k, heads), blk)
+        for k in range(1, heads)
+    ]
+    start(gh_copies)
+    finish(w2_copies)
+    part = w2[0].astype(F32)
+    for source in range(1, blks):
+        part = part + w2[source].astype(F32)
+    w3[head] = part.astype(BF16)
+    w3_copies = [
+        remote(w3.at[head], w3.at[head], w3_send.at[k], w3_recv.at[k], around(head, k, heads), blk)
+        for k in range(1, heads)
+    ]
+    start(w3_copies)
+
+    gain_tile[...] = jnp.zeros_like(gain_tile)
+    gain_tile[0:1, 0:rows] = g1_ref[...].astype(F32)
+    gain = jnp.transpose(jnp.broadcast_to(gain_tile[0:1, :], (LANES, LANES)))[:rows]
+    low_half = lane_ids((rows, LANES)) < HALF
+    finish(gh_copies)
+    d_gain = jnp.zeros((rows, LANES), F32)
+    for source in range(heads):
+        both = [gh[source, :, i * LANES : (i + 1) * LANES].astype(F32) for i in range(3)]
+        grads = (
+            both[2] * HS ** (-0.5),
+            jnp.where(low_half, both[0], both[1]),
+            pltpu.roll(jnp.where(low_half, both[1], both[0]), HALF, 1),
+        )
+        for which, value in enumerate(grads):
+            columns = slice(which * model + source * LANES, which * model + (source + 1) * LANES)
+            d_gain = d_gain + value * w_ref[:, columns].astype(F32)
+            dw_ref[:, columns] = value * gain
+    finish(w3_copies)
+    shared = w3[...].reshape(rows, w3.shape[-1]).astype(F32)
+    shared_ref[:, 0:model] = shared[:, 0:model]
+    gain_col = jnp.sum(d_gain, axis=1, keepdims=True)
+    shared_ref[:, model : model + LANES] = jnp.where(
+        lane_ids((rows, LANES)) == blks + 1, gain_col, shared[:, model : model + LANES]
+    )
+    for step, there, back, slot in directions:
+
+        @pl.when(two_away(step))
+        def _():
+            for side in range(2):
+                far_copy(step, slot, side).wait_send()
+
+        @pl.when(there)
+        def _():
+            for side in range(2):
+                near_copy(step, slot, side).wait_send()
+
+    finish(wide_out)
+
+
+def call_last(x, dh, dq, dkv, xa, wa, w_qkv, g1, grads, rx, win, wout, heads, blks):
+    tokens, model = x.shape
+    span = tokens * heads
+    rows = w_qkv.shape[0]
+    wide = model + LANES
+    part = rows // heads
+    ff = wout.shape[0]
+
+    def block(*lead):
+        return pltpu.VMEM((*lead, span, LANES), BF16)
+
+    return pl.pallas_call(
+        functools.partial(last_kernel, heads, blks),
+        out_shape=(
+            jax.ShapeDtypeStruct((tokens, model), F32),
+            jax.ShapeDtypeStruct((rows, 3 * model), F32),
+            jax.ShapeDtypeStruct((rows, wide), F32),
+            jax.ShapeDtypeStruct((2, model, ff // 2), BF16),
+            jax.ShapeDtypeStruct((2, ff // 2, model), BF16),
+        ),
+        in_specs=vmem_specs(12),
+        out_specs=(*vmem_specs(3), *any_specs(2)),
+        scratch_shapes=[
+            pltpu.VMEM((8, LANES), F32),
+            block(4), block(4), block(2, 2), block(), block(),
+            pltpu.VMEM((heads, tokens, model), BF16), pltpu.VMEM((heads, tokens, model), BF16),
+            pltpu.VMEM((blks, rows, 3 * LANES), BF16), pltpu.VMEM((blks, rows, 3 * LANES), BF16),
+            pltpu.VMEM((heads, rows, 3 * LANES), BF16),
+            pltpu.VMEM((heads, blks, part, wide), BF16), pltpu.VMEM((blks, part, wide), BF16),
+            pltpu.VMEM((blks, part, wide), BF16), pltpu.VMEM((heads, part, wide), BF16),
+            pltpu.VMEM((model, ff // 2), BF16), pltpu.VMEM((ff // 2, model), BF16),
+            pltpu.VMEM((model, ff // 2), BF16), pltpu.VMEM((ff // 2, model), BF16),
+            pltpu.SemaphoreType.DMA, pltpu.SemaphoreType.DMA, pltpu.SemaphoreType.DMA, pltpu.SemaphoreType.DMA,
+            dma(4), dma(4), dma(4), dma(2, 2),
+            dma(heads), dma(heads), dma(blks), dma(blks), dma(heads), dma(heads), dma(heads), dma(heads),
+            dma(blks), dma(blks), dma(heads), dma(heads), dma(2), dma(2), dma(4),
+        ],
+        compiler_params=pltpu.CompilerParams(
+            collective_id=3, has_side_effects=True, vmem_limit_bytes=VMEM_LIMIT
+        ),
+        name="last",
+    )(
+        x, dh, dq.reshape(2, span, LANES), dkv, xa, wa, w_qkv, g1.reshape(1, rows),
+        grads.reshape(blks, heads, part, wide), rx, win, wout,
+    )
+
+
+def local_kernels(
+    inputs, ln1_gain, w_qkv, w_out, ln2_gain, w_router,
+    expert_in, expert_out, routes, priority, doc_lengths, d_out,
+):
+    heads, blks = lax.axis_size("head"), lax.axis_size("blk")
+    model = inputs.shape[1]
+    tokens = inputs.shape[0]
+    win, wout = expert_in[0], expert_out[0]
+    q, kv, xa, wa, wo = call_qkv(inputs, w_qkv, ln1_gain, w_out, w_router, ln2_gain, heads, blks)
+    o, o_low, lse = call_forward(doc_lengths, q, kv)
+    output, dh, d_o, grads, rx = call_middle(
+        inputs, o_low.reshape(2, heads, tokens, LANES), wo.reshape(model, model + LANES),
+        routes, priority, d_out, win, wout, heads, blks,
+    )
+    dq, dkv = call_backward(doc_lengths, q, kv, d_o, o, lse)
+    d_inputs, d_qkv, shared, d_in, d_out_weight = call_last(
+        inputs, dh, dq, dkv, xa, wa, w_qkv, ln1_gain, grads, rx, win, wout, heads, blks
+    )
+    return (
+        output,
+        d_inputs,
+        shared[:, model + blks + 1],
+        d_qkv,
+        shared[:, :model],
+        shared[:, model + blks],
+        shared[:, model : model + blks],
+        jnp.concatenate([d_in[0], d_in[1]], axis=1).astype(F32)[None],
+        d_out_weight.reshape(wout.shape).astype(F32)[None],
+    )
+
+
 def solution(mesh):
     in_specs = (
         P(("blk", "head"), None),
@@ -398,4 +1464,6 @@
         P("blk", None, None),
         P("blk", None, None),
     )
-    return jax.shard_map(local, mesh=mesh, in_specs=in_specs, out_specs=out_specs, check_vma=False)
+    fits = mesh.shape["head"] == 4 and mesh.shape["blk"] == 8
+    body = local_kernels if fits else local
+    return jax.shard_map(body, mesh=mesh, in_specs=in_specs, out_specs=out_specs, check_vma=False)

time: 763 us -> 162 us (0.21)
  waiting for transfers between devices: 444 us -> 0 us
  Pallas kernels: 0 us -> 140 us
  blocking collectives: 125 us -> 0 us
  matrix products: 50.5 us -> 0 us
  starting transfers between devices: 43.4 us -> 0 us
  other arithmetic: 34.8 us -> 5.15 us
  loops' own time: 16 us -> 0 us
  between operations: 16.2 us -> 0.76 us
  local copies, waits for them, and re-layouts: 30.1 us -> 15.6 us
    reduce_scatter x4 -> x0, waiting for transfers between devices: 242 us -> none  [the longest x1 70.8 us: local(): lax.psum_scatter(value_grad.astype(jnp.bfloat16), 'blk', scatter_dimensio...]
    pallas_call x0 -> x5, Pallas kernels: none -> 140 us  [the longest x1 48.3 us: call_middle(): pl.pallas_call(functools.partial(middle_kernel, heads, blks), out_shape=(...]
    unnamed x10 -> x0, waiting for transfers between devices: 63.6 us -> none
    psum x1 -> x0, waiting for transfers between devices: 62.7 us -> none  [local(): lax.psum(qkv_sum.astype(jnp.bfloat16), 'head').astype(jnp.float32)]
    all_gather x2 -> x0, blocking collectives: 61.9 us -> none  [the longest x1 33.9 us: local(): lax.all_gather(w_out, 'blk', axis=0, tiled=True)]
    dot_general x26 -> x0, matrix products: 50.5 us -> none  [the longest x1 6.22 us: local(): jnp.dot(expert_rows, weight_in, preferred_element_type=jnp.float32)]
    all_to_all x10 -> x0, starting transfers between devices: 43 us -> none  [the longest x1 12.1 us: local(): lax.all_to_all(send_rows.reshape(blk_size, capacity, model_width), 'blk',...]
    unnamed x2 -> x0, blocking collectives: 42.7 us -> none
  transfers between devices with their start and end apart: 19 -> 0, of which waited for: 16 -> 0; matrix products, arithmetic and copies ran while one was open for 5% -> 0% of each run, Pallas kernels for 0% -> 0%
where the time goes in v1:
time: 162 us
  Pallas kernels  140 us (86%)
  local copies, waits for them, and re-layouts  15.6 us (10%)
  other arithmetic  5.15 us (3%)
    pallas_call x1, Pallas kernels, call_middle(): pl.pallas_call(functools.partial(middle_kernel, heads, blks), out_shape=(...  48.3 us
    pallas_call x1, Pallas kernels, call_last(): pl.pallas_call(functools.partial(last_kernel, heads, blks), out_shape=(ja...  43.4 us
    pallas_call x1, Pallas kernels, call_qkv(): pl.pallas_call(functools.partial(qkv_kernel, heads, blks), out_shape=(jax...  33.3 us
    unnamed x34, local copies, waits for them, and re-layouts  11.8 us
    pallas_call x1, Pallas kernels, call_forward(): pl.pallas_call(forward_kernel, out_shape=(jax.ShapeDtypeStruct((tiles, QU...  7.62 us
    pallas_call x1, Pallas kernels, call_backward(): pl.pallas_call(backward_kernel, out_shape=(jax.ShapeDtypeStruct((tiles, Q...  7.44 us

profile of v1, /device:TPU:0, one launch (start us, length us, event | category | flops | bytes accessed | tf_op | source)
XLA Modules:
  0.0 161.7 jit_solution(17944354019704681182)
XLA Ops:
  0.6 0.8 copy.26.g2_ref
  1.4 0.8 copy.25.wr_ref
  2.2 0.8 copy.27.routes_ref
  3.0 0.0 copy-start
  3.0 0.9 copy-done
  3.9 0.0 copy-start.4
  3.9 0.9 copy-done.4
  4.8 0.0 copy-start.7
  4.8 0.8 copy-done.7
  5.6 0.0 copy-start.10
  5.6 0.7 copy-done.10
  6.3 33.3 %qkv.1 = (bf16[2,512,128]{2,1,0:T(8,128)(2,1)S(1)}, bf16[8,512,128]{2,1,0:T(8,128)(2,1)S(1)}, bf16[4,128,512]{2,1,0:T(8,128)(2,1)S(1)}, bf16[8,64,384]{2,1,0:T(8,128)(2,1)S(1)}, bf16[8,4,16,640]{3,2,1,0:T(8,128)(2,1)S(1)}) custom-call(bf16[128,512]{1,0:T(8,128)(2,1)S(1)} %copy-done, bf16[64,1536]{1,0:T(8,128)(2,1)S(1)} %copy-done.4, ...), custom_call_target="tpu_custom_call" | custom-call | tf_op jit(solution)/shard_map/qkv/pallas_call | solution.py:640
  39.6 0.0 copy-start.8
  39.6 0.6 copy-done.8
  40.3 7.6 %attend.1 = (f32[4,256,128]{2,1,0:T(8,128)S(1)}, bf16[4,256,128]{2,1,0:T(8,128)(2,1)S(1)}, f32[4,8,256]{2,1,0:T(8,128)S(1)}) custom-call(s32[16]{0:T(128)S(1)} %copy-done.8, bf16[2,512,128]{2,1,0:T(8,128)(2,1)S(1)} %get-tuple-element.29.q_ref, bf16[8,512,128]{2,1,0:T(8,128)(2,1)S(1)} %get-tuple-element.30.kv_ref), custom_call_target="tpu_custom_call" | custom-call | tf_op jit(solution)/shard_map/attend/pallas_call | solution.py:750
  47.9 0.0 copy-start.1
  47.9 0.9 copy-done.1
  48.8 0.0 copy-start.6
  48.8 0.9 copy-done.6
  49.8 0.0 copy-start.12
  49.8 0.7 copy-done.12
  50.4 0.0 copy-start.9
  50.4 48.3 %experts.1 = (bf16[128,512]{1,0:T(8,128)(2,1)S(1)}, f32[128,512]{1,0:T(8,128)S(1)}, bf16[2,4,128,128]{3,2,1,0:T(8,128)(2,1)S(1)}, bf16[8,64,640]{2,1,0:T(8,128)(2,1)S(1)}, bf16[4,256,1024]{2,1,0:T(8,128)(2,1)}) custom-call(bf16[128,512]{1,0:T(8,128)(2,1)S(1)} %copy-done.1, bf16[2,4,128,128]{3,2,1,0:T(8,128)(2,1)S(1)} %bitcast.17, ...), custom_call_target="tpu_custom_call" | custom-call | tf_op jit(solution)/shard_map/experts/pallas_call | solution.py:1068
  98.8 0.0 copy-start.2
  98.8 0.0 copy-start.5
  98.8 0.0 copy-start.11
  98.8 0.0 copy-done.9
  98.8 7.4 %attend_back.1 = (bf16[4,256,128]{2,1,0:T(8,128)(2,1)S(1)}, bf16[8,512,128]{2,1,0:T(8,128)(2,1)S(1)}) custom-call(s32[16]{0:T(128)S(1)} %copy-done.9, bf16[2,512,128]{2,1,0:T(8,128)(2,1)S(1)} %get-tuple-element.29.q_ref, bf16[8,512,128]{2,1,0:T(8,128)(2,1)S(1)} %get-tuple-element.30.kv_ref, bf16[4,256,128]{2,1,0:T(8,128)(2,1)S(1)} %bitcast.16, ...), custom_call_target="tpu_custom_call" | custom-call | tf_op jit(solution)/shard_map/attend_back/pallas_call | solution.py:815
  106.3 0.0 copy-start.3
  106.3 1.0 copy-done.3
  107.2 0.0 copy-done.2
  107.2 0.0 copy-done.5
  107.2 0.0 copy-done.11
  107.3 43.4 %last.1 = (f32[128,512]{1,0:T(8,128)S(1)}, f32[64,1536]{1,0:T(8,128)S(1)}, f32[64,640]{1,0:T(8,128)S(1)}, bf16[2,512,1024]{2,1,0:T(8,128)(2,1)}, bf16[2,1024,512]{2,1,0:T(8,128)(2,1)}) custom-call(bf16[128,512]{1,0:T(8,128)(2,1)S(1)} %copy-done.2, f32[128,512]{1,0:T(8,128)S(1)} %get-tuple-element.34.dh_ref, bf16[2,512,128]{2,1,0:T(8,128)(2,1)S(1)} %bitcast.15, ...), custom_call_target="tpu_custom_call" | custom-call | tf_op jit(solution)/shard_map/last/pallas_call | solution.py:1374
  150.7 0.7 slice_reduce_fusion
  151.4 0.7 slice.19
  152.0 0.7 copy.28
  152.7 1.7 %fusion = (bf16[1,512,1024]{2,1,0:T(8,128)(2,1)S(1)}, bf16[1,512,1024]{2,1,0:T(8,128)(2,1)S(1)}) fusion(bf16[2,512,1024]{2,1,0:T(8,128)(2,1)} %get-tuple-element.47), kind=kLoop, calls=%fused_computation.4 | loop fusion | bytes 4194304 | tf_op jit(solution)/shard_map/slice | solution.py:1436
  154.4 0.0 copy-start.13
  154.4 2.6 %maximum_convert_fusion = f32[1,512,2048]{2,1,0:T(8,128)} fusion(bf16[1,512,1024]{2,1,0:T(8,128)(2,1)S(1)} %get-tuple-element.70, bf16[1,512,1024]{2,1,0:T(8,128)(2,1)S(1)} %get-tuple-element.69), kind=kLoop, calls=%fused_computation | loop fusion | flops 4194304 | bytes 6291456 | tf_op jit(solution)/shard_map/convert_element_type | solution.py:1436
  157.0 0.0 copy-done.13
  157.0 2.6 %bitcast_convert_fusion = f32[1,2048,512]{2,1,0:T(8,128)} fusion(bf16[1,2048,512]{2,1,0:T(8,128)(2,1)S(1)} %bitcast.24), kind=kLoop, calls=%fused_computation.1 | loop fusion | flops 1048576 | bytes 6291456 | tf_op jit(solution)/shard_map/convert_element_type | solution.py:1437
  159.6 0.7 copy.32
  160.2 0.7 copy.33
  160.9 0.7 copy.34
  (1 shorter events, 0.0 us)
Async XLA Ops:
  3.0 0.9 copy-start
  3.9 0.9 copy-start.4
  4.8 0.8 copy-start.7
  5.6 0.7 copy-start.10
  39.6 0.7 copy-start.8
  47.9 0.9 copy-start.1
  48.8 0.9 copy-start.6
  49.8 0.7 copy-start.12
  50.4 48.4 %copy-start.9 = (s32[16]{0:T(128)S(1)}, s32[16]{0:T(128)}, u32[]{:S(2)}) copy-start(s32[16]{0:T(128)} %doc_ref.3) | copy-start | bytes 196
  98.8 8.5 %copy-start.2 = (bf16[128,512]{1,0:T(8,128)(2,1)S(1)}, bf16[128,512]{1,0:T(8,128)(2,1)}, u32[]{:S(2)}) copy-start(bf16[128,512]{1,0:T(8,128)(2,1)} %x_ref.5) | copy-start | bytes 393220
  98.8 8.5 %copy-start.5 = (bf16[64,1536]{1,0:T(8,128)(2,1)S(1)}, bf16[64,1536]{1,0:T(8,128)(2,1)}, u32[]{:S(2)}) copy-start(bf16[64,1536]{1,0:T(8,128)(2,1)} %w_ref.3) | copy-start | bytes 589828
  98.8 8.4 %copy-start.11 = (bf16[64]{0:T(256)(128)(2,1)S(1)}, bf16[64]{0:T(256)(128)(2,1)}, u32[]{:S(2)}) copy-start(bf16[64]{0:T(256)(128)(2,1)} %param.13) | copy-start | bytes 388
  106.3 1.0 copy-start.3
  154.4 2.6 %copy-start.13 = (bf16[2,1024,512]{2,1,0:T(8,128)(2,1)S(1)}, bf16[2,1024,512]{2,1,0:T(8,128)(2,1)}, u32[]{:S(2)}) copy-start(bf16[2,1024,512]{2,1,0:T(8,128)(2,1)} %get-tuple-element.48) | copy-start | bytes 6291460

commit v2 on v1

--- a/solution.py
+++ b/solution.py
@@ -381,7 +381,7 @@
 MESH = pl.DeviceIdType.MESH
 LANES = 128
 HALF = LANES // 2
-VMEM_LIMIT = 50 * 2**20
+MIB = 2**20
 F32 = jnp.float32
 BF16 = jnp.bfloat16
 
@@ -457,25 +457,40 @@
 
 def qkv_kernel(
     heads, blks,
-    x_ref, w_ref, g1_ref, wo_ref, wr_ref, g2_ref,
-    q_out, kv_out, xa_out, wa_out, wo_out,
-    gain_tile, xall, wall, wo_own, wo_all, kvall, kv_other, qall,
+    x_hbm, w_hbm, g1_hbm, wo_hbm, wr_hbm, g2_hbm,
+    qall, kvall, xall, wall, wo_all,
+    x_ref, w_ref, rows_in, g1_ref, g2_ref, wr_ref, wo_own, kv_other, in_sem,
     x_send, x_recv, w_send, w_recv, o_send, o_recv, p_send, p_recv,
-    k_send, k_recv, q_recv, out_sem,
+    k_send, k_recv, q_recv,
 ):
     head, blk, z, y = place()
     planes = blks // 2
     model = x_ref.shape[1]
     rows = w_ref.shape[0]
     part = rows // heads
+    experts = wr_ref.shape[0]
+    wanted = (
+        (w_hbm, w_ref), (g1_hbm, g1_ref), (g2_hbm, g2_ref), (wr_hbm, wr_ref), (x_hbm, x_ref),
+        (wo_hbm, wo_own.at[:, pl.ds(0, model)]),
+    )
+    fetched = [
+        pltpu.make_async_copy(src, dst, in_sem.at[i]) for i, (src, dst) in enumerate(wanted)
+    ]
+    for copy in fetched:
+        copy.start()
+    rows_in[...] = jnp.zeros_like(rows_in)
     greet(
         [(around(head, k, heads), blk) for k in range(1, heads)]
         + [(head, around(blk, k, blks)) for k in range(1, blks)]
     )
     lanes = lane_ids((rows, LANES))
-    gain_tile[...] = jnp.zeros_like(gain_tile)
-    gain_tile[0:1, 0:rows] = g1_ref[...].astype(F32)
-    gain = jnp.transpose(jnp.broadcast_to(gain_tile[0:1, :], (LANES, LANES)))[:rows]
+    for copy in fetched:
+        copy.wait()
+    rows_in[0:experts, 0:rows] = wr_ref[...].astype(F32)
+    rows_in[experts : experts + 1, 0:rows] = g2_ref[...].astype(F32)
+    rows_in[experts + 1 : experts + 2, 0:rows] = g1_ref[...].astype(F32)
+    vectors = jnp.transpose(rows_in[...])[:rows]
+    gain = vectors[:, experts + 1 : experts + 2]
 
     def columns(which):
         start = pl.multiple_of(which * model + head * LANES, LANES)
@@ -500,10 +515,7 @@
     ]
     for copy in x_copies:
         copy.start()
-    wo_own[...] = jnp.zeros_like(wo_own)
-    wo_own[:, 0:model] = wo_ref[...]
-    wo_own[:, model : model + wr_ref.shape[1]] = wr_ref[...]
-    wo_own[:, model + wr_ref.shape[1] : model + wr_ref.shape[1] + 1] = g2_ref[...]
+    wo_own[:, model : model + LANES] = vectors.astype(BF16)
     wo_all[blk, head] = wo_own[pl.ds(pl.multiple_of(head * part, part), part), :]
     o_copies = [
         remote(
@@ -594,14 +606,6 @@
     q_pair.wait()
     for copy in p_copies:
         copy.wait()
-    outs = [
-        pltpu.make_async_copy(src, dst, out_sem.at[i])
-        for i, (src, dst) in enumerate(
-            ((qall, q_out), (kvall, kv_out), (xall, xa_out), (wall, wa_out), (wo_all, wo_out))
-        )
-    ]
-    for copy in outs:
-        copy.start()
     to_pair.wait_send()
     for step, there, back, slot in sides:
 
@@ -615,16 +619,17 @@
             for side in range(2):
                 onward(6 + slot + side, step, side).wait_send()
 
-    for copy in outs:
-        copy.wait()
-
 
 def vmem_specs(count):
     return [pl.BlockSpec(memory_space=pltpu.VMEM)] * count
 
 
-def any_specs(count):
-    return [pl.BlockSpec(memory_space=pl.ANY)] * count
+def hbm_specs(count):
+    return [pl.BlockSpec(memory_space=pltpu.HBM)] * count
+
+
+def in_hbm(*arrays):
+    return [pltpu.with_memory_space_constraint(array, pltpu.HBM) for array in arrays]
 
 
 def dma(*shape):
@@ -646,25 +651,26 @@
             jax.ShapeDtypeStruct((blks, rows, 3 * LANES), BF16),
             jax.ShapeDtypeStruct((blks, heads, part, wide), BF16),
         ),
-        in_specs=vmem_specs(6),
-        out_specs=tuple(any_specs(5)),
+        in_specs=hbm_specs(6),
+        out_specs=tuple(vmem_specs(5)),
         scratch_shapes=[
-            pltpu.VMEM((8, LANES), F32),
-            pltpu.VMEM((heads, tokens, model), BF16),
-            pltpu.VMEM((blks, rows, 3 * LANES), BF16),
+            pltpu.VMEM((tokens, model), BF16),
+            pltpu.VMEM((rows, 3 * model), BF16),
+            pltpu.VMEM((LANES, LANES), F32),
+            pltpu.VMEM((1, rows), BF16),
+            pltpu.VMEM((1, rows), BF16),
+            pltpu.VMEM((w_router.shape[1], rows), BF16),
             pltpu.VMEM((rows, wide), BF16),
-            pltpu.VMEM((blks, heads, part, wide), BF16),
-            pltpu.VMEM((blks, span, LANES), BF16),
             pltpu.VMEM((span, LANES), BF16),
-            pltpu.VMEM((2, span, LANES), BF16),
+            dma(6),
             dma(heads), dma(heads), dma(blks), dma(blks), dma(blks), dma(blks), dma(heads), dma(heads),
-            dma(10), dma(blks), pltpu.SemaphoreType.DMA, dma(5),
+            dma(10), dma(blks), pltpu.SemaphoreType.DMA,
         ],
         compiler_params=pltpu.CompilerParams(
-            collective_id=1, has_side_effects=True, vmem_limit_bytes=VMEM_LIMIT
+            collective_id=1, has_side_effects=True, vmem_limit_bytes=16 * MIB
         ),
         name="qkv",
-    )(x, w_qkv, g1.reshape(1, rows), w_out, w_router, g2.reshape(rows, 1))
+    )(*in_hbm(x, w_qkv, g1.reshape(1, rows), w_out, w_router.T, g2.reshape(1, rows)))
 
 
 QUERY_TILE = 256
@@ -699,8 +705,10 @@
             kvt[:, block * size : (block + 1) * size] = jnp.transpose(kv_ref[block])
 
 
-def forward_kernel(doc_ref, q_ref, kv_ref, o_out, ob_out, lse_out, kvt):
+def forward_kernel(doc_hbm, q_ref, kv_ref, o_out, ob_out, lse_out, kvt, doc_ref, doc_sem):
     _, _, z, y = place()
+    pltpu.make_async_copy(doc_hbm, doc_ref, doc_sem).start()
+    pltpu.make_async_copy(doc_hbm, doc_ref, doc_sem).wait()
     total = q_ref.shape[0] * q_ref.shape[1]
     key_columns(doc_ref, kv_ref, kvt, z, total)
     lanes = lane_ids((QUERY_TILE, LANES))
@@ -754,16 +762,24 @@
             jax.ShapeDtypeStruct((tiles, QUERY_TILE, LANES), BF16),
             jax.ShapeDtypeStruct((tiles, 8, QUERY_TILE), F32),
         ),
-        in_specs=[pl.BlockSpec(memory_space=pltpu.SMEM)] + vmem_specs(2),
+        in_specs=hbm_specs(1) + vmem_specs(2),
         out_specs=tuple(vmem_specs(3)),
-        scratch_shapes=[pltpu.VMEM((LANES, blks * span), BF16)],
-        compiler_params=pltpu.CompilerParams(vmem_limit_bytes=VMEM_LIMIT),
+        scratch_shapes=[
+            pltpu.VMEM((LANES, blks * span), BF16),
+            pltpu.SMEM(doc_lengths.shape, jnp.int32),
+            pltpu.SemaphoreType.DMA,
+        ],
+        compiler_params=pltpu.CompilerParams(vmem_limit_bytes=16 * MIB),
         name="attend",
-    )(doc_lengths, q, kv)
-
-
-def backward_kernel(doc_ref, q_ref, kv_ref, do_ref, o_ref, lse_ref, dq_out, dkv_out, kvt, dkv):
+    )(*in_hbm(doc_lengths), q, kv)
+
+
+def backward_kernel(
+    doc_hbm, q_ref, kv_ref, do_ref, o_ref, lse_ref, dq_out, dkv_out, kvt, dkv, doc_ref, doc_sem
+):
     _, _, z, y = place()
+    pltpu.make_async_copy(doc_hbm, doc_ref, doc_sem).start()
+    pltpu.make_async_copy(doc_hbm, doc_ref, doc_sem).wait()
     total = q_ref.shape[0] * q_ref.shape[1]
     key_columns(doc_ref, kv_ref, kvt, z, total)
     dkv[...] = jnp.zeros_like(dkv)
@@ -818,15 +834,17 @@
             jax.ShapeDtypeStruct((tiles, QUERY_TILE, LANES), BF16),
             jax.ShapeDtypeStruct((blks, span, LANES), BF16),
         ),
-        in_specs=[pl.BlockSpec(memory_space=pltpu.SMEM)] + vmem_specs(5),
+        in_specs=hbm_specs(1) + vmem_specs(5),
         out_specs=tuple(vmem_specs(2)),
         scratch_shapes=[
             pltpu.VMEM((LANES, blks * span), BF16),
             pltpu.VMEM((blks, span, LANES), F32),
+            pltpu.SMEM(doc_lengths.shape, jnp.int32),
+            pltpu.SemaphoreType.DMA,
         ],
-        compiler_params=pltpu.CompilerParams(vmem_limit_bytes=VMEM_LIMIT),
+        compiler_params=pltpu.CompilerParams(vmem_limit_bytes=16 * MIB),
         name="attend_back",
-    )(doc_lengths, q, kv, d_o.reshape(tiles, QUERY_TILE, LANES), o, lse)
+    )(*in_hbm(doc_lengths), q, kv, d_o.reshape(tiles, QUERY_TILE, LANES), o, lse)
 
 
 def gelu_parts(values):
@@ -853,20 +871,30 @@
 
 def middle_kernel(
     heads, blks,
-    x_ref, o_ref, wo_ref, routes_ref, rank_ref, d_out_ref, win_ref, wout_ref,
-    out_ref, dh_ref, do_out, grads_ref, rows_out,
-    o_all, dos, doa, rs, ra, po, pa, dr, da, dms, dma_all, rx, acc_out, acc_row, mix,
+    x_hbm, o_ref, wo_ref, routes_hbm, rank_hbm, d_out_hbm, win_hbm, wout_hbm,
+    out_ref, dh_ref, dma_all, grads_ref, rx,
+    x_ref, routes_ref, rank_ref, d_out_ref, win_ref, wout_ref, rows_in, in_sem,
+    o_all, dos, doa, rs, ra, po, pa, dr, da, dms, acc_out, acc_row, mix,
     o_send, o_recv, dos_send, dos_recv, r_send, r_recv, po_send, po_recv,
-    dr_send, dr_recv, dm_send, dm_recv, rx_send, rx_recv, out_sem,
+    dr_send, dr_recv, dm_send, dm_recv, rx_send, rx_recv,
 ):
     head, blk, z, y = place()
     tokens, model = x_ref.shape
     capacity = 2 * tokens // blks
     slots = capacity * blks
     plane = [(k % heads, k // heads) for k in range(1, 2 * heads)]
+    wanted = (
+        (routes_hbm, routes_ref), (rank_hbm, rank_ref), (d_out_hbm, d_out_ref), (x_hbm, x_ref),
+        (win_hbm, win_ref), (wout_hbm, wout_ref),
+    )
+    fetched = [
+        pltpu.make_async_copy(src, dst, in_sem.at[i]) for i, (src, dst) in enumerate(wanted)
+    ]
+    for copy in fetched:
+        copy.start()
     greet(
         [(around(head, kh, heads), 2 * z + around(y, ky, 2)) for kh, ky in plane]
-        + [(head, around(blk, k, blks)) for k in range(1, blks) if True]
+        + [(head, around(blk, k, blks)) for k in range(1, blks)]
     )
 
     def plane_copies(src_of, dst, send, recv):
@@ -900,12 +928,15 @@
     o_all[y, head] = o_ref[y, head]
 
     lanes = lane_ids((tokens, LANES))
-    routes = routes_ref[...].astype(F32)
-    e_cols = [routes[:, 0:1], routes[:, 1:2]]
-    e_mix = jnp.transpose(jnp.where(lanes == 0, e_cols[0], e_cols[1]))
-    e_rows = [e_mix[0:1, :], e_mix[1:2, :]]
+    for copy in fetched[:4]:
+        copy.wait()
+    e_rows = [routes_ref[i : i + 1, :].astype(F32) for i in range(2)]
     rank_row = rank_ref[...].astype(F32)
-    rank_col = jnp.transpose(jnp.broadcast_to(rank_row, (tokens, tokens)))[:, 0:1]
+    rows_in[...] = jnp.zeros_like(rows_in)
+    rows_in[0:1, :], rows_in[1:2, :], rows_in[2:3, :] = *e_rows, rank_row
+    columns = jnp.transpose(rows_in[...])
+    e_cols = [columns[:, 0:1], columns[:, 1:2]]
+    rank_col = columns[:, 2:3]
     pos_rows, pos_cols = positions(e_rows, e_cols, rank_row, rank_col)
 
     def slot_of(expert, position):
@@ -976,6 +1007,8 @@
     rx[head, :, 0:model] = arrived_rows[:, 0:model]
     rx[head, :, model : 2 * model] = (out_rows.astype(F32) * gate_col).astype(BF16)
     half_ff = wout_ref.shape[0] // 4
+    for copy in fetched[4:]:
+        copy.wait()
 
     @pl.loop(0, 4)
     def _(chunk):
@@ -998,7 +1031,6 @@
     da[blk] = dr[blk]
     po[...] = result.reshape(blks, capacity, model)
     po_copies = blk_copies(po, pa, po_send, po_recv)
-    start(po_copies)
     pa[blk] = po[blk]
     core = lax.rem(head, 2)
     sibling, across = head - core + 1 - core, around(head, 2, heads)
@@ -1008,6 +1040,7 @@
     to_sibling.start()
 
     finish(dr_copies)
+    start(po_copies)
     back = da[...].reshape(slots, model + LANES)
     d_routed = dot(put_any, back[:, 0:model])
     back_gate = back[:, model : model + LANES]
@@ -1042,15 +1075,9 @@
     forward = remote(rx.at[across], rx.at[across], rx_send.at[2], rx_recv.at[2], sibling, blk)
     forward.start()
     finish(dm_copies)
-    do_copy = pltpu.make_async_copy(dma_all, do_out, out_sem.at[0])
-    do_copy.start()
     to_sibling.wait()
     to_across.wait_send()
     forward.wait()
-    rows_copy = pltpu.make_async_copy(rx, rows_out, out_sem.at[1])
-    rows_copy.start()
-    do_copy.wait()
-    rows_copy.wait()
 
 
 def call_middle(x, o, wo, routes, rank, d_out, win, wout, heads, blks):
@@ -1074,38 +1101,53 @@
             jax.ShapeDtypeStruct((blks, model // blks, wide), BF16),
             jax.ShapeDtypeStruct((heads, slots, 2 * model), BF16),
         ),
-        in_specs=vmem_specs(8),
-        out_specs=(*vmem_specs(2), *any_specs(1), *vmem_specs(1), *any_specs(1)),
+        in_specs=hbm_specs(1) + vmem_specs(2) + hbm_specs(5),
+        out_specs=tuple(vmem_specs(5)),
         scratch_shapes=[
+            pltpu.VMEM((tokens, model), BF16),
+            pltpu.VMEM((2, tokens), jnp.int32),
+            pltpu.VMEM((1, tokens), jnp.int32),
+            pltpu.VMEM((tokens, model), F32),
+            pltpu.VMEM(win.shape, BF16),
+            pltpu.VMEM(wout.shape, BF16),
+            pltpu.VMEM((tokens, tokens), F32),
+            dma(6),
             block(2, heads), rows(model), rows(model), rows(wide), rows(wide), rows(model), rows(model),
-            rows(wide), rows(wide), block(heads), block(2, heads),
-            pltpu.VMEM((heads, slots, 2 * model), BF16),
+            rows(wide), rows(wide), block(heads),
             pltpu.VMEM((slots, model), F32), pltpu.VMEM((slots, model), F32),
             pltpu.VMEM((tokens, model), BF16),
             dma(2 * heads), dma(2 * heads), dma(blks), dma(blks), dma(blks), dma(blks), dma(blks), dma(blks),
-            dma(blks), dma(blks), dma(2 * heads), dma(2 * heads), dma(3), dma(3), dma(2),
+            dma(blks), dma(blks), dma(2 * heads), dma(2 * heads), dma(3), dma(3),
         ],
         compiler_params=pltpu.CompilerParams(
-            collective_id=2, has_side_effects=True, vmem_limit_bytes=VMEM_LIMIT
+            collective_id=2, has_side_effects=True, vmem_limit_bytes=20 * MIB
         ),
         name="experts",
-    )(x, o, wo, routes, rank, d_out, win, wout)
+    )(*in_hbm(x), o, wo, *in_hbm(routes.T, rank, d_out, win, wout))
 
 
 def last_kernel(
     heads, blks,
-    x_ref, dh_ref, dq_ref, dkv_ref, xa_ref, wa_ref, w_ref, g1_ref, grads_ref, rx_ref, win_ref, wout_ref,
-    dx_ref, dw_ref, shared_ref, din_out, dout_out,
+    x_hbm, dh_ref, dq_ref, dkv_ref, xa_ref, wa_ref, w_hbm, g1_hbm, grads_ref, rx_ref, win_hbm, wout_hbm,
+    dx_ref, dw_ref, shared_ref, din_ref, dout_ref,
+    x_ref, w_ref, g1_ref, win_ref, wout_ref, in_sem,
     gain_tile, far_all, near_send_buf, near_all, pair_all, dq_all, us, ua, gs, ga, gh, w1, w2s, w2, w3,
-    din_own, dout_own, din_other, dout_other,
     q_send, q_recv, pair_send, pair_recv, far_send, far_recv, near_send, near_recv,
     u_send, u_recv, g_send, g_recv, gh_send, gh_recv, w1_send, w1_recv, w2_send, w2_recv,
-    w3_send, w3_recv, e_send, e_recv, out_sem,
+    w3_send, w3_recv, e_send, e_recv,
 ):
     head, blk, z, y = place()
     planes = blks // 2
     tokens, model = x_ref.shape
     rows = w_ref.shape[0]
+    wanted = (
+        (win_hbm, win_ref), (wout_hbm, wout_ref), (x_hbm, x_ref), (w_hbm, w_ref), (g1_hbm, g1_ref)
+    )
+    fetched = [
+        pltpu.make_async_copy(src, dst, in_sem.at[i]) for i, (src, dst) in enumerate(wanted)
+    ]
+    for copy in fetched:
+        copy.start()
     greet(
         [(around(head, k, heads), blk) for k in range(1, heads)]
         + [(head, around(blk, k, blks)) for k in range(1, blks)]
@@ -1180,8 +1222,10 @@
             d_act = dot(grads_out, outof, (1, 1))
             d_in = d_in + dot(rows_in, (slope * d_act).astype(BF16), (0, 0))
             d_out = d_out + dot(act.astype(BF16), grads_out, (0, 0))
-        din_own[:, pl.ds(there, ff_step)] = d_in.astype(BF16)
-        dout_own[pl.ds(there, ff_step), :] = d_out.astype(BF16)
+        din_ref[core, :, pl.ds(there, ff_step)] = d_in.astype(BF16)
+        dout_ref[core, pl.ds(there, ff_step), :] = d_out.astype(BF16)
+
+    finish(fetched)
 
     @pl.loop(0, 2)
     def _(chunk):
@@ -1212,8 +1256,8 @@
         expert_chunk(chunk)
 
     e_copies = [
-        remote(din_own, din_other, e_send.at[0], e_recv.at[0], sibling, blk),
-        remote(dout_own, dout_other, e_send.at[1], e_recv.at[1], sibling, blk),
+        remote(din_ref.at[core], din_ref.at[core], e_send.at[0], e_recv.at[0], sibling, blk),
+        remote(dout_ref.at[core], dout_ref.at[core], e_send.at[1], e_recv.at[1], sibling, blk),
     ]
     start(e_copies)
 
@@ -1284,15 +1328,6 @@
     start(w2_copies)
     w2[blk] = w2s[blk]
 
-    finish(e_copies)
-    wide_out = [
-        pltpu.make_async_copy(din_own, din_out.at[core], out_sem.at[0]),
-        pltpu.make_async_copy(din_other, din_out.at[1 - core], out_sem.at[1]),
-        pltpu.make_async_copy(dout_own, dout_out.at[core], out_sem.at[2]),
-        pltpu.make_async_copy(dout_other, dout_out.at[1 - core], out_sem.at[3]),
-    ]
-    start(wide_out)
-
     finish(u_copies)
     grad = ua[0].astype(F32)
     for source in range(1, heads):
@@ -1357,7 +1392,7 @@
             for side in range(2):
                 near_copy(step, slot, side).wait_send()
 
-    finish(wide_out)
+    finish(e_copies)
 
 
 def call_last(x, dh, dq, dkv, xa, wa, w_qkv, g1, grads, rx, win, wout, heads, blks):
@@ -1380,9 +1415,15 @@
             jax.ShapeDtypeStruct((2, model, ff // 2), BF16),
             jax.ShapeDtypeStruct((2, ff // 2, model), BF16),
         ),
-        in_specs=vmem_specs(12),
-        out_specs=(*vmem_specs(3), *any_specs(2)),
+        in_specs=hbm_specs(1) + vmem_specs(5) + hbm_specs(2) + vmem_specs(2) + hbm_specs(2),
+        out_specs=tuple(vmem_specs(5)),
         scratch_shapes=[
+            pltpu.VMEM((tokens, model), BF16),
+            pltpu.VMEM((rows, 3 * model), BF16),
+            pltpu.VMEM((1, rows), BF16),
+            pltpu.VMEM(win.shape, BF16),
+            pltpu.VMEM(wout.shape, BF16),
+            dma(5),
             pltpu.VMEM((8, LANES), F32),
             block(4), block(4), block(2, 2), block(), block(),
             pltpu.VMEM((heads, tokens, model), BF16), pltpu.VMEM((heads, tokens, model), BF16),
@@ -1390,21 +1431,95 @@
             pltpu.VMEM((heads, rows, 3 * LANES), BF16),
             pltpu.VMEM((heads, blks, part, wide), BF16), pltpu.VMEM((blks, part, wide), BF16),
             pltpu.VMEM((blks, part, wide), BF16), pltpu.VMEM((heads, part, wide), BF16),
-            pltpu.VMEM((model, ff // 2), BF16), pltpu.VMEM((ff // 2, model), BF16),
-            pltpu.VMEM((model, ff // 2), BF16), pltpu.VMEM((ff // 2, model), BF16),
             pltpu.SemaphoreType.DMA, pltpu.SemaphoreType.DMA, pltpu.SemaphoreType.DMA, pltpu.SemaphoreType.DMA,
             dma(4), dma(4), dma(4), dma(2, 2),
             dma(heads), dma(heads), dma(blks), dma(blks), dma(heads), dma(heads), dma(heads), dma(heads),
-            dma(blks), dma(blks), dma(heads), dma(heads), dma(2), dma(2), dma(4),
+            dma(blks), dma(blks), dma(heads), dma(heads), dma(2), dma(2),
         ],
         compiler_params=pltpu.CompilerParams(
-            collective_id=3, has_side_effects=True, vmem_limit_bytes=VMEM_LIMIT
+            collective_id=3, has_side_effects=True, vmem_limit_bytes=24 * MIB
         ),
         name="last",
     )(
-        x, dh, dq.reshape(2, span, LANES), dkv, xa, wa, w_qkv, g1.reshape(1, rows),
-        grads.reshape(blks, heads, part, wide), rx, win, wout,
-    )
+        *in_hbm(x), dh, dq.reshape(2, span, LANES), dkv, xa, wa, *in_hbm(w_qkv, g1.reshape(1, rows)),
+        grads.reshape(blks, heads, part, wide), rx, *in_hbm(win, wout),
+    )
+
+
+def finish_kernel(
+    experts,
+    dx_ref, dw_ref, shared_ref, din_ref, dout_ref,
+    dx_out, g1_out, dw_out, dwo_out, g2_out, wr_out, din_out, dout_out,
+    tile, wr, g2, g1, din, dout, sem, wide_sem,
+):
+    rows = shared_ref.shape[0]
+    model = dx_ref.shape[1]
+    copies = [
+        pltpu.make_async_copy(dx_ref, dx_out, sem.at[0]),
+        pltpu.make_async_copy(dw_ref, dw_out, sem.at[1]),
+        pltpu.make_async_copy(shared_ref.at[:, pl.ds(0, model)], dwo_out, sem.at[2]),
+    ]
+    for copy in copies:
+        copy.start()
+    half = dout_ref.shape[1]
+    quarter = half // 2
+    for piece in range(4):
+        down = slice(piece * quarter, (piece + 1) * quarter)
+        dout[down, :] = dout_ref[piece // 2, (piece % 2) * quarter : (piece % 2 + 1) * quarter, :].astype(F32)
+        copies.append(pltpu.make_async_copy(dout.at[down], dout_out.at[down], wide_sem.at[piece]))
+        copies[-1].start()
+    step = model // 4
+    for piece in range(4):
+        down = slice(piece * step, (piece + 1) * step)
+        for side in range(2):
+            din[down, side * half : (side + 1) * half] = din_ref[side, down, :].astype(F32)
+        copies.append(pltpu.make_async_copy(din.at[down], din_out.at[down], wide_sem.at[4 + piece]))
+        copies[-1].start()
+    tile[...] = jnp.zeros_like(tile)
+    tile[0:rows, :] = shared_ref[:, model : model + LANES]
+    across = jnp.transpose(tile[...])[:, 0:rows]
+    wr[...] = across[0:experts]
+    g2[...] = across[experts : experts + 1]
+    g1[...] = across[experts + 1 : experts + 2]
+    for index, (src, dst) in enumerate(((wr, wr_out), (g2, g2_out), (g1, g1_out))):
+        copies.append(pltpu.make_async_copy(src, dst, sem.at[3 + index]))
+        copies[-1].start()
+    for copy in copies:
+        copy.wait()
+
+
+def call_finish(dx, dw, shared, d_in, d_out):
+    rows = shared.shape[0]
+    model = dx.shape[1]
+    experts = model // rows
+    ff = 2 * d_out.shape[1]
+    return pl.pallas_call(
+        functools.partial(finish_kernel, experts),
+        out_shape=(
+            jax.ShapeDtypeStruct(dx.shape, F32),
+            jax.ShapeDtypeStruct((1, rows), F32),
+            jax.ShapeDtypeStruct(dw.shape, F32),
+            jax.ShapeDtypeStruct((rows, model), F32),
+            jax.ShapeDtypeStruct((1, rows), F32),
+            jax.ShapeDtypeStruct((experts, rows), F32),
+            jax.ShapeDtypeStruct((model, ff), F32),
+            jax.ShapeDtypeStruct((ff, model), F32),
+        ),
+        in_specs=vmem_specs(5),
+        out_specs=tuple(hbm_specs(8)),
+        scratch_shapes=[
+            pltpu.VMEM((LANES, LANES), F32),
+            pltpu.VMEM((experts, rows), F32),
+            pltpu.VMEM((1, rows), F32),
+            pltpu.VMEM((1, rows), F32),
+            pltpu.VMEM((model, ff), F32),
+            pltpu.VMEM((ff, model), F32),
+            dma(6),
+            dma(8),
+        ],
+        compiler_params=pltpu.CompilerParams(vmem_limit_bytes=16 * MIB),
+        name="finish",
+    )(dx, dw, shared, d_in, d_out)
 
 
 def local_kernels(
@@ -1422,19 +1537,20 @@
         routes, priority, d_out, win, wout, heads, blks,
     )
     dq, dkv = call_backward(doc_lengths, q, kv, d_o, o, lse)
-    d_inputs, d_qkv, shared, d_in, d_out_weight = call_last(
+    ends = call_last(
         inputs, dh, dq, dkv, xa, wa, w_qkv, ln1_gain, grads, rx, win, wout, heads, blks
     )
+    d_inputs, d_gain_one, d_qkv, d_out_proj, d_gain_two, d_router, d_in, d_out_weight = call_finish(*ends)
     return (
         output,
         d_inputs,
-        shared[:, model + blks + 1],
+        d_gain_one.reshape(-1),
         d_qkv,
-        shared[:, :model],
-        shared[:, model + blks],
-        shared[:, model : model + blks],
-        jnp.concatenate([d_in[0], d_in[1]], axis=1).astype(F32)[None],
-        d_out_weight.reshape(wout.shape).astype(F32)[None],
+        d_out_proj,
+        d_gain_two.reshape(-1),
+        d_router.T,
+        d_in[None],
+        d_out_weight[None],
     )
 
 

time: 162 us -> 141 us (0.87)
  local copies, waits for them, and re-layouts: 15.6 us -> 0.66 us
  other arithmetic: 5.15 us -> 0 us
    unnamed x34 -> x1, local copies, waits for them, and re-layouts: 11.8 us -> 0.66 us
    pallas_call x1, Pallas kernels: 43.4 us -> 37.5 us  [call_last(): pl.pallas_call(functools.partial(last_kernel, heads, blks), out_shape=(ja...]
    convert_element_type x2 -> x0, other arithmetic: 5.15 us -> none  [the longest x1 2.6 us: local_kernels(): d_out_weight.reshape(wout.shape).astype(F32)[None]]
    pallas_call x1, Pallas kernels: 48.3 us -> 43.6 us  [call_middle(): pl.pallas_call(functools.partial(middle_kernel, heads, blks), out_shape=(...]
    pallas_call x0 -> x1, Pallas kernels: none -> 3.7 us  [call_finish(): pl.pallas_call(functools.partial(finish_kernel, experts), out_shape=(jax....]
    pallas_call x1, Pallas kernels: 7.62 us -> 10.8 us  [call_forward(): pl.pallas_call(forward_kernel, out_shape=(jax.ShapeDtypeStruct((tiles, QU...]
    slice x4 -> x0, local copies, waits for them, and re-layouts: 3.08 us -> none  [the longest x1 1.71 us: local_kernels(): d_in[0]]
    pallas_call x1, Pallas kernels: 7.44 us -> 10.3 us  [call_backward(): pl.pallas_call(backward_kernel, out_shape=(jax.ShapeDtypeStruct((tiles, Q...]
where the time goes in v2:
time: 141 us; the launch traced here: 140 us
  Pallas kernels  139 us (99%)
    pallas_call x1, Pallas kernels, call_middle(): pl.pallas_call(functools.partial(middle_kernel, heads, blks), out_shape=(...  43.6 us
    pallas_call x1, Pallas kernels, call_last(): pl.pallas_call(functools.partial(last_kernel, heads, blks), out_shape=(ja...  37.5 us
    pallas_call x1, Pallas kernels, call_qkv(): pl.pallas_call(functools.partial(qkv_kernel, heads, blks), out_shape=(jax...  32.8 us
    pallas_call x1, Pallas kernels, call_forward(): pl.pallas_call(forward_kernel, out_shape=(jax.ShapeDtypeStruct((tiles, QU...  10.8 us
    pallas_call x1, Pallas kernels, call_backward(): pl.pallas_call(backward_kernel, out_shape=(jax.ShapeDtypeStruct((tiles, Q...  10.3 us
    pallas_call x1, Pallas kernels, call_finish(): pl.pallas_call(functools.partial(finish_kernel, experts), out_shape=(jax....  3.7 us

profile of v2, /device:TPU:0, one launch (start us, length us, event | category | flops | bytes accessed | tf_op | source)
XLA Modules:
  0.0 140.1 jit_solution(12440020892144355059)
XLA Ops:
  0.6 32.8 %qkv.1 = (bf16[2,512,128]{2,1,0:T(8,128)(2,1)S(1)}, bf16[8,512,128]{2,1,0:T(8,128)(2,1)S(1)}, bf16[4,128,512]{2,1,0:T(8,128)(2,1)S(1)}, bf16[8,64,384]{2,1,0:T(8,128)(2,1)S(1)}, bf16[8,4,16,640]{3,2,1,0:T(8,128)(2,1)S(1)}) custom-call(bf16[128,512]{1,0:T(8,128)(2,1)} %x_hbm.5, bf16[64,1536]{1,0:T(8,128)(2,1)} %w_hbm.3, bf16[1,64]{1,0:T(2,128)(2,1)} %bitcast.26, ...), custom_call_target="tpu_custom_call" | custom-call | tf_op jit(solution)/shard_map/qkv/pallas_call | solution.py:645
  33.5 10.8 %attend.1 = (f32[4,256,128]{2,1,0:T(8,128)S(1)}, bf16[4,256,128]{2,1,0:T(8,128)(2,1)S(1)}, f32[4,8,256]{2,1,0:T(8,128)S(1)}) custom-call(s32[16]{0:T(128)} %doc_hbm.3, bf16[2,512,128]{2,1,0:T(8,128)(2,1)S(1)} %get-tuple-element.37.q_ref, bf16[8,512,128]{2,1,0:T(8,128)(2,1)S(1)} %get-tuple-element.38.kv_ref), custom_call_target="tpu_custom_call" | custom-call | tf_op jit(solution)/shard_map/attend/pallas_call | solution.py:758
  44.3 43.6 %experts.1 = (bf16[128,512]{1,0:T(8,128)(2,1)S(1)}, f32[128,512]{1,0:T(8,128)S(1)}, bf16[2,4,128,128]{3,2,1,0:T(8,128)(2,1)S(1)}, bf16[8,64,640]{2,1,0:T(8,128)(2,1)S(1)}, bf16[4,256,1024]{2,1,0:T(8,128)(2,1)S(1)}) custom-call(bf16[128,512]{1,0:T(8,128)(2,1)} %x_hbm.5, bf16[2,4,128,128]{3,2,1,0:T(8,128)(2,1)S(1)} %bitcast.20, bf16[512,640]{1,0:T(8,128)(2,1)S(1)} %bitcast.17, ...), custom_call_target="tpu_custom_call" | custom-call | tf_op jit(solution)/shard_map/experts/pallas_call | solution.py:1095
  87.9 10.3 %attend_back.1 = (bf16[4,256,128]{2,1,0:T(8,128)(2,1)S(1)}, bf16[8,512,128]{2,1,0:T(8,128)(2,1)S(1)}) custom-call(s32[16]{0:T(128)} %doc_hbm.3, bf16[2,512,128]{2,1,0:T(8,128)(2,1)S(1)} %get-tuple-element.37.q_ref, bf16[8,512,128]{2,1,0:T(8,128)(2,1)S(1)} %get-tuple-element.38.kv_ref, bf16[4,256,128]{2,1,0:T(8,128)(2,1)S(1)} %bitcast.19, ...), custom_call_target="tpu_custom_call" | custom-call | tf_op jit(solution)/shard_map/attend_back/pallas_call | solution.py:831
  98.2 37.5 %last.1 = (f32[128,512]{1,0:T(8,128)S(1)}, f32[64,1536]{1,0:T(8,128)S(1)}, f32[64,640]{1,0:T(8,128)S(1)}, bf16[2,512,1024]{2,1,0:T(8,128)(2,1)S(1)}, bf16[2,1024,512]{2,1,0:T(8,128)(2,1)S(1)}) custom-call(bf16[128,512]{1,0:T(8,128)(2,1)} %x_hbm.5, f32[128,512]{1,0:T(8,128)S(1)} %get-tuple-element.42.dh_ref, bf16[2,512,128]{2,1,0:T(8,128)(2,1)S(1)} %bitcast.18, ...), custom_call_target="tpu_custom_call" | custom-call | tf_op jit(solution)/shard_map/last/pallas_call | solution.py:1409
  135.7 3.7 %finish.1 = (f32[128,512]{1,0:T(8,128)}, f32[1,64]{1,0:T(1,128)}, f32[64,1536]{1,0:T(8,128)}, f32[64,512]{1,0:T(8,128)}, f32[1,64]{1,0:T(1,128)}, /*index=5*/f32...) custom-call(f32[128,512]{1,0:T(8,128)S(1)} %get-tuple-element.52.dx_ref, f32[64,1536]{1,0:T(8,128)S(1)} %get-tuple-element.53.dw_ref, ...), custom_call_target="tpu_custom_call" | custom-call | tf_op jit(solution)/shard_map/finish/pallas_call | solution.py:1496
  139.4 0.7 copy.22

commit v3 on v2

--- a/solution.py
+++ b/solution.py
@@ -457,9 +457,9 @@
 
 def qkv_kernel(
     heads, blks,
-    x_hbm, w_hbm, g1_hbm, wo_hbm, wr_hbm, g2_hbm,
-    qall, kvall, xall, wall, wo_all,
-    x_ref, w_ref, rows_in, g1_ref, g2_ref, wr_ref, wo_own, kv_other, in_sem,
+    x_hbm, w_hbm, g1_hbm, wo_hbm, wr_hbm, g2_hbm, docs_hbm,
+    qall, kvall, xall, wall, wo_all, kvt, bounds,
+    x_ref, w_ref, rows_in, g1_ref, g2_ref, wr_ref, docs_ref, wo_own, kv_other, in_sem,
     x_send, x_recv, w_send, w_recv, o_send, o_recv, p_send, p_recv,
     k_send, k_recv, q_recv,
 ):
@@ -471,7 +471,7 @@
     experts = wr_ref.shape[0]
     wanted = (
         (w_hbm, w_ref), (g1_hbm, g1_ref), (g2_hbm, g2_ref), (wr_hbm, wr_ref), (x_hbm, x_ref),
-        (wo_hbm, wo_own.at[:, pl.ds(0, model)]),
+        (wo_hbm, wo_own.at[:, pl.ds(0, model)]), (docs_hbm, docs_ref),
     )
     fetched = [
         pltpu.make_async_copy(src, dst, in_sem.at[i]) for i, (src, dst) in enumerate(wanted)
@@ -526,6 +526,7 @@
     ]
     for copy in o_copies:
         copy.start()
+    document_bounds(docs_ref, bounds, z)
     for copy in x_copies:
         copy.wait()
     for copy in w_copies:
@@ -543,6 +544,10 @@
     above, below = z < planes - 1, z > 0
     own = kvall.at[blk]
 
+    def turn(span):
+        size = kvall.shape[1]
+        kvt[:, pl.ds(pl.multiple_of(span * size, size), size)] = jnp.transpose(kvall[span])
+
     def outward(slot, step, across):
         target = 2 * (z + step) + around(y, across, 2)
         return remote(kv_other if across else own, own, k_send.at[slot], k_recv.at[blk], head, target)
@@ -564,6 +569,7 @@
     to_pair.start()
     q_pair = remote(qall.at[y], qall.at[y], k_send.at[5], q_recv, head, 2 * z + around(y, 1, 2))
     q_pair.start()
+    turn(blk)
     for copy in o_copies:
         copy.wait()
     p_copies = [
@@ -575,6 +581,9 @@
     ]
     for copy in p_copies:
         copy.start()
+    pair = 2 * z + around(y, 1, 2)
+    arrived(kvall.at[pair], k_recv.at[pair])
+    turn(pair)
     for step, there, back, slot in sides:
 
         @pl.when(back)
@@ -588,21 +597,22 @@
             for side in range(2):
                 onward(6 + slot + side, step, side).start()
 
-    far = jnp.zeros(kv_other.shape, BF16)
+    for step, there, back, slot in sides:
+
+        @pl.when(back)
+        def _():
+            for side in range(2):
+                turn(2 * (z - step) + side)
+
     for other in range(planes):
         for side in range(2):
             span = 2 * other + side
 
-            @pl.when(jnp.logical_or(z - other > 2, other - z > 2))
-            def _():
-                kvall[span] = far
-
             @pl.when(jnp.logical_or(z - other == 2, other - z == 2))
             def _():
                 arrived(kvall.at[span], k_recv.at[span])
-
-    pair = 2 * z + around(y, 1, 2)
-    arrived(kvall.at[pair], k_recv.at[pair])
+                turn(span)
+
     q_pair.wait()
     for copy in p_copies:
         copy.wait()
@@ -620,6 +630,21 @@
                 onward(6 + slot + side, step, side).wait_send()
 
 
+def document_bounds(docs_ref, bounds, z):
+    count = docs_ref.shape[1]
+    lengths = docs_ref[...].astype(F32)
+    doc = lax.broadcasted_iota(jnp.int32, (count, count), 0)
+    other = lane_ids((count, count))
+    start = jnp.sum(jnp.where(other < doc, lengths, 0.0), axis=1, keepdims=True)
+    end = jnp.sum(jnp.where(other <= doc, lengths, 0.0), axis=1, keepdims=True)
+    queries = bounds.shape[1]
+    token = (z * queries + lane_ids((count, queries))).astype(F32)
+    begun = start <= token
+    bounds[...] = jnp.zeros_like(bounds)
+    bounds[0:1, :] = jnp.max(jnp.where(begun, start, 0.0), axis=0, keepdims=True).astype(jnp.int32)
+    bounds[1:2, :] = jnp.max(jnp.where(begun, end, 0.0), axis=0, keepdims=True).astype(jnp.int32)
+
+
 def vmem_specs(count):
     return [pl.BlockSpec(memory_space=pltpu.VMEM)] * count
 
@@ -636,7 +661,7 @@
     return pltpu.SemaphoreType.DMA(shape)
 
 
-def call_qkv(x, w_qkv, g1, w_out, w_router, g2, heads, blks):
+def call_qkv(x, w_qkv, g1, w_out, w_router, g2, doc_lengths, heads, blks):
     tokens, model = x.shape
     rows = w_qkv.shape[0]
     span = tokens * heads
@@ -650,9 +675,11 @@
             jax.ShapeDtypeStruct((heads, tokens, model), BF16),
             jax.ShapeDtypeStruct((blks, rows, 3 * LANES), BF16),
             jax.ShapeDtypeStruct((blks, heads, part, wide), BF16),
+            jax.ShapeDtypeStruct((LANES, blks * span), BF16),
+            jax.ShapeDtypeStruct((8, 2 * span), jnp.int32),
         ),
-        in_specs=hbm_specs(6),
-        out_specs=tuple(vmem_specs(5)),
+        in_specs=hbm_specs(7),
+        out_specs=tuple(vmem_specs(7)),
         scratch_shapes=[
             pltpu.VMEM((tokens, model), BF16),
             pltpu.VMEM((rows, 3 * model), BF16),
@@ -660,9 +687,10 @@
             pltpu.VMEM((1, rows), BF16),
             pltpu.VMEM((1, rows), BF16),
             pltpu.VMEM((w_router.shape[1], rows), BF16),
+            pltpu.VMEM((1, doc_lengths.shape[0]), jnp.int32),
             pltpu.VMEM((rows, wide), BF16),
             pltpu.VMEM((span, LANES), BF16),
-            dma(6),
+            dma(7),
             dma(heads), dma(heads), dma(blks), dma(blks), dma(blks), dma(blks), dma(heads), dma(heads),
             dma(10), dma(blks), pltpu.SemaphoreType.DMA,
         ],
@@ -670,89 +698,79 @@
             collective_id=1, has_side_effects=True, vmem_limit_bytes=16 * MIB
         ),
         name="qkv",
-    )(*in_hbm(x, w_qkv, g1.reshape(1, rows), w_out, w_router.T, g2.reshape(1, rows)))
+    )(
+        *in_hbm(
+            x, w_qkv, g1.reshape(1, rows), w_out, w_router.T, g2.reshape(1, rows),
+            doc_lengths.reshape(1, -1),
+        )
+    )
 
 
 QUERY_TILE = 256
-KEY_TILE = 512
-
-
-def tile_docs(doc_ref, first, size):
-    token = first + lane_ids((1, size))
-    last = first + size - 1
-    start = jnp.int32(0)
-    low_row, high_row = jnp.zeros((1, size), jnp.int32), jnp.zeros((1, size), jnp.int32)
-    low = low_last = high = jnp.int32(0)
-    for index in range(doc_ref.shape[0]):
-        end = start + doc_ref[index]
-        low_row = jnp.where(token >= start, start, low_row)
-        high_row = jnp.where(token >= start, end, high_row)
-        low = jnp.where(first >= start, start, low)
-        low_last = jnp.where(last >= start, start, low_last)
-        high = jnp.where(last >= start, end, high)
-        start = end
-    return low_row, high_row, low, high, low == low_last
-
-
-def key_columns(doc_ref, kv_ref, kvt, z, span):
-    _, _, low, _, _ = tile_docs(doc_ref, z * span, LANES)
-    _, _, _, high, _ = tile_docs(doc_ref, (z + 1) * span - LANES, LANES)
-    for block in range(kv_ref.shape[0]):
-        size = kv_ref.shape[1]
-
-        @pl.when(jnp.logical_and(block * size < high, (block + 1) * size > low))
-        def _():
-            kvt[:, block * size : (block + 1) * size] = jnp.transpose(kv_ref[block])
-
-
-def forward_kernel(doc_hbm, q_ref, kv_ref, o_out, ob_out, lse_out, kvt, doc_ref, doc_sem):
+CHAINS = 2
+
+
+def masked_queries(q_ref, tile, key_lanes, query_tile):
+    tiles_per_span = q_ref.shape[1] // query_tile
+    inner = tile % tiles_per_span * query_tile
+    query = q_ref[tile // tiles_per_span, inner : inner + query_tile, :]
+    return jnp.where(key_lanes, query, jnp.zeros_like(query))
+
+
+def group_blocks(bounds_ref, group, size, key_tile):
+    first, last = group * size, (group + 1) * size
+    low = jnp.min(bounds_ref[0:1, first : first + LANES])
+    high = jnp.max(bounds_ref[1:2, last - LANES : last])
+    return low // key_tile, (high + key_tile - 1) // key_tile
+
+
+def inside_document(bounds_ref, tile, first, shape):
+    key = first + lax.broadcasted_iota(jnp.int32, shape, 0)
+    columns = slice(tile * shape[1], (tile + 1) * shape[1])
+    return jnp.logical_and(key >= bounds_ref[0:1, columns], key < bounds_ref[1:2, columns])
+
+
+def forward_kernel(bounds_ref, q_ref, kv_ref, kvt_ref, o_out, ob_out, lse_out):
     _, _, z, y = place()
-    pltpu.make_async_copy(doc_hbm, doc_ref, doc_sem).start()
-    pltpu.make_async_copy(doc_hbm, doc_ref, doc_sem).wait()
+    key_tile = kv_ref.shape[1]
     total = q_ref.shape[0] * q_ref.shape[1]
-    key_columns(doc_ref, kv_ref, kvt, z, total)
-    lanes = lane_ids((QUERY_TILE, LANES))
-    tiles_per_span = q_ref.shape[1] // QUERY_TILE
-    key_lanes = (lanes < HALF) == (y == 0)
-    for tile in range(total // QUERY_TILE):
-        inner = tile % tiles_per_span * QUERY_TILE
-        query = q_ref[tile // tiles_per_span, inner : inner + QUERY_TILE, :]
-        query = jnp.where(key_lanes, query, jnp.zeros_like(query))
-        low_row, high_row, low, high, single = tile_docs(
-            doc_ref, z * total + tile * QUERY_TILE, QUERY_TILE
-        )
-
-        def step(block, carry, query=query, low_row=low_row, high_row=high_row):
-            biggest, weight, mixed = carry
-            first = pl.multiple_of(block * KEY_TILE, KEY_TILE)
-            scores = dot(kv_ref[block], query, (1, 1))
-            key = first + lax.broadcasted_iota(jnp.int32, scores.shape, 0)
-            inside = jnp.logical_and(key >= low_row, key < high_row)
-            scores = jnp.where(inside, scores, MASKED)
-            bigger = jnp.maximum(biggest, jnp.max(scores, axis=0, keepdims=True))
-            fade = jnp.exp(biggest - bigger)
-            terms = jnp.where(inside, jnp.exp(scores - bigger), 0.0)
-            weight = weight * fade + jnp.sum(terms, axis=0, keepdims=True)
-            mixed = mixed * fade + dot(kvt[:, pl.ds(first, KEY_TILE)], terms.astype(BF16))
-            return bigger, weight, mixed
-
-        biggest, weight, mixed = lax.fori_loop(
-            low // KEY_TILE,
-            (high + KEY_TILE - 1) // KEY_TILE,
-            step,
-            (
-                jnp.full((1, QUERY_TILE), MASKED, F32),
-                jnp.zeros((1, QUERY_TILE), F32),
-                jnp.zeros((LANES, QUERY_TILE), F32),
-            ),
-        )
-        result = jnp.transpose(mixed / weight)
-        o_out[tile] = result
-        ob_out[tile] = result.astype(BF16)
-        lse_out[tile] = jnp.broadcast_to(biggest + jnp.log(weight), (8, QUERY_TILE))
-
-
-def call_forward(doc_lengths, q, kv):
+    key_lanes = (lane_ids((QUERY_TILE, LANES)) < HALF) == (y == 0)
+    group_size = CHAINS * QUERY_TILE
+    for group in range(total // group_size):
+        tiles = range(group * CHAINS, (group + 1) * CHAINS)
+        queries = [masked_queries(q_ref, tile, key_lanes, QUERY_TILE) for tile in tiles]
+        low, high = group_blocks(bounds_ref, group, group_size, key_tile)
+
+        def step(block, carry, queries=queries, tiles=tiles):
+            first = pl.multiple_of(block * key_tile, key_tile)
+            keys = kv_ref[block]
+            keys_across = kvt_ref[:, pl.ds(first, key_tile)]
+            scores = [dot(keys, query, (1, 1)) for query in queries]
+            made = []
+            for tile, score, (biggest, weight, mixed) in zip(tiles, scores, carry):
+                inside = inside_document(bounds_ref, tile, first, score.shape)
+                score = jnp.where(inside, score, MASKED)
+                bigger = jnp.maximum(biggest, jnp.max(score, axis=0, keepdims=True))
+                fade = jnp.exp(biggest - bigger)
+                terms = jnp.exp(score - bigger)
+                weight = weight * fade + jnp.sum(terms, axis=0, keepdims=True)
+                made.append((bigger, weight, mixed * fade + dot(keys_across, terms.astype(BF16))))
+            return tuple(made)
+
+        start = (
+            jnp.full((1, QUERY_TILE), MASKED, F32),
+            jnp.zeros((1, QUERY_TILE), F32),
+            jnp.zeros((LANES, QUERY_TILE), F32),
+        )
+        ends = lax.fori_loop(low, high, step, (start,) * CHAINS)
+        for tile, (biggest, weight, mixed) in zip(tiles, ends):
+            result = jnp.transpose(mixed / weight)
+            o_out[tile] = result
+            ob_out[tile] = result.astype(BF16)
+            lse_out[tile] = jnp.broadcast_to(biggest + jnp.log(weight), (8, QUERY_TILE))
+
+
+def call_forward(bounds, q, kv, kvt):
     blks, span, _ = kv.shape
     tiles = 2 * span // QUERY_TILE
     return pl.pallas_call(
@@ -762,70 +780,62 @@
             jax.ShapeDtypeStruct((tiles, QUERY_TILE, LANES), BF16),
             jax.ShapeDtypeStruct((tiles, 8, QUERY_TILE), F32),
         ),
-        in_specs=hbm_specs(1) + vmem_specs(2),
+        in_specs=vmem_specs(4),
         out_specs=tuple(vmem_specs(3)),
-        scratch_shapes=[
-            pltpu.VMEM((LANES, blks * span), BF16),
-            pltpu.SMEM(doc_lengths.shape, jnp.int32),
-            pltpu.SemaphoreType.DMA,
-        ],
         compiler_params=pltpu.CompilerParams(vmem_limit_bytes=16 * MIB),
         name="attend",
-    )(*in_hbm(doc_lengths), q, kv)
+    )(bounds, q, kv, kvt)
 
 
 def backward_kernel(
-    doc_hbm, q_ref, kv_ref, do_ref, o_ref, lse_ref, dq_out, dkv_out, kvt, dkv, doc_ref, doc_sem
+    bounds_ref, q_ref, kv_ref, kvt_ref, do_ref, o_ref, lse_ref, dq_out, dkv_out, dkv
 ):
     _, _, z, y = place()
-    pltpu.make_async_copy(doc_hbm, doc_ref, doc_sem).start()
-    pltpu.make_async_copy(doc_hbm, doc_ref, doc_sem).wait()
+    key_tile = kv_ref.shape[1]
     total = q_ref.shape[0] * q_ref.shape[1]
-    key_columns(doc_ref, kv_ref, kvt, z, total)
     dkv[...] = jnp.zeros_like(dkv)
-    lanes = lane_ids((QUERY_TILE, LANES))
-    tiles_per_span = q_ref.shape[1] // QUERY_TILE
-    key_lanes = (lanes < HALF) == (y == 0)
-    for tile in range(total // QUERY_TILE):
-        inner = tile % tiles_per_span * QUERY_TILE
-        query = q_ref[tile // tiles_per_span, inner : inner + QUERY_TILE, :]
-        query = jnp.where(key_lanes, query, jnp.zeros_like(query))
-        out_grad = do_ref[tile]
-        out_grad = jnp.where(key_lanes, jnp.zeros_like(out_grad), out_grad)
-        delta = jnp.sum(
-            jnp.transpose(out_grad.astype(F32) * o_ref[tile]), axis=0, keepdims=True
-        )
-        log_total = lse_ref[tile, 0:1, :]
-        low_row, high_row, low, high, single = tile_docs(
-            doc_ref, z * total + tile * QUERY_TILE, QUERY_TILE
-        )
+    key_lanes = (lane_ids((QUERY_TILE, LANES)) < HALF) == (y == 0)
+    group_size = CHAINS * QUERY_TILE
+    for group in range(total // group_size):
+        tiles = range(group * CHAINS, (group + 1) * CHAINS)
+        queries, out_grads, deltas, log_totals = [], [], [], []
+        for tile in tiles:
+            queries.append(masked_queries(q_ref, tile, key_lanes, QUERY_TILE))
+            out_grad = do_ref[tile]
+            out_grads.append(jnp.where(key_lanes, jnp.zeros_like(out_grad), out_grad))
+            product = jnp.transpose(out_grads[-1].astype(F32) * o_ref[tile])
+            deltas.append(jnp.sum(product, axis=0, keepdims=True))
+            log_totals.append(lse_ref[tile, 0:1, :])
+        low, high = group_blocks(bounds_ref, group, group_size, key_tile)
 
         def step(
-            block, mixed, query=query, out_grad=out_grad, delta=delta, log_total=log_total,
-            low_row=low_row, high_row=high_row,
+            block, carry, queries=queries, out_grads=out_grads, deltas=deltas,
+            log_totals=log_totals, tiles=tiles,
         ):
-            first = pl.multiple_of(block * KEY_TILE, KEY_TILE)
-            scores = dot(kv_ref[block], query, (1, 1))
-            key = first + lax.broadcasted_iota(jnp.int32, scores.shape, 0)
-            inside = jnp.logical_and(key >= low_row, key < high_row)
-            weights = jnp.where(inside, jnp.exp(scores - log_total), 0.0)
-            weight_grads = dot(kv_ref[block], out_grad, (1, 1))
-            score_grads = (weights * (weight_grads - delta)).astype(BF16)
-            dkv[block] += dot(score_grads, query) + dot(weights.astype(BF16), out_grad)
-            return mixed + dot(kvt[:, pl.ds(first, KEY_TILE)], score_grads)
-
-        mixed = lax.fori_loop(
-            low // KEY_TILE,
-            (high + KEY_TILE - 1) // KEY_TILE,
-            step,
-            jnp.zeros((LANES, QUERY_TILE), F32),
-        )
-        dq_out[tile] = jnp.transpose(mixed).astype(BF16)
+            first = pl.multiple_of(block * key_tile, key_tile)
+            keys = kv_ref[block]
+            keys_across = kvt_ref[:, pl.ds(first, key_tile)]
+            scores = [dot(keys, query, (1, 1)) for query in queries]
+            weight_grads = [dot(keys, out_grad, (1, 1)) for out_grad in out_grads]
+            pieces, score_grads = [], []
+            for i, tile in enumerate(tiles):
+                inside = inside_document(bounds_ref, tile, first, scores[i].shape)
+                weights = jnp.exp(jnp.where(inside, scores[i], MASKED) - log_totals[i])
+                score_grads.append((weights * (weight_grads[i] - deltas[i])).astype(BF16))
+                pieces.append(weights.astype(BF16))
+            wide = jnp.concatenate(score_grads + pieces, axis=1)
+            dkv[block] += dot(wide, jnp.concatenate(queries + out_grads, axis=0))
+            return tuple(c + dot(keys_across, s) for c, s in zip(carry, score_grads))
+
+        zero = jnp.zeros((LANES, QUERY_TILE), F32)
+        ends = lax.fori_loop(low, high, step, (zero,) * CHAINS)
+        for tile, mixed in zip(tiles, ends):
+            dq_out[tile] = jnp.transpose(mixed).astype(BF16)
     for block in range(dkv.shape[0]):
         dkv_out[block] = dkv[block].astype(BF16)
 
 
-def call_backward(doc_lengths, q, kv, d_o, o, lse):
+def call_backward(bounds, q, kv, kvt, d_o, o, lse):
     blks, span, _ = kv.shape
     tiles = 2 * span // QUERY_TILE
     return pl.pallas_call(
@@ -834,17 +844,12 @@
             jax.ShapeDtypeStruct((tiles, QUERY_TILE, LANES), BF16),
             jax.ShapeDtypeStruct((blks, span, LANES), BF16),
         ),
-        in_specs=hbm_specs(1) + vmem_specs(5),
+        in_specs=vmem_specs(7),
         out_specs=tuple(vmem_specs(2)),
-        scratch_shapes=[
-            pltpu.VMEM((LANES, blks * span), BF16),
-            pltpu.VMEM((blks, span, LANES), F32),
-            pltpu.SMEM(doc_lengths.shape, jnp.int32),
-            pltpu.SemaphoreType.DMA,
-        ],
+        scratch_shapes=[pltpu.VMEM((blks, span, LANES), F32)],
         compiler_params=pltpu.CompilerParams(vmem_limit_bytes=16 * MIB),
         name="attend_back",
-    )(*in_hbm(doc_lengths), q, kv, d_o.reshape(tiles, QUERY_TILE, LANES), o, lse)
+    )(bounds, q, kv, kvt, d_o.reshape(tiles, QUERY_TILE, LANES), o, lse)
 
 
 def gelu_parts(values):
@@ -1448,8 +1453,8 @@
 
 def finish_kernel(
     experts,
-    dx_ref, dw_ref, shared_ref, din_ref, dout_ref,
-    dx_out, g1_out, dw_out, dwo_out, g2_out, wr_out, din_out, dout_out,
+    y_ref, dx_ref, dw_ref, shared_ref, din_ref, dout_ref,
+    y_out, dx_out, g1_out, dw_out, dwo_out, g2_out, wr_out, din_out, dout_out,
     tile, wr, g2, g1, din, dout, sem, wide_sem,
 ):
     rows = shared_ref.shape[0]
@@ -1458,6 +1463,7 @@
         pltpu.make_async_copy(dx_ref, dx_out, sem.at[0]),
         pltpu.make_async_copy(dw_ref, dw_out, sem.at[1]),
         pltpu.make_async_copy(shared_ref.at[:, pl.ds(0, model)], dwo_out, sem.at[2]),
+        pltpu.make_async_copy(y_ref, y_out, sem.at[6]),
     ]
     for copy in copies:
         copy.start()
@@ -1488,7 +1494,7 @@
         copy.wait()
 
 
-def call_finish(dx, dw, shared, d_in, d_out):
+def call_finish(output, dx, dw, shared, d_in, d_out):
     rows = shared.shape[0]
     model = dx.shape[1]
     experts = model // rows
@@ -1496,6 +1502,7 @@
     return pl.pallas_call(
         functools.partial(finish_kernel, experts),
         out_shape=(
+            jax.ShapeDtypeStruct(output.shape, BF16),
             jax.ShapeDtypeStruct(dx.shape, F32),
             jax.ShapeDtypeStruct((1, rows), F32),
             jax.ShapeDtypeStruct(dw.shape, F32),
@@ -1505,8 +1512,8 @@
             jax.ShapeDtypeStruct((model, ff), F32),
             jax.ShapeDtypeStruct((ff, model), F32),
         ),
-        in_specs=vmem_specs(5),
-        out_specs=tuple(hbm_specs(8)),
+        in_specs=vmem_specs(6),
+        out_specs=tuple(hbm_specs(9)),
         scratch_shapes=[
             pltpu.VMEM((LANES, LANES), F32),
             pltpu.VMEM((experts, rows), F32),
@@ -1514,12 +1521,12 @@
             pltpu.VMEM((1, rows), F32),
             pltpu.VMEM((model, ff), F32),
             pltpu.VMEM((ff, model), F32),
-            dma(6),
+            dma(7),
             dma(8),
         ],
         compiler_params=pltpu.CompilerParams(vmem_limit_bytes=16 * MIB),
         name="finish",
-    )(dx, dw, shared, d_in, d_out)
+    )(output, dx, dw, shared, d_in, d_out)
 
 
 def local_kernels(
@@ -1530,17 +1537,19 @@
     model = inputs.shape[1]
     tokens = inputs.shape[0]
     win, wout = expert_in[0], expert_out[0]
-    q, kv, xa, wa, wo = call_qkv(inputs, w_qkv, ln1_gain, w_out, w_router, ln2_gain, heads, blks)
-    o, o_low, lse = call_forward(doc_lengths, q, kv)
+    q, kv, xa, wa, wo, kvt, bounds = call_qkv(
+        inputs, w_qkv, ln1_gain, w_out, w_router, ln2_gain, doc_lengths, heads, blks
+    )
+    o, o_low, lse = call_forward(bounds, q, kv, kvt)
     output, dh, d_o, grads, rx = call_middle(
         inputs, o_low.reshape(2, heads, tokens, LANES), wo.reshape(model, model + LANES),
         routes, priority, d_out, win, wout, heads, blks,
     )
-    dq, dkv = call_backward(doc_lengths, q, kv, d_o, o, lse)
+    dq, dkv = call_backward(bounds, q, kv, kvt, d_o, o, lse)
     ends = call_last(
         inputs, dh, dq, dkv, xa, wa, w_qkv, ln1_gain, grads, rx, win, wout, heads, blks
     )
-    d_inputs, d_gain_one, d_qkv, d_out_proj, d_gain_two, d_router, d_in, d_out_weight = call_finish(*ends)
+    output, d_inputs, d_gain_one, d_qkv, d_out_proj, d_gain_two, d_router, d_in, d_out_weight = call_finish(output, *ends)
     return (
         output,
         d_inputs,

time: 141 us -> 133 us (0.943)
  Pallas kernels: 139 us -> 131 us
    pallas_call x1, Pallas kernels: 10.8 us -> 4.29 us  [call_forward(): pl.pallas_call(forward_kernel, out_shape=(jax.ShapeDtypeStruct((tiles, QU...]
    pallas_call x1, Pallas kernels: 10.3 us -> 5.6 us  [call_backward(): pl.pallas_call(backward_kernel, out_shape=(jax.ShapeDtypeStruct((tiles, Q...]
    pallas_call x1, Pallas kernels: 37.5 us -> 39.7 us  [call_last(): pl.pallas_call(functools.partial(last_kernel, heads, blks), out_shape=(ja...]
    pallas_call x1, Pallas kernels: 32.8 us -> 34.3 us  [call_qkv(): pl.pallas_call(functools.partial(qkv_kernel, heads, blks), out_shape=(jax...]
where the time goes in v3:
time: 133 us; the launch traced here: 131 us
  Pallas kernels  131 us (98%)
    pallas_call x1, Pallas kernels, call_middle(): pl.pallas_call(functools.partial(middle_kernel, heads, blks), out_shape=(...  42.9 us
    pallas_call x1, Pallas kernels, call_last(): pl.pallas_call(functools.partial(last_kernel, heads, blks), out_shape=(ja...  39.7 us
    pallas_call x1, Pallas kernels, call_qkv(): pl.pallas_call(functools.partial(qkv_kernel, heads, blks), out_shape=(jax...  34.3 us
    pallas_call x1, Pallas kernels, call_backward(): pl.pallas_call(backward_kernel, out_shape=(jax.ShapeDtypeStruct((tiles, Q...  5.6 us
    pallas_call x1, Pallas kernels, call_forward(): pl.pallas_call(forward_kernel, out_shape=(jax.ShapeDtypeStruct((tiles, QU...  4.29 us
    pallas_call x1, Pallas kernels, call_finish(): pl.pallas_call(functools.partial(finish_kernel, experts), out_shape=(jax....  3.75 us

profile of v3, /device:TPU:0, one launch (start us, length us, event | category | flops | bytes accessed | tf_op | source)
XLA Modules:
  0.0 131.4 jit_solution(13113684822283070167)
XLA Ops:
  0.6 34.3 %qkv.1 = (bf16[2,512,128]{2,1,0:T(8,128)(2,1)S(1)}, bf16[8,512,128]{2,1,0:T(8,128)(2,1)S(1)}, bf16[4,128,512]{2,1,0:T(8,128)(2,1)S(1)}, bf16[8,64,384]{2,1,0:T(8...) custom-call(bf16[128,512]{1,0:T(8,128)(2,1)} %x_hbm.5, ...), custom_call_target="tpu_custom_call" | custom-call | tf_op jit(solution)/shard_map/qkv/pallas_call | solution.py:670
  35.0 4.3 %attend.1 = (f32[4,256,128]{2,1,0:T(8,128)S(1)}, bf16[4,256,128]{2,1,0:T(8,128)(2,1)S(1)}, f32[4,8,256]{2,1,0:T(8,128)S(1)}) custom-call(s32[8,1024]{1,0:T(8,128)S(1)} %get-tuple-element.40.bounds_ref, bf16[2,512,128]{2,1,0:T(8,128)(2,1)S(1)} %get-tuple-element.41.q_ref, bf16[8,512,128]{2,1,0:T(8,128)(2,1)S(1)} %get-tuple-element.42.kv_ref, ...), custom_call_target="tpu_custom_call" | custom-call | tf_op jit(solution)/shard_map/attend/pallas_call | solution.py:776
  39.3 42.9 %experts.1 = (bf16[128,512]{1,0:T(8,128)(2,1)S(1)}, f32[128,512]{1,0:T(8,128)S(1)}, bf16[2,4,128,128]{3,2,1,0:T(8,128)(2,1)S(1)}, bf16[8,64,640]{2,1,0:T(8,128)(2,1)S(1)}, bf16[4,256,1024]{2,1,0:T(8,128)(2,1)S(1)}) custom-call(bf16[128,512]{1,0:T(8,128)(2,1)} %x_hbm.5, bf16[2,4,128,128]{3,2,1,0:T(8,128)(2,1)S(1)} %bitcast.21, bf16[512,640]{1,0:T(8,128)(2,1)S(1)} %bitcast.18, ...), custom_call_target="tpu_custom_call" | custom-call | tf_op jit(solution)/shard_map/experts/pallas_call | solution.py:1100
  82.2 5.6 %attend_back.1 = (bf16[4,256,128]{2,1,0:T(8,128)(2,1)S(1)}, bf16[8,512,128]{2,1,0:T(8,128)(2,1)S(1)}) custom-call(s32[8,1024]{1,0:T(8,128)S(1)} %get-tuple-element.40.bounds_ref, bf16[2,512,128]{2,1,0:T(8,128)(2,1)S(1)} %get-tuple-element.41.q_ref, bf16[8,512,128]{2,1,0:T(8,128)(2,1)S(1)} %get-tuple-element.42.kv_ref, ...), custom_call_target="tpu_custom_call" | custom-call | tf_op jit(solution)/shard_map/attend_back/pallas_call | solution.py:841
  87.8 39.7 %last.1 = (f32[128,512]{1,0:T(8,128)S(1)}, f32[64,1536]{1,0:T(8,128)S(1)}, f32[64,640]{1,0:T(8,128)S(1)}, bf16[2,512,1024]{2,1,0:T(8,128)(2,1)S(1)}, bf16[2,1024,512]{2,1,0:T(8,128)(2,1)S(1)}) custom-call(bf16[128,512]{1,0:T(8,128)(2,1)} %x_hbm.5, f32[128,512]{1,0:T(8,128)S(1)} %get-tuple-element.47.dh_ref, bf16[2,512,128]{2,1,0:T(8,128)(2,1)S(1)} %bitcast.19, ...), custom_call_target="tpu_custom_call" | custom-call | tf_op jit(solution)/shard_map/last/pallas_call | solution.py:1414
  127.5 3.7 %finish.1 = (bf16[128,512]{1,0:T(8,128)(2,1)}, f32[128,512]{1,0:T(8,128)}, f32[1,64]{1,0:T(1,128)}, f32[64,1536]{1,0:T(8,128)}, f32[64,512]{1,0:T(8,128)}, /*ind...) custom-call(bf16[128,512]{1,0:T(8,128)(2,1)S(1)} %get-tuple-element.46.y_ref, ...), custom_call_target="tpu_custom_call" | custom-call | tf_op jit(solution)/shard_map/finish/pallas_call | solution.py:1502

commit v4 on v3

--- a/solution.py
+++ b/solution.py
@@ -413,7 +413,17 @@
         pl.semaphore_signal(
             barrier, inc=1, device_id={"head": head, "blk": blk}, device_id_type=MESH
         )
-    pl.semaphore_wait(barrier, len(peers))
+    return len(peers)
+
+
+def meet(count):
+    pl.semaphore_wait(pltpu.get_barrier_semaphore(), count)
+
+
+def halves(values, lanes_kept):
+    rows = values.shape[0] // 2
+    moved = pltpu.roll(values[rows:], HALF, 1)
+    return jnp.where(lanes_kept, values[:rows], moved)
 
 
 def lane_ids(shape):
@@ -479,7 +489,7 @@
     for copy in fetched:
         copy.start()
     rows_in[...] = jnp.zeros_like(rows_in)
-    greet(
+    met = greet(
         [(around(head, k, heads), blk) for k in range(1, heads)]
         + [(head, around(blk, k, blks)) for k in range(1, blks)]
     )
@@ -505,10 +515,11 @@
         remote(wall.at[blk], wall.at[blk], w_send.at[k], w_recv.at[k], head, around(blk, k, blks))
         for k in range(1, blks)
     ]
+    xhat, _ = centre(x_ref[...].astype(F32))
+    xall[head] = xhat.astype(BF16)
+    meet(met)
     for copy in w_copies:
         copy.start()
-    xhat, _ = centre(x_ref[...].astype(F32))
-    xall[head] = xhat.astype(BF16)
     x_copies = [
         remote(xall.at[head], xall.at[head], x_send.at[k], x_recv.at[k], around(head, k, heads), blk)
         for k in range(1, heads)
@@ -534,40 +545,49 @@
     weight = wall[...].reshape(model, 3 * LANES)
     tokens = x_ref.shape[0]
     even = y == 0
-    for piece in range(heads):
-        made = dot(xall[piece], weight).astype(BF16)
-        first, second = made[:, 0:LANES], made[:, LANES : 2 * LANES]
-        span = slice(piece * tokens, (piece + 1) * tokens)
-        kvall[blk, span, :] = jnp.where(even, first, second)
-        kv_other[span, :] = jnp.where(even, second, first)
-        qall[y, span, :] = made[:, 2 * LANES : 3 * LANES]
     above, below = z < planes - 1, z > 0
-    own = kvall.at[blk]
+    half_span = kvall.shape[1] // 2
+    sides = ((1, above, below, 0), (-1, below, above, 4))
+
+    def half_of(ref, half):
+        return ref.at[pl.ds(half * half_span, half_span)]
+
+    def outward(slot, step, across, half):
+        target = 2 * (z + step) + around(y, across, 2)
+        return remote(
+            half_of(kv_other if across else kvall.at[blk], half), half_of(kvall.at[blk], half),
+            k_send.at[slot], k_recv.at[blk, half], head, target,
+        )
+
+    def onward(slot, step, side, half):
+        from_span = 2 * (z - step) + side
+        ref = half_of(kvall.at[from_span], half)
+        return remote(ref, ref, k_send.at[slot], k_recv.at[from_span, half], head, 2 * (z + step) + y)
+
+    def await_half(span, half):
+        arrived(half_of(kvall.at[span], half), k_recv.at[span, half])
 
     def turn(span):
         size = kvall.shape[1]
         kvt[:, pl.ds(pl.multiple_of(span * size, size), size)] = jnp.transpose(kvall[span])
 
-    def outward(slot, step, across):
-        target = 2 * (z + step) + around(y, across, 2)
-        return remote(kv_other if across else own, own, k_send.at[slot], k_recv.at[blk], head, target)
-
-    def onward(slot, step, side):
-        from_span = 2 * (z - step) + side
-        ref = kvall.at[from_span]
-        return remote(ref, ref, k_send.at[slot], k_recv.at[from_span], head, 2 * (z + step) + y)
-
-    sides = ((1, above, below, 0), (-1, below, above, 2))
-    for step, there, _, slot in sides:
-
-        @pl.when(there)
-        def _():
-            outward(slot, step, 0).start()
-            outward(slot + 1, step, 1).start()
-
-    to_pair = outward(4, 0, 1)
-    to_pair.start()
-    q_pair = remote(qall.at[y], qall.at[y], k_send.at[5], q_recv, head, 2 * z + around(y, 1, 2))
+    for half in range(2):
+        for piece in range(half * heads // 2, (half + 1) * heads // 2):
+            made = dot(xall[piece], weight).astype(BF16)
+            first, second = made[:, 0:LANES], made[:, LANES : 2 * LANES]
+            span = slice(piece * tokens, (piece + 1) * tokens)
+            kvall[blk, span, :] = jnp.where(even, first, second)
+            kv_other[span, :] = jnp.where(even, second, first)
+            qall[y, span, :] = made[:, 2 * LANES : 3 * LANES]
+        for step, there, _, slot in sides:
+
+            @pl.when(there)
+            def _():
+                outward(slot + 2 * half, step, 0, half).start()
+                outward(slot + 2 * half + 1, step, 1, half).start()
+
+        outward(8 + half, 0, 1, half).start()
+    q_pair = remote(qall.at[y], qall.at[y], k_send.at[10], q_recv, head, 2 * z + around(y, 1, 2))
     q_pair.start()
     turn(blk)
     for copy in o_copies:
@@ -581,22 +601,23 @@
     ]
     for copy in p_copies:
         copy.start()
+    for half in range(2):
+        for step, there, back, slot in sides:
+
+            @pl.when(back)
+            def _():
+                for side in range(2):
+                    await_half(2 * (z - step) + side, half)
+
+            @pl.when(jnp.logical_and(there, back))
+            def _():
+                for side in range(2):
+                    onward(11 + slot + 2 * half + side, step, side, half).start()
+
     pair = 2 * z + around(y, 1, 2)
-    arrived(kvall.at[pair], k_recv.at[pair])
+    for half in range(2):
+        await_half(pair, half)
     turn(pair)
-    for step, there, back, slot in sides:
-
-        @pl.when(back)
-        def _():
-            for side in range(2):
-                span = 2 * (z - step) + side
-                arrived(kvall.at[span], k_recv.at[span])
-
-        @pl.when(jnp.logical_and(there, back))
-        def _():
-            for side in range(2):
-                onward(6 + slot + side, step, side).start()
-
     for step, there, back, slot in sides:
 
         @pl.when(back)
@@ -610,24 +631,26 @@
 
             @pl.when(jnp.logical_or(z - other == 2, other - z == 2))
             def _():
-                arrived(kvall.at[span], k_recv.at[span])
+                for half in range(2):
+                    await_half(span, half)
                 turn(span)
 
     q_pair.wait()
     for copy in p_copies:
         copy.wait()
-    to_pair.wait_send()
-    for step, there, back, slot in sides:
-
-        @pl.when(there)
-        def _():
-            outward(slot, step, 0).wait_send()
-            outward(slot + 1, step, 1).wait_send()
-
-        @pl.when(jnp.logical_and(there, back))
-        def _():
-            for side in range(2):
-                onward(6 + slot + side, step, side).wait_send()
+    for half in range(2):
+        outward(8 + half, 0, 1, half).wait_send()
+        for step, there, back, slot in sides:
+
+            @pl.when(there)
+            def _():
+                outward(slot + 2 * half, step, 0, half).wait_send()
+                outward(slot + 2 * half + 1, step, 1, half).wait_send()
+
+            @pl.when(jnp.logical_and(there, back))
+            def _():
+                for side in range(2):
+                    onward(11 + slot + 2 * half + side, step, side, half).wait_send()
 
 
 def document_bounds(docs_ref, bounds, z):
@@ -692,7 +715,7 @@
             pltpu.VMEM((span, LANES), BF16),
             dma(7),
             dma(heads), dma(heads), dma(blks), dma(blks), dma(blks), dma(blks), dma(heads), dma(heads),
-            dma(10), dma(blks), pltpu.SemaphoreType.DMA,
+            dma(19), dma(blks, 2), pltpu.SemaphoreType.DMA,
         ],
         compiler_params=pltpu.CompilerParams(
             collective_id=1, has_side_effects=True, vmem_limit_bytes=16 * MIB
@@ -735,6 +758,7 @@
     key_tile = kv_ref.shape[1]
     total = q_ref.shape[0] * q_ref.shape[1]
     key_lanes = (lane_ids((QUERY_TILE, LANES)) < HALF) == (y == 0)
+    value_lanes = (lane_ids((HALF, LANES)) < HALF) == (y == 1)
     group_size = CHAINS * QUERY_TILE
     for group in range(total // group_size):
         tiles = range(group * CHAINS, (group + 1) * CHAINS)
@@ -766,7 +790,9 @@
         for tile, (biggest, weight, mixed) in zip(tiles, ends):
             result = jnp.transpose(mixed / weight)
             o_out[tile] = result
-            ob_out[tile] = result.astype(BF16)
+            for part in range(QUERY_TILE // LANES):
+                block = result[part * LANES : (part + 1) * LANES]
+                ob_out[tile, part] = halves(block, value_lanes).astype(BF16)
             lse_out[tile] = jnp.broadcast_to(biggest + jnp.log(weight), (8, QUERY_TILE))
 
 
@@ -777,7 +803,7 @@
         forward_kernel,
         out_shape=(
             jax.ShapeDtypeStruct((tiles, QUERY_TILE, LANES), F32),
-            jax.ShapeDtypeStruct((tiles, QUERY_TILE, LANES), BF16),
+            jax.ShapeDtypeStruct((tiles, QUERY_TILE // LANES, HALF, LANES), BF16),
             jax.ShapeDtypeStruct((tiles, 8, QUERY_TILE), F32),
         ),
         in_specs=vmem_specs(4),
@@ -801,8 +827,12 @@
         queries, out_grads, deltas, log_totals = [], [], [], []
         for tile in tiles:
             queries.append(masked_queries(q_ref, tile, key_lanes, QUERY_TILE))
-            out_grad = do_ref[tile]
-            out_grads.append(jnp.where(key_lanes, jnp.zeros_like(out_grad), out_grad))
+            parts = []
+            for part in range(QUERY_TILE // LANES):
+                packed = do_ref[tile, part].astype(F32)
+                parts += [packed, pltpu.roll(packed, HALF, 1)]
+            out_grad = jnp.concatenate(parts, axis=0)
+            out_grads.append(jnp.where(key_lanes, 0.0, out_grad).astype(BF16))
             product = jnp.transpose(out_grads[-1].astype(F32) * o_ref[tile])
             deltas.append(jnp.sum(product, axis=0, keepdims=True))
             log_totals.append(lse_ref[tile, 0:1, :])
@@ -849,7 +879,7 @@
         scratch_shapes=[pltpu.VMEM((blks, span, LANES), F32)],
         compiler_params=pltpu.CompilerParams(vmem_limit_bytes=16 * MIB),
         name="attend_back",
-    )(bounds, q, kv, kvt, d_o.reshape(tiles, QUERY_TILE, LANES), o, lse)
+    )(bounds, q, kv, kvt, d_o.reshape(tiles, QUERY_TILE // LANES, HALF, LANES), o, lse)
 
 
 def gelu_parts(values):
@@ -874,14 +904,26 @@
     return row, col
 
 
+def own_columns(rows_ref, turned, blk, capacity):
+    blks, _, slots = rows_ref.shape
+    rows = jnp.concatenate(
+        [rows_ref[...].reshape(blks, slots), jnp.zeros((LANES - blks, slots), F32)], axis=0
+    )
+    for piece in range(slots // LANES):
+        columns = slice(piece * LANES, (piece + 1) * LANES)
+        turned[columns, :] = jnp.transpose(rows[:, columns])
+    own = turned[pl.ds(pl.multiple_of(blk * capacity, capacity), capacity), :]
+    return jnp.concatenate([own[:, source : source + 1] for source in range(blks)], axis=0)
+
+
 def middle_kernel(
     heads, blks,
     x_hbm, o_ref, wo_ref, routes_hbm, rank_hbm, d_out_hbm, win_hbm, wout_hbm,
     out_ref, dh_ref, dma_all, grads_ref, rx,
     x_ref, routes_ref, rank_ref, d_out_ref, win_ref, wout_ref, rows_in, in_sem,
-    o_all, dos, doa, rs, ra, po, pa, dr, da, dms, acc_out, acc_row, mix,
+    o_all, dos, doa, rs, ra, po, pa, dr, da, dms, acc_out, acc_row, mix, gate_rows, d_gate_rows, turned,
     o_send, o_recv, dos_send, dos_recv, r_send, r_recv, po_send, po_recv,
-    dr_send, dr_recv, dm_send, dm_recv, rx_send, rx_recv,
+    dr_send, dr_recv, dm_send, dm_recv, rx_send, rx_recv, g_send, g_recv, dg_send, dg_recv,
 ):
     head, blk, z, y = place()
     tokens, model = x_ref.shape
@@ -897,10 +939,11 @@
     ]
     for copy in fetched:
         copy.start()
-    greet(
+    met = greet(
         [(around(head, kh, heads), 2 * z + around(y, ky, 2)) for kh, ky in plane]
         + [(head, around(blk, k, blks)) for k in range(1, blks)]
     )
+    meet(met)
 
     def plane_copies(src_of, dst, send, recv):
         copies = []
@@ -976,40 +1019,51 @@
     gain = small_across[blks : blks + 1, :]
 
     finish(o_copies)
+    low_lanes = lanes[:HALF] < HALF
     for piece in range(heads):
-        mix[:, piece * LANES : (piece + 1) * LANES] = jnp.where(
-            lanes < HALF, o_all[1, piece], o_all[0, piece]
-        )
+        columns = slice(piece * LANES, (piece + 1) * LANES)
+        first, second = o_all[1, piece].astype(F32), o_all[0, piece].astype(F32)
+        mix[:HALF, columns] = jnp.where(low_lanes, first, second).astype(BF16)
+        swapped = pltpu.roll(jnp.where(low_lanes, second, first), HALF, 1)
+        mix[HALF:, columns] = swapped.astype(BF16)
     mixed = mix[...]
     hidden = x_ref[...].astype(F32) + dot(mixed, weight_out)
     xhat, scale = centre(hidden)
     routed = (xhat * gain).astype(BF16)
+    rs[...] = dot(pick_any, routed).astype(BF16).reshape(rs.shape)
+    r_copies = blk_copies(rs, ra, r_send, r_recv)
+    start(r_copies)
+    ra[blk] = rs[blk]
     logits = jnp.where(lanes < blks, dot(routed, small), MASKED)
     powers = jnp.exp(logits - jnp.max(logits, axis=1, keepdims=True))
     probs = powers / jnp.sum(powers, axis=1, keepdims=True)
     lanes_f = lanes.astype(F32)
     hots = [lanes_f == e for e in e_cols]
     gates = [jnp.sum(jnp.where(hot, probs, 0.0), axis=1, keepdims=True) for hot in hots]
-    gate_mats = [split_high_low(g, lanes) for g in gates]
-
-    rs[:, :, 0:model] = dot(pick_any, routed).astype(BF16).reshape(blks, capacity, model)
-    rs[:, :, model : model + LANES] = (
-        (dot(pick[0], gate_mats[0]) + dot(pick[1], gate_mats[1]))
-        .astype(BF16)
-        .reshape(blks, capacity, LANES)
-    )
-    r_copies = blk_copies(rs, ra, r_send, r_recv)
-    start(r_copies)
-    ra[blk] = rs[blk]
+    gate_high = [g.astype(BF16).astype(F32) for g in gates]
+    gate_across = jnp.transpose(
+        jnp.where(lanes == 0, gate_high[0], jnp.where(lanes == 1, gates[0] - gate_high[0], 0.0))
+        + jnp.where(lanes == 2, gate_high[1], jnp.where(lanes == 3, gates[1] - gate_high[1], 0.0))
+    ).astype(BF16)
+    by_slot = (dot(gate_across, put[0]), dot(gate_across, put[1]))
+    gate_rows[blk] = by_slot[0][0:1] + by_slot[0][1:2] + by_slot[1][2:3] + by_slot[1][3:4]
+    g_copies = [
+        remote(
+            gate_rows.at[blk], gate_rows.at[blk],
+            g_send.at[k], g_recv.at[k], head, around(blk, k, blks),
+        )
+        for k in range(1, blks)
+    ]
+    start(g_copies)
     acc_out[...] = jnp.zeros_like(acc_out)
     acc_row[...] = jnp.zeros_like(acc_row)
     finish(dos_copies)
     finish(r_copies)
 
-    arrived_rows = ra[...].reshape(slots, model + LANES)
     out_rows = doa[...].reshape(slots, model)
-    gate_col = join_high_low(arrived_rows, model)
-    rx[head, :, 0:model] = arrived_rows[:, 0:model]
+    rx[head, :, 0:model] = ra[...].reshape(slots, model)
+    finish(g_copies)
+    gate_col = own_columns(gate_rows, turned, blk, capacity)
     rx[head, :, model : 2 * model] = (out_rows.astype(F32) * gate_col).astype(BF16)
     half_ff = wout_ref.shape[0] // 4
     for copy in fetched[4:]:
@@ -1027,13 +1081,23 @@
 
     result = acc_out[...].astype(BF16)
     d_gate = jnp.sum(out_rows.astype(F32) * result.astype(F32), axis=1, keepdims=True)
-    dr[:, :, 0:model] = acc_row[...].astype(BF16).reshape(blks, capacity, model)
-    dr[:, :, model : model + LANES] = split_high_low(d_gate, lane_ids((slots, LANES))).reshape(
-        blks, capacity, LANES
-    )
+    dr[...] = acc_row[...].astype(BF16).reshape(dr.shape)
     dr_copies = blk_copies(dr, da, dr_send, dr_recv)
     start(dr_copies)
     da[blk] = dr[blk]
+    d_wide = jnp.broadcast_to(d_gate, (slots, LANES))
+    d_gate_rows[blk] = jnp.concatenate(
+        [jnp.transpose(d_wide[i * LANES : (i + 1) * LANES])[0:1] for i in range(slots // LANES)],
+        axis=1,
+    )
+    dg_copies = [
+        remote(
+            d_gate_rows.at[blk], d_gate_rows.at[blk],
+            dg_send.at[k], dg_recv.at[k], head, around(blk, k, blks),
+        )
+        for k in range(1, blks)
+    ]
+    start(dg_copies)
     po[...] = result.reshape(blks, capacity, model)
     po_copies = blk_copies(po, pa, po_send, po_recv)
     pa[blk] = po[blk]
@@ -1044,26 +1108,29 @@
     to_across.start()
     to_sibling.start()
 
-    finish(dr_copies)
-    start(po_copies)
-    back = da[...].reshape(slots, model + LANES)
-    d_routed = dot(put_any, back[:, 0:model])
-    back_gate = back[:, model : model + LANES]
+    finish(dg_copies)
+    back_gate = own_columns(d_gate_rows, turned, blk, capacity)
+    back_gate = split_high_low(back_gate, lane_ids((slots, LANES)))
     d_gates = [join_high_low(dot(p, back_gate), 0) for p in put]
     d_probs = jnp.where(hots[0], d_gates[0], 0.0) + jnp.where(hots[1], d_gates[1], 0.0)
     d_logits = probs * (d_probs - jnp.sum(probs * d_probs, axis=1, keepdims=True))
     d_high = d_logits.astype(BF16)
     d_low = (d_logits - d_high.astype(F32)).astype(BF16)
-    d_routed = d_routed + dot(d_high, small, (1, 1)) + dot(d_low, small, (1, 1))
+    d_router_part = dot(d_high, small, (1, 1)) + dot(d_low, small, (1, 1))
+    finish(dr_copies)
+    start(po_copies)
+    d_routed = dot(put_any, da[...].reshape(slots, model)) + d_router_part
     d_hidden = d_out + centre_back(d_routed * gain, xhat, scale)
     dh_ref[...] = d_hidden
     d_attn = d_hidden.astype(BF16)
-    d_mixed = dot(d_attn, weight_out, (1, 1)).astype(BF16)
+    d_mixed = dot(d_attn, weight_out, (1, 1))
     for piece in range(heads):
-        dms[piece] = d_mixed[:, piece * LANES : (piece + 1) * LANES]
-    dm_copies = plane_copies(lambda to_y, to_head: dms.at[to_head], dma_all.at[y, head], dm_send, dm_recv)
+        block = d_mixed[:, piece * LANES : (piece + 1) * LANES]
+        for to_y in range(2):
+            dms[to_y, piece] = halves(block, low_lanes == (to_y == 1)).astype(BF16)
+    dm_copies = plane_copies(lambda to_y, to_head: dms.at[to_y, to_head], dma_all.at[y, head], dm_send, dm_recv)
     start(dm_copies)
-    dma_all[y, head] = dms[head]
+    dma_all[y, head] = dms[y, head]
 
     d_weight = dot(mixed, d_attn, (0, 0)).astype(BF16)
     for b in range(blks):
@@ -1095,14 +1162,14 @@
         return pltpu.VMEM((blks, capacity, width), BF16)
 
     def block(*lead):
-        return pltpu.VMEM((*lead, tokens, LANES), BF16)
+        return pltpu.VMEM((*lead, tokens // 2, LANES), BF16)
 
     return pl.pallas_call(
         functools.partial(middle_kernel, heads, blks),
         out_shape=(
             jax.ShapeDtypeStruct((tokens, model), BF16),
             jax.ShapeDtypeStruct((tokens, model), F32),
-            jax.ShapeDtypeStruct((2, heads, tokens, LANES), BF16),
+            jax.ShapeDtypeStruct((2, heads, tokens // 2, LANES), BF16),
             jax.ShapeDtypeStruct((blks, model // blks, wide), BF16),
             jax.ShapeDtypeStruct((heads, slots, 2 * model), BF16),
         ),
@@ -1117,12 +1184,15 @@
             pltpu.VMEM(wout.shape, BF16),
             pltpu.VMEM((tokens, tokens), F32),
             dma(6),
-            block(2, heads), rows(model), rows(model), rows(wide), rows(wide), rows(model), rows(model),
-            rows(wide), rows(wide), block(heads),
+            block(2, heads), rows(model), rows(model), rows(model), rows(model), rows(model), rows(model),
+            rows(model), rows(model), block(2, heads),
             pltpu.VMEM((slots, model), F32), pltpu.VMEM((slots, model), F32),
             pltpu.VMEM((tokens, model), BF16),
+            pltpu.VMEM((blks, 1, slots), F32), pltpu.VMEM((blks, 1, slots), F32),
+            pltpu.VMEM((slots, LANES), F32),
             dma(2 * heads), dma(2 * heads), dma(blks), dma(blks), dma(blks), dma(blks), dma(blks), dma(blks),
             dma(blks), dma(blks), dma(2 * heads), dma(2 * heads), dma(3), dma(3),
+            dma(blks), dma(blks), dma(blks), dma(blks),
         ],
         compiler_params=pltpu.CompilerParams(
             collective_id=2, has_side_effects=True, vmem_limit_bytes=20 * MIB
@@ -1153,10 +1223,11 @@
     ]
     for copy in fetched:
         copy.start()
-    greet(
+    met = greet(
         [(around(head, k, heads), blk) for k in range(1, heads)]
         + [(head, around(blk, k, blks)) for k in range(1, blks)]
     )
+    meet(met)
 
     def start(copies):
         for copy in copies:
@@ -1542,7 +1613,7 @@
     )
     o, o_low, lse = call_forward(bounds, q, kv, kvt)
     output, dh, d_o, grads, rx = call_middle(
-        inputs, o_low.reshape(2, heads, tokens, LANES), wo.reshape(model, model + LANES),
+        inputs, o_low.reshape(2, heads, tokens // 2, LANES), wo.reshape(model, model + LANES),
         routes, priority, d_out, win, wout, heads, blks,
     )
     dq, dkv = call_backward(bounds, q, kv, kvt, d_o, o, lse)

time: 133 us -> 129 us (0.970); the launches traced: 131 us -> 130 us
  Pallas kernels: 131 us -> 129 us
    pallas_call x1, Pallas kernels: 34.3 us -> 30.5 us  [call_qkv(): pl.pallas_call(functools.partial(qkv_kernel, heads, blks), out_shape=(jax...]
    pallas_call x1, Pallas kernels: 5.6 us -> 8.64 us  [call_backward(): pl.pallas_call(backward_kernel, out_shape=(jax.ShapeDtypeStruct((tiles, Q...]
    pallas_call x1, Pallas kernels: 42.9 us -> 40.4 us  [call_middle(): pl.pallas_call(functools.partial(middle_kernel, heads, blks), out_shape=(...]
    pallas_call x1, Pallas kernels: 4.29 us -> 6.69 us  [call_forward(): pl.pallas_call(forward_kernel, out_shape=(jax.ShapeDtypeStruct((tiles, QU...]
where the time goes in v4:
time: 129 us; the launch traced here: 130 us
  Pallas kernels  129 us (100%)
    pallas_call x1, Pallas kernels, call_middle(): pl.pallas_call(functools.partial(middle_kernel, heads, blks), out_shape=(...  40.4 us
    pallas_call x1, Pallas kernels, call_last(): pl.pallas_call(functools.partial(last_kernel, heads, blks), out_shape=(ja...  39.2 us
    pallas_call x1, Pallas kernels, call_qkv(): pl.pallas_call(functools.partial(qkv_kernel, heads, blks), out_shape=(jax...  30.5 us
    pallas_call x1, Pallas kernels, call_backward(): pl.pallas_call(backward_kernel, out_shape=(jax.ShapeDtypeStruct((tiles, Q...  8.64 us
    pallas_call x1, Pallas kernels, call_forward(): pl.pallas_call(forward_kernel, out_shape=(jax.ShapeDtypeStruct((tiles, QU...  6.69 us
    pallas_call x1, Pallas kernels, call_finish(): pl.pallas_call(functools.partial(finish_kernel, experts), out_shape=(jax....  3.75 us

profile of v4, /device:TPU:0, one launch (start us, length us, event | category | flops | bytes accessed | tf_op | source)
XLA Modules:
  0.0 130.0 jit_solution(16493636294865043375)
XLA Ops:
  0.6 30.5 %qkv.1 = (bf16[2,512,128]{2,1,0:T(8,128)(2,1)S(1)}, bf16[8,512,128]{2,1,0:T(8,128)(2,1)S(1)}, bf16[4,128,512]{2,1,0:T(8,128)(2,1)S(1)}, bf16[8,64,384]{2,1,0:T(8...) custom-call(bf16[128,512]{1,0:T(8,128)(2,1)} %x_hbm.5, ...), custom_call_target="tpu_custom_call" | custom-call | tf_op jit(solution)/shard_map/qkv/pallas_call | solution.py:693
  31.1 6.7 %attend.1 = (f32[4,256,128]{2,1,0:T(8,128)S(1)}, bf16[4,2,64,128]{3,2,1,0:T(8,128)(2,1)S(1)}, f32[4,8,256]{2,1,0:T(8,128)S(1)}) custom-call(s32[8,1024]{1,0:T(8,128)S(1)} %get-tuple-element.40.bounds_ref, bf16[2,512,128]{2,1,0:T(8,128)(2,1)S(1)} %get-tuple-element.41.q_ref, bf16[8,512,128]{2,1,0:T(8,128)(2,1)S(1)} %get-tuple-element.42.kv_ref, ...), custom_call_target="tpu_custom_call" | custom-call | tf_op jit(solution)/shard_map/attend/pallas_call | solution.py:802
  37.8 40.4 %experts.1 = (bf16[128,512]{1,0:T(8,128)(2,1)S(1)}, f32[128,512]{1,0:T(8,128)S(1)}, bf16[2,4,64,128]{3,2,1,0:T(8,128)(2,1)S(1)}, bf16[8,64,640]{2,1,0:T(8,128)(2,1)S(1)}, bf16[4,256,1024]{2,1,0:T(8,128)(2,1)S(1)}) custom-call(bf16[128,512]{1,0:T(8,128)(2,1)} %x_hbm.5, bf16[2,4,64,128]{3,2,1,0:T(8,128)(2,1)S(1)} %bitcast.21, bf16[512,640]{1,0:T(8,128)(2,1)S(1)} %bitcast.18, ...), custom_call_target="tpu_custom_call" | custom-call | tf_op jit(solution)/shard_map/experts/pallas_call | solution.py:1167
  78.2 8.6 %attend_back.1 = (bf16[4,256,128]{2,1,0:T(8,128)(2,1)S(1)}, bf16[8,512,128]{2,1,0:T(8,128)(2,1)S(1)}) custom-call(s32[8,1024]{1,0:T(8,128)S(1)} %get-tuple-element.40.bounds_ref, bf16[2,512,128]{2,1,0:T(8,128)(2,1)S(1)} %get-tuple-element.41.q_ref, bf16[8,512,128]{2,1,0:T(8,128)(2,1)S(1)} %get-tuple-element.42.kv_ref, ...), custom_call_target="tpu_custom_call" | custom-call | tf_op jit(solution)/shard_map/attend_back/pallas_call | solution.py:871
  86.9 39.2 %last.1 = (f32[128,512]{1,0:T(8,128)S(1)}, f32[64,1536]{1,0:T(8,128)S(1)}, f32[64,640]{1,0:T(8,128)S(1)}, bf16[2,512,1024]{2,1,0:T(8,128)(2,1)S(1)}, bf16[2,1024,512]{2,1,0:T(8,128)(2,1)S(1)}) custom-call(bf16[128,512]{1,0:T(8,128)(2,1)} %x_hbm.5, f32[128,512]{1,0:T(8,128)S(1)} %get-tuple-element.47.dh_ref, bf16[2,512,128]{2,1,0:T(8,128)(2,1)S(1)} %bitcast.19, ...), custom_call_target="tpu_custom_call" | custom-call | tf_op jit(solution)/shard_map/last/pallas_call | solution.py:1485
  126.1 3.7 %finish.1 = (bf16[128,512]{1,0:T(8,128)(2,1)}, f32[128,512]{1,0:T(8,128)}, f32[1,64]{1,0:T(1,128)}, f32[64,1536]{1,0:T(8,128)}, f32[64,512]{1,0:T(8,128)}, /*ind...) custom-call(bf16[128,512]{1,0:T(8,128)(2,1)S(1)} %get-tuple-element.46.y_ref, ...), custom_call_target="tpu_custom_call" | custom-call | tf_op jit(solution)/shard_map/finish/pallas_call | solution.py:1573

commit v5 on v4

--- a/solution.py
+++ b/solution.py
@@ -465,11 +465,90 @@
     return lax.rem(index + step, size)
 
 
+QUERY_TILE = 256
+CHAINS = 2
+
+
+def masked_queries(q_ref, tile, key_lanes, query_tile):
+    tiles_per_span = q_ref.shape[1] // query_tile
+    inner = tile % tiles_per_span * query_tile
+    query = q_ref[tile // tiles_per_span, inner : inner + query_tile, :]
+    return jnp.where(key_lanes, query, jnp.zeros_like(query))
+
+
+def group_blocks(bounds_ref, group, size, key_tile):
+    first, last = group * size, (group + 1) * size
+    low = jnp.min(bounds_ref[0:1, first : first + LANES])
+    high = jnp.max(bounds_ref[1:2, last - LANES : last])
+    return low // key_tile, (high + key_tile - 1) // key_tile
+
+
+def inside_document(bounds_ref, tile, first, shape):
+    key = first + lax.broadcasted_iota(jnp.int32, shape, 0)
+    columns = slice(tile * shape[1], (tile + 1) * shape[1])
+    return jnp.logical_and(key >= bounds_ref[0:1, columns], key < bounds_ref[1:2, columns])
+
+
+def query_group(q_ref, group, y):
+    key_lanes = (lane_ids((QUERY_TILE, LANES)) < HALF) == (y == 0)
+    tiles = range(group * CHAINS, (group + 1) * CHAINS)
+    return tiles, [masked_queries(q_ref, tile, key_lanes, QUERY_TILE) for tile in tiles]
+
+
+def attend(bounds_ref, tiles, first, keys, keys_across, queries, carry):
+    scores = [dot(keys, query, (1, 1)) for query in queries]
+    made = []
+    for tile, score, (biggest, weight, mixed) in zip(tiles, scores, carry):
+        inside = inside_document(bounds_ref, tile, first, score.shape)
+        score = jnp.where(inside, score, MASKED)
+        bigger = jnp.maximum(biggest, jnp.max(score, axis=0, keepdims=True))
+        fade = jnp.exp(biggest - bigger)
+        terms = jnp.exp(score - bigger)
+        weight = weight * fade + jnp.sum(terms, axis=0, keepdims=True)
+        made.append((bigger, weight, mixed * fade + dot(keys_across, terms.astype(BF16))))
+    return tuple(made)
+
+
+def nothing_attended():
+    return (
+        jnp.full((1, QUERY_TILE), MASKED, F32),
+        jnp.zeros((1, QUERY_TILE), F32),
+        jnp.zeros((LANES, QUERY_TILE), F32),
+    )
+
+
+def attend_back(bounds_ref, tiles, first, keys, keys_across, group, carry):
+    queries, out_grads, deltas, log_totals = group
+    scores = [dot(keys, query, (1, 1)) for query in queries]
+    weight_grads = [dot(keys, out_grad, (1, 1)) for out_grad in out_grads]
+    pieces, score_grads = [], []
+    for i, tile in enumerate(tiles):
+        inside = inside_document(bounds_ref, tile, first, scores[i].shape)
+        weights = jnp.exp(jnp.where(inside, scores[i], MASKED) - log_totals[i])
+        score_grads.append((weights * (weight_grads[i] - deltas[i])).astype(BF16))
+        pieces.append(weights.astype(BF16))
+    wide = jnp.concatenate(score_grads + pieces, axis=1)
+    given = dot(wide, jnp.concatenate(queries + out_grads, axis=0))
+    return given, tuple(c + dot(keys_across, g) for c, g in zip(carry, score_grads))
+
+
+def group_grads(do_ref, tiles, y):
+    key_lanes = (lane_ids((QUERY_TILE, LANES)) < HALF) == (y == 0)
+    out_grads = []
+    for tile in tiles:
+        parts = []
+        for part in range(QUERY_TILE // LANES):
+            packed = do_ref[tile, part].astype(F32)
+            parts += [packed, pltpu.roll(packed, HALF, 1)]
+        out_grads.append(jnp.where(key_lanes, 0.0, jnp.concatenate(parts, axis=0)).astype(BF16))
+    return out_grads
+
+
 def qkv_kernel(
     heads, blks,
     x_hbm, w_hbm, g1_hbm, wo_hbm, wr_hbm, g2_hbm, docs_hbm,
-    qall, kvall, xall, wall, wo_all, kvt, bounds,
-    x_ref, w_ref, rows_in, g1_ref, g2_ref, wr_ref, docs_ref, wo_own, kv_other, in_sem,
+    qall, kvall, xall, wall, wo_all, kvt, bounds, begun,
+    x_ref, w_ref, rows_in, g1_ref, g2_ref, wr_ref, docs_ref, wo_own, kv_other, q_packed, q_landed, in_sem,
     x_send, x_recv, w_send, w_recv, o_send, o_recv, p_send, p_recv,
     k_send, k_recv, q_recv,
 ):
@@ -535,13 +614,15 @@
         )
         for k in range(1, blks)
     ]
+    document_bounds(docs_ref, bounds, z)
+    for copy in w_copies:
+        copy.wait_send()
     for copy in o_copies:
         copy.start()
-    document_bounds(docs_ref, bounds, z)
     for copy in x_copies:
         copy.wait()
     for copy in w_copies:
-        copy.wait()
+        copy.wait_recv()
     weight = wall[...].reshape(model, 3 * LANES)
     tokens = x_ref.shape[0]
     even = y == 0
@@ -579,6 +660,7 @@
             kvall[blk, span, :] = jnp.where(even, first, second)
             kv_other[span, :] = jnp.where(even, second, first)
             qall[y, span, :] = made[:, 2 * LANES : 3 * LANES]
+        outward(8 + half, 0, 1, half).start()
         for step, there, _, slot in sides:
 
             @pl.when(there)
@@ -586,21 +668,25 @@
                 outward(slot + 2 * half, step, 0, half).start()
                 outward(slot + 2 * half + 1, step, 1, half).start()
 
-        outward(8 + half, 0, 1, half).start()
-    q_pair = remote(qall.at[y], qall.at[y], k_send.at[10], q_recv, head, 2 * z + around(y, 1, 2))
+    other_y = around(y, 1, 2)
+    kept = (lane_ids(q_packed.shape) < HALF) == (y == 1)
+    q_packed[...] = halves(qall[y].astype(F32), kept).astype(BF16)
+    q_pair = remote(q_packed, q_landed, k_send.at[10], q_recv, head, 2 * z + other_y)
     q_pair.start()
     turn(blk)
     for copy in o_copies:
         copy.wait()
-    p_copies = [
-        remote(
-            wo_all.at[:, head], wo_all.at[:, head],
-            p_send.at[k], p_recv.at[k], around(head, k, heads), blk,
-        )
-        for k in range(1, heads)
-    ]
+    core = lax.rem(head, 2)
+    sibling, across = head - core + 1 - core, around(head, 2, heads)
+
+    def quarter_copy(index, quarter, to_head):
+        ref = wo_all.at[:, quarter]
+        return remote(ref, ref, p_send.at[index], p_recv.at[index], to_head, blk)
+
+    p_copies = [quarter_copy(0, head, sibling), quarter_copy(1, head, across)]
     for copy in p_copies:
         copy.start()
+    p_copies.append(quarter_copy(2, across, sibling))
     for half in range(2):
         for step, there, back, slot in sides:
 
@@ -614,10 +700,28 @@
                 for side in range(2):
                     onward(11 + slot + 2 * half + side, step, side, half).start()
 
-    pair = 2 * z + around(y, 1, 2)
+    arrived(wo_all.at[:, across], p_recv.at[1])
+    p_copies[2].start()
+    pair = 2 * z + other_y
     for half in range(2):
         await_half(pair, half)
     turn(pair)
+    q_pair.wait()
+    landed = q_landed[...]
+    qall[other_y, 0:half_span, :] = landed
+    qall[other_y, half_span : 2 * half_span, :] = pltpu.roll(landed.astype(F32), HALF, 1).astype(BF16)
+    key_tile = kvall.shape[1]
+    for group in range(2 * key_tile // (CHAINS * QUERY_TILE)):
+        tiles, queries = query_group(qall, group, y)
+        carry = (nothing_attended(),) * CHAINS
+        for side in range(2):
+            first = pl.multiple_of((2 * z + side) * key_tile, key_tile)
+            keys_across = kvt[:, pl.ds(first, key_tile)]
+            carry = attend(bounds, tiles, first, kvall[2 * z + side], keys_across, queries, carry)
+        for tile, (biggest, weight, mixed) in zip(tiles, carry):
+            begun[tile, 0:LANES] = mixed
+            begun[tile, LANES : LANES + 8] = jnp.broadcast_to(biggest, (8, QUERY_TILE))
+            begun[tile, LANES + 8 : LANES + 16] = jnp.broadcast_to(weight, (8, QUERY_TILE))
     for step, there, back, slot in sides:
 
         @pl.when(back)
@@ -635,9 +739,10 @@
                     await_half(span, half)
                 turn(span)
 
-    q_pair.wait()
+    for index, quarter in ((0, sibling), (2, around(sibling, 2, heads))):
+        arrived(wo_all.at[:, quarter], p_recv.at[index])
     for copy in p_copies:
-        copy.wait()
+        copy.wait_send()
     for half in range(2):
         outward(8 + half, 0, 1, half).wait_send()
         for step, there, back, slot in sides:
@@ -700,9 +805,10 @@
             jax.ShapeDtypeStruct((blks, heads, part, wide), BF16),
             jax.ShapeDtypeStruct((LANES, blks * span), BF16),
             jax.ShapeDtypeStruct((8, 2 * span), jnp.int32),
+            jax.ShapeDtypeStruct((2 * span // QUERY_TILE, LANES + 16, QUERY_TILE), F32),
         ),
         in_specs=hbm_specs(7),
-        out_specs=tuple(vmem_specs(7)),
+        out_specs=tuple(vmem_specs(8)),
         scratch_shapes=[
             pltpu.VMEM((tokens, model), BF16),
             pltpu.VMEM((rows, 3 * model), BF16),
@@ -713,6 +819,8 @@
             pltpu.VMEM((1, doc_lengths.shape[0]), jnp.int32),
             pltpu.VMEM((rows, wide), BF16),
             pltpu.VMEM((span, LANES), BF16),
+            pltpu.VMEM((span // 2, LANES), BF16),
+            pltpu.VMEM((span // 2, LANES), BF16),
             dma(7),
             dma(heads), dma(heads), dma(blks), dma(blks), dma(blks), dma(blks), dma(heads), dma(heads),
             dma(19), dma(blks, 2), pltpu.SemaphoreType.DMA,
@@ -729,64 +837,29 @@
     )
 
 
-QUERY_TILE = 256
-CHAINS = 2
-
-
-def masked_queries(q_ref, tile, key_lanes, query_tile):
-    tiles_per_span = q_ref.shape[1] // query_tile
-    inner = tile % tiles_per_span * query_tile
-    query = q_ref[tile // tiles_per_span, inner : inner + query_tile, :]
-    return jnp.where(key_lanes, query, jnp.zeros_like(query))
-
-
-def group_blocks(bounds_ref, group, size, key_tile):
-    first, last = group * size, (group + 1) * size
-    low = jnp.min(bounds_ref[0:1, first : first + LANES])
-    high = jnp.max(bounds_ref[1:2, last - LANES : last])
-    return low // key_tile, (high + key_tile - 1) // key_tile
-
-
-def inside_document(bounds_ref, tile, first, shape):
-    key = first + lax.broadcasted_iota(jnp.int32, shape, 0)
-    columns = slice(tile * shape[1], (tile + 1) * shape[1])
-    return jnp.logical_and(key >= bounds_ref[0:1, columns], key < bounds_ref[1:2, columns])
-
-
-def forward_kernel(bounds_ref, q_ref, kv_ref, kvt_ref, o_out, ob_out, lse_out):
+def other_blocks(bounds_ref, group, key_tile, z, step, carry):
+    low, high = group_blocks(bounds_ref, group, CHAINS * QUERY_TILE, key_tile)
+    carry = lax.fori_loop(low, 2 * z, step, carry)
+    return lax.fori_loop(2 * z + 2, high, step, carry)
+
+
+def forward_kernel(bounds_ref, q_ref, kv_ref, kvt_ref, begun_ref, o_out, ob_out, lse_out):
     _, _, z, y = place()
     key_tile = kv_ref.shape[1]
-    total = q_ref.shape[0] * q_ref.shape[1]
-    key_lanes = (lane_ids((QUERY_TILE, LANES)) < HALF) == (y == 0)
     value_lanes = (lane_ids((HALF, LANES)) < HALF) == (y == 1)
-    group_size = CHAINS * QUERY_TILE
-    for group in range(total // group_size):
-        tiles = range(group * CHAINS, (group + 1) * CHAINS)
-        queries = [masked_queries(q_ref, tile, key_lanes, QUERY_TILE) for tile in tiles]
-        low, high = group_blocks(bounds_ref, group, group_size, key_tile)
+    for group in range(q_ref.shape[0] * q_ref.shape[1] // (CHAINS * QUERY_TILE)):
+        tiles, queries = query_group(q_ref, group, y)
 
         def step(block, carry, queries=queries, tiles=tiles):
             first = pl.multiple_of(block * key_tile, key_tile)
-            keys = kv_ref[block]
-            keys_across = kvt_ref[:, pl.ds(first, key_tile)]
-            scores = [dot(keys, query, (1, 1)) for query in queries]
-            made = []
-            for tile, score, (biggest, weight, mixed) in zip(tiles, scores, carry):
-                inside = inside_document(bounds_ref, tile, first, score.shape)
-                score = jnp.where(inside, score, MASKED)
-                bigger = jnp.maximum(biggest, jnp.max(score, axis=0, keepdims=True))
-                fade = jnp.exp(biggest - bigger)
-                terms = jnp.exp(score - bigger)
-                weight = weight * fade + jnp.sum(terms, axis=0, keepdims=True)
-                made.append((bigger, weight, mixed * fade + dot(keys_across, terms.astype(BF16))))
-            return tuple(made)
-
-        start = (
-            jnp.full((1, QUERY_TILE), MASKED, F32),
-            jnp.zeros((1, QUERY_TILE), F32),
-            jnp.zeros((LANES, QUERY_TILE), F32),
-        )
-        ends = lax.fori_loop(low, high, step, (start,) * CHAINS)
+            across = kvt_ref[:, pl.ds(first, key_tile)]
+            return attend(bounds_ref, tiles, first, kv_ref[block], across, queries, carry)
+
+        start = tuple(
+            (begun_ref[t, LANES : LANES + 1], begun_ref[t, LANES + 8 : LANES + 9], begun_ref[t, 0:LANES])
+            for t in tiles
+        )
+        ends = other_blocks(bounds_ref, group, key_tile, z, step, start)
         for tile, (biggest, weight, mixed) in zip(tiles, ends):
             result = jnp.transpose(mixed / weight)
             o_out[tile] = result
@@ -796,7 +869,7 @@
             lse_out[tile] = jnp.broadcast_to(biggest + jnp.log(weight), (8, QUERY_TILE))
 
 
-def call_forward(bounds, q, kv, kvt):
+def call_forward(bounds, q, kv, kvt, begun):
     blks, span, _ = kv.shape
     tiles = 2 * span // QUERY_TILE
     return pl.pallas_call(
@@ -806,61 +879,41 @@
             jax.ShapeDtypeStruct((tiles, QUERY_TILE // LANES, HALF, LANES), BF16),
             jax.ShapeDtypeStruct((tiles, 8, QUERY_TILE), F32),
         ),
-        in_specs=vmem_specs(4),
+        in_specs=vmem_specs(5),
         out_specs=tuple(vmem_specs(3)),
         compiler_params=pltpu.CompilerParams(vmem_limit_bytes=16 * MIB),
         name="attend",
-    )(bounds, q, kv, kvt)
+    )(bounds, q, kv, kvt, begun)
 
 
 def backward_kernel(
-    bounds_ref, q_ref, kv_ref, kvt_ref, do_ref, o_ref, lse_ref, dq_out, dkv_out, dkv
+    bounds_ref, q_ref, kv_ref, kvt_ref, do_ref, o_ref, lse_ref, dq_out, dkv_out, delta_out, dkv
 ):
     _, _, z, y = place()
     key_tile = kv_ref.shape[1]
-    total = q_ref.shape[0] * q_ref.shape[1]
     dkv[...] = jnp.zeros_like(dkv)
-    key_lanes = (lane_ids((QUERY_TILE, LANES)) < HALF) == (y == 0)
-    group_size = CHAINS * QUERY_TILE
-    for group in range(total // group_size):
-        tiles = range(group * CHAINS, (group + 1) * CHAINS)
-        queries, out_grads, deltas, log_totals = [], [], [], []
-        for tile in tiles:
-            queries.append(masked_queries(q_ref, tile, key_lanes, QUERY_TILE))
-            parts = []
-            for part in range(QUERY_TILE // LANES):
-                packed = do_ref[tile, part].astype(F32)
-                parts += [packed, pltpu.roll(packed, HALF, 1)]
-            out_grad = jnp.concatenate(parts, axis=0)
-            out_grads.append(jnp.where(key_lanes, 0.0, out_grad).astype(BF16))
-            product = jnp.transpose(out_grads[-1].astype(F32) * o_ref[tile])
+    for group in range(q_ref.shape[0] * q_ref.shape[1] // (CHAINS * QUERY_TILE)):
+        tiles, queries = query_group(q_ref, group, y)
+        out_grads = group_grads(do_ref, tiles, y)
+        deltas, log_totals = [], []
+        for tile, out_grad in zip(tiles, out_grads):
+            product = jnp.transpose(out_grad.astype(F32) * o_ref[tile])
             deltas.append(jnp.sum(product, axis=0, keepdims=True))
+            delta_out[tile] = jnp.broadcast_to(deltas[-1], delta_out.shape[1:])
             log_totals.append(lse_ref[tile, 0:1, :])
-        low, high = group_blocks(bounds_ref, group, group_size, key_tile)
-
-        def step(
-            block, carry, queries=queries, out_grads=out_grads, deltas=deltas,
-            log_totals=log_totals, tiles=tiles,
-        ):
+        known = (queries, out_grads, deltas, log_totals)
+
+        def step(block, carry, tiles=tiles, known=known):
             first = pl.multiple_of(block * key_tile, key_tile)
-            keys = kv_ref[block]
-            keys_across = kvt_ref[:, pl.ds(first, key_tile)]
-            scores = [dot(keys, query, (1, 1)) for query in queries]
-            weight_grads = [dot(keys, out_grad, (1, 1)) for out_grad in out_grads]
-            pieces, score_grads = [], []
-            for i, tile in enumerate(tiles):
-                inside = inside_document(bounds_ref, tile, first, scores[i].shape)
-                weights = jnp.exp(jnp.where(inside, scores[i], MASKED) - log_totals[i])
-                score_grads.append((weights * (weight_grads[i] - deltas[i])).astype(BF16))
-                pieces.append(weights.astype(BF16))
-            wide = jnp.concatenate(score_grads + pieces, axis=1)
-            dkv[block] += dot(wide, jnp.concatenate(queries + out_grads, axis=0))
-            return tuple(c + dot(keys_across, s) for c, s in zip(carry, score_grads))
+            across = kvt_ref[:, pl.ds(first, key_tile)]
+            given, carry = attend_back(bounds_ref, tiles, first, kv_ref[block], across, known, carry)
+            dkv[block] += given
+            return carry
 
         zero = jnp.zeros((LANES, QUERY_TILE), F32)
-        ends = lax.fori_loop(low, high, step, (zero,) * CHAINS)
+        ends = other_blocks(bounds_ref, group, key_tile, z, step, (zero,) * CHAINS)
         for tile, mixed in zip(tiles, ends):
-            dq_out[tile] = jnp.transpose(mixed).astype(BF16)
+            dq_out[tile] = mixed
     for block in range(dkv.shape[0]):
         dkv_out[block] = dkv[block].astype(BF16)
 
@@ -871,15 +924,16 @@
     return pl.pallas_call(
         backward_kernel,
         out_shape=(
-            jax.ShapeDtypeStruct((tiles, QUERY_TILE, LANES), BF16),
+            jax.ShapeDtypeStruct((tiles, LANES, QUERY_TILE), F32),
             jax.ShapeDtypeStruct((blks, span, LANES), BF16),
+            jax.ShapeDtypeStruct((tiles, 8, QUERY_TILE), F32),
         ),
         in_specs=vmem_specs(7),
-        out_specs=tuple(vmem_specs(2)),
+        out_specs=tuple(vmem_specs(3)),
         scratch_shapes=[pltpu.VMEM((blks, span, LANES), F32)],
         compiler_params=pltpu.CompilerParams(vmem_limit_bytes=16 * MIB),
         name="attend_back",
-    )(bounds, q, kv, kvt, d_o.reshape(tiles, QUERY_TILE // LANES, HALF, LANES), o, lse)
+    )(bounds, q, kv, kvt, d_o, o, lse)
 
 
 def gelu_parts(values):
@@ -919,10 +973,10 @@
 def middle_kernel(
     heads, blks,
     x_hbm, o_ref, wo_ref, routes_hbm, rank_hbm, d_out_hbm, win_hbm, wout_hbm,
-    out_ref, dh_ref, dma_all, grads_ref, rx,
+    po, hidden_ref, share_ref, dh_ref, dma_all, grads_ref, rx,
     x_ref, routes_ref, rank_ref, d_out_ref, win_ref, wout_ref, rows_in, in_sem,
-    o_all, dos, doa, rs, ra, po, pa, dr, da, dms, acc_out, acc_row, mix, gate_rows, d_gate_rows, turned,
-    o_send, o_recv, dos_send, dos_recv, r_send, r_recv, po_send, po_recv,
+    o_all, dos, doa, rs, ra, dr, da, dms, acc_out, acc_row, mix, gate_rows, d_gate_rows, turned,
+    o_send, o_recv, dos_send, dos_recv, r_send, r_recv,
     dr_send, dr_recv, dm_send, dm_recv, rx_send, rx_recv, g_send, g_recv, dg_send, dg_recv,
 ):
     head, blk, z, y = place()
@@ -1065,6 +1119,29 @@
     finish(g_copies)
     gate_col = own_columns(gate_rows, turned, blk, capacity)
     rx[head, :, model : 2 * model] = (out_rows.astype(F32) * gate_col).astype(BF16)
+    core = lax.rem(head, 2)
+    sibling, across = head - core + 1 - core, around(head, 2, heads)
+
+    def half_rows(source, half):
+        return rx.at[source, pl.ds(half * slots // 2, slots // 2)]
+
+    to_across = [
+        remote(
+            half_rows(head, half), half_rows(head, half),
+            rx_send.at[1 + half], rx_recv.at[1 + half], across, blk,
+        )
+        for half in range(2)
+    ]
+    to_sibling = remote(rx.at[head], rx.at[head], rx_send.at[0], rx_recv.at[0], sibling, blk)
+    forwards = [
+        remote(
+            half_rows(across, half), half_rows(across, half),
+            rx_send.at[3 + half], rx_recv.at[3 + half], sibling, blk,
+        )
+        for half in range(2)
+    ]
+    start(to_across)
+    to_sibling.start()
     half_ff = wout_ref.shape[0] // 4
     for copy in fetched[4:]:
         copy.wait()
@@ -1099,14 +1176,6 @@
     ]
     start(dg_copies)
     po[...] = result.reshape(blks, capacity, model)
-    po_copies = blk_copies(po, pa, po_send, po_recv)
-    pa[blk] = po[blk]
-    core = lax.rem(head, 2)
-    sibling, across = head - core + 1 - core, around(head, 2, heads)
-    to_sibling = remote(rx.at[head], rx.at[head], rx_send.at[0], rx_recv.at[0], sibling, blk)
-    to_across = remote(rx.at[head], rx.at[head], rx_send.at[1], rx_recv.at[1], across, blk)
-    to_across.start()
-    to_sibling.start()
 
     finish(dg_copies)
     back_gate = own_columns(d_gate_rows, turned, blk, capacity)
@@ -1118,7 +1187,6 @@
     d_low = (d_logits - d_high.astype(F32)).astype(BF16)
     d_router_part = dot(d_high, small, (1, 1)) + dot(d_low, small, (1, 1))
     finish(dr_copies)
-    start(po_copies)
     d_routed = dot(put_any, da[...].reshape(slots, model)) + d_router_part
     d_hidden = d_out + centre_back(d_routed * gain, xhat, scale)
     dh_ref[...] = d_hidden
@@ -1131,6 +1199,8 @@
     dm_copies = plane_copies(lambda to_y, to_head: dms.at[to_y, to_head], dma_all.at[y, head], dm_send, dm_recv)
     start(dm_copies)
     dma_all[y, head] = dms[y, head]
+    arrived(half_rows(across, 0), rx_recv.at[1])
+    forwards[0].start()
 
     d_weight = dot(mixed, d_attn, (0, 0)).astype(BF16)
     for b in range(blks):
@@ -1138,18 +1208,18 @@
     last = (lanes == blks).astype(BF16)
     d_small = dot(routed, d_high, (0, 0)) + dot((d_routed * xhat).astype(BF16), last, (0, 0))
     grads_ref[:, :, model : model + LANES] = d_small.astype(BF16).reshape(blks, HALF, LANES)
-    finish(po_copies)
-    parts = pa[...].reshape(slots, model)
-    mixture = gates[0] * dot(put[0], parts) + gates[1] * dot(put[1], parts)
-    out_ref[...] = (hidden + mixture).astype(BF16)
-
-    arrived(rx.at[across], rx_recv.at[1])
-    forward = remote(rx.at[across], rx.at[across], rx_send.at[2], rx_recv.at[2], sibling, blk)
-    forward.start()
+    share = gates[0] * put[0].astype(F32) + gates[1] * put[1].astype(F32)
+    share_ref[0] = share.astype(BF16)
+    share_ref[1] = (share - share_ref[0].astype(F32)).astype(BF16)
+    hidden_ref[...] = hidden
+
+    arrived(half_rows(across, 1), rx_recv.at[2])
+    forwards[1].start()
     finish(dm_copies)
     to_sibling.wait()
-    to_across.wait_send()
-    forward.wait()
+    for copy in to_across:
+        copy.wait_send()
+    finish(forwards)
 
 
 def call_middle(x, o, wo, routes, rank, d_out, win, wout, heads, blks):
@@ -1167,14 +1237,16 @@
     return pl.pallas_call(
         functools.partial(middle_kernel, heads, blks),
         out_shape=(
-            jax.ShapeDtypeStruct((tokens, model), BF16),
+            jax.ShapeDtypeStruct((blks, capacity, model), BF16),
+            jax.ShapeDtypeStruct((tokens, model), F32),
+            jax.ShapeDtypeStruct((2, tokens, slots), BF16),
             jax.ShapeDtypeStruct((tokens, model), F32),
             jax.ShapeDtypeStruct((2, heads, tokens // 2, LANES), BF16),
             jax.ShapeDtypeStruct((blks, model // blks, wide), BF16),
             jax.ShapeDtypeStruct((heads, slots, 2 * model), BF16),
         ),
         in_specs=hbm_specs(1) + vmem_specs(2) + hbm_specs(5),
-        out_specs=tuple(vmem_specs(5)),
+        out_specs=tuple(vmem_specs(7)),
         scratch_shapes=[
             pltpu.VMEM((tokens, model), BF16),
             pltpu.VMEM((2, tokens), jnp.int32),
@@ -1184,14 +1256,14 @@
             pltpu.VMEM(wout.shape, BF16),
             pltpu.VMEM((tokens, tokens), F32),
             dma(6),
-            block(2, heads), rows(model), rows(model), rows(model), rows(model), rows(model), rows(model),
+            block(2, heads), rows(model), rows(model), rows(model), rows(model),
             rows(model), rows(model), block(2, heads),
             pltpu.VMEM((slots, model), F32), pltpu.VMEM((slots, model), F32),
             pltpu.VMEM((tokens, model), BF16),
             pltpu.VMEM((blks, 1, slots), F32), pltpu.VMEM((blks, 1, slots), F32),
             pltpu.VMEM((slots, LANES), F32),
-            dma(2 * heads), dma(2 * heads), dma(blks), dma(blks), dma(blks), dma(blks), dma(blks), dma(blks),
-            dma(blks), dma(blks), dma(2 * heads), dma(2 * heads), dma(3), dma(3),
+            dma(2 * heads), dma(2 * heads), dma(blks), dma(blks), dma(blks), dma(blks),
+            dma(blks), dma(blks), dma(2 * heads), dma(2 * heads), dma(5), dma(5),
             dma(blks), dma(blks), dma(blks), dma(blks),
         ],
         compiler_params=pltpu.CompilerParams(
@@ -1203,13 +1275,14 @@
 
 def last_kernel(
     heads, blks,
-    x_hbm, dh_ref, dq_ref, dkv_ref, xa_ref, wa_ref, w_hbm, g1_hbm, grads_ref, rx_ref, win_hbm, wout_hbm,
-    dx_ref, dw_ref, shared_ref, din_ref, dout_ref,
+    x_hbm, dh_ref, begun_ref, dkv_ref, xa_ref, wa_ref, w_hbm, g1_hbm, grads_ref, rx_ref, win_hbm, wout_hbm,
+    po_ref, hidden_ref, share_ref, bounds_ref, q_ref, kv_ref, kvt_ref, do_ref, lse_ref, delta_ref,
+    y_ref, dx_ref, dw_ref, shared_ref, din_ref, dout_ref,
     x_ref, w_ref, g1_ref, win_ref, wout_ref, in_sem,
-    gain_tile, far_all, near_send_buf, near_all, pair_all, dq_all, us, ua, gs, ga, gh, w1, w2s, w2, w3,
+    gain_tile, far_all, near_send_buf, near_all, pair_all, dq_all, dq_ref, dq_packed, dkv_own, pair_buf, us, ua, gs, ga, gqs, gqa, u_part, xat, pa, gh, w1, w2s, w2, w3,
     q_send, q_recv, pair_send, pair_recv, far_send, far_recv, near_send, near_recv,
     u_send, u_recv, g_send, g_recv, gh_send, gh_recv, w1_send, w1_recv, w2_send, w2_recv,
-    w3_send, w3_recv, e_send, e_recv,
+    w3_send, w3_recv, e_send, e_recv, gq_send, gq_recv, po_send, po_recv,
 ):
     head, blk, z, y = place()
     planes = blks // 2
@@ -1265,10 +1338,6 @@
             for side in range(2):
                 far_copy(step, slot, side).start()
 
-    pair_copy = remote(dkv_ref.at[pair], pair_all, pair_send, pair_recv, head, pair)
-    pair_copy.start()
-    q_copy = remote(dq_ref.at[other_y], dq_all, q_send, q_recv, head, pair)
-    q_copy.start()
     w1_copies = [
         remote(
             grads_ref.at[:, around(head, k, heads)], w1.at[head],
@@ -1301,11 +1370,56 @@
         din_ref[core, :, pl.ds(there, ff_step)] = d_in.astype(BF16)
         dout_ref[core, pl.ds(there, ff_step), :] = d_out.astype(BF16)
 
-    finish(fetched)
-
-    @pl.loop(0, 2)
-    def _(chunk):
-        expert_chunk(chunk)
+    key_tile = kv_ref.shape[1]
+    for group in range(2 * key_tile // (CHAINS * QUERY_TILE)):
+        tiles, queries = query_group(q_ref, group, y)
+        known = (
+            queries,
+            group_grads(do_ref, tiles, y),
+            [delta_ref[tile, 0:1, :] for tile in tiles],
+            [lse_ref[tile, 0:1, :] for tile in tiles],
+        )
+        carry = tuple(begun_ref[tile] for tile in tiles)
+        for side in range(2):
+            first = pl.multiple_of((2 * z + side) * key_tile, key_tile)
+            keys_across = kvt_ref[:, pl.ds(first, key_tile)]
+            given, carry = attend_back(
+                bounds_ref, tiles, first, kv_ref[2 * z + side], keys_across, known, carry
+            )
+            dkv_own[side] = given if group == 0 else dkv_own[side] + given
+        for tile, total in zip(tiles, carry):
+            at = tile * QUERY_TILE % key_tile
+            dq_ref[tile * QUERY_TILE // key_tile, at : at + QUERY_TILE] = jnp.transpose(total)
+    pair_buf[...] = dkv_own[other_y].astype(BF16)
+    pair_copy = remote(pair_buf, pair_all, pair_send, pair_recv, head, pair)
+    pair_copy.start()
+    own_lanes = (lane_ids(dq_packed.shape) < HALF) == (y == 0)
+    dq_packed[...] = halves(dq_ref[other_y], own_lanes).astype(BF16)
+    q_copy = remote(dq_packed, dq_all, q_send, q_recv, head, pair)
+    q_copy.start()
+    finish(fetched[:2])
+    weight = wa_ref[...].reshape(model, 3 * LANES)
+    for piece in range(heads):
+        xat[:, piece * tokens : (piece + 1) * tokens] = jnp.transpose(xa_ref[piece])
+    even = y == 0
+
+    expert_chunk(0)
+    q_copy.wait()
+    landed = dq_all[...].astype(F32)
+    landed = jnp.concatenate([landed, pltpu.roll(landed, HALF, 1)], axis=0)
+    own_lanes = (lane_ids(landed.shape) < HALF) == even
+    q_grads = jnp.where(own_lanes, dq_ref[y], landed).astype(BF16)
+    gqs[...] = dot(xat[...], q_grads).astype(BF16).reshape(gqs.shape)
+    gq_copies = [
+        remote(
+            gqs.at[around(blk, k, blks)], gqa.at[blk],
+            gq_send.at[k], gq_recv.at[k], head, around(blk, k, blks),
+        )
+        for k in range(1, blks)
+    ]
+    start(gq_copies)
+    gqa[blk] = gqs[blk]
+    u_part[...] = dot(q_grads, weight[:, 2 * LANES : 3 * LANES], (1, 1)).reshape(u_part.shape)
 
     for step, there, back, slot in directions:
 
@@ -1326,68 +1440,6 @@
         def _():
             for side in range(2):
                 near_copy(step, slot, side).start()
-
-    @pl.loop(2, 4)
-    def _(chunk):
-        expert_chunk(chunk)
-
-    e_copies = [
-        remote(din_ref.at[core], din_ref.at[core], e_send.at[0], e_recv.at[0], sibling, blk),
-        remote(dout_ref.at[core], dout_ref.at[core], e_send.at[1], e_recv.at[1], sibling, blk),
-    ]
-    start(e_copies)
-
-    pair_copy.wait()
-    q_copy.wait()
-    for step, there, back, slot in directions:
-
-        @pl.when(back)
-        def _():
-            for side in range(2):
-                arrived(near_all.at[slot // 2, side], near_recv.at[slot // 2, side])
-
-        @pl.when(jnp.logical_not(back))
-        def _():
-            near_all[slot // 2] = jnp.zeros(near_all.shape[1:], BF16)
-
-    lanes = lane_ids((tokens, LANES))
-    even = y == 0
-    weight = wa_ref[...].reshape(model, 3 * LANES)
-    g_sum = jnp.zeros((model, 3 * LANES), F32)
-    for piece in range(heads):
-        span = slice(piece * tokens, (piece + 1) * tokens)
-        own = dkv_ref[blk, span, :].astype(F32)
-        other = pair_all[span, :].astype(F32)
-        kv_grads = [
-            jnp.where(even, own, other) + near_all[0, 0, span, :].astype(F32) + near_all[1, 0, span, :].astype(F32),
-            jnp.where(even, other, own) + near_all[0, 1, span, :].astype(F32) + near_all[1, 1, span, :].astype(F32),
-        ]
-        q_own = dq_ref[y, span, :]
-        q_other = dq_all[span, :]
-        own_lanes = (lanes < HALF) == even
-        q_grads = jnp.where(own_lanes, q_own, q_other)
-        made = jnp.concatenate([kv_grads[0].astype(BF16), kv_grads[1].astype(BF16), q_grads], axis=1)
-        us[piece] = dot(made, weight, (1, 1)).astype(BF16)
-        g_sum = g_sum + dot(xa_ref[piece], made, (0, 0))
-    u_copies = [
-        remote(
-            us.at[around(head, k, heads)], ua.at[head],
-            u_send.at[k], u_recv.at[k], around(head, k, heads), blk,
-        )
-        for k in range(1, heads)
-    ]
-    start(u_copies)
-    ua[head] = us[head]
-    gs[...] = g_sum.astype(BF16).reshape(gs.shape)
-    g_copies = [
-        remote(
-            gs.at[around(blk, k, blks)], ga.at[blk],
-            g_send.at[k], g_recv.at[k], head, around(blk, k, blks),
-        )
-        for k in range(1, blks)
-    ]
-    start(g_copies)
-    ga[blk] = gs[blk]
 
     finish(w1_copies)
     summed = w1[0].astype(F32)
@@ -1404,23 +1456,76 @@
     start(w2_copies)
     w2[blk] = w2s[blk]
 
-    finish(u_copies)
-    grad = ua[0].astype(F32)
-    for source in range(1, heads):
-        grad = grad + ua[source].astype(F32)
-    xhat, scale = centre(x_ref[...].astype(F32))
-    dx_ref[...] = dh_ref[...] + centre_back(grad, xhat, scale)
-
-    finish(g_copies)
-    total = ga[0].astype(F32)
-    for source in range(1, blks):
-        total = total + ga[source].astype(F32)
-    gh[head] = total.astype(BF16)
-    gh_copies = [
-        remote(gh.at[head], gh.at[head], gh_send.at[k], gh_recv.at[k], around(head, k, heads), blk)
+    @pl.loop(1, 4)
+    def _(chunk):
+        expert_chunk(chunk)
+
+    e_copies = [
+        remote(din_ref.at[core], din_ref.at[core], e_send.at[0], e_recv.at[0], sibling, blk),
+        remote(dout_ref.at[core], dout_ref.at[core], e_send.at[1], e_recv.at[1], sibling, blk),
+    ]
+    start(e_copies)
+
+    pair_copy.wait()
+    for step, there, back, slot in directions:
+
+        @pl.when(back)
+        def _():
+            for side in range(2):
+                arrived(near_all.at[slot // 2, side], near_recv.at[slot // 2, side])
+
+        @pl.when(jnp.logical_not(back))
+        def _():
+            near_all[slot // 2] = jnp.zeros(near_all.shape[1:], BF16)
+
+    own = dkv_own[y]
+    other = pair_all[...].astype(F32)
+    made = jnp.concatenate(
+        [
+            (
+                jnp.where(even == (side == 0), own, other)
+                + near_all[0, side].astype(F32)
+                + near_all[1, side].astype(F32)
+            ).astype(BF16)
+            for side in range(2)
+        ],
+        axis=1,
+    )
+    gs[...] = dot(xat[...], made).astype(BF16).reshape(gs.shape)
+    g_copies = [
+        remote(
+            gs.at[around(blk, k, blks)], ga.at[blk],
+            g_send.at[k], g_recv.at[k], head, around(blk, k, blks),
+        )
+        for k in range(1, blks)
+    ]
+    start(g_copies)
+    ga[blk] = gs[blk]
+    us[...] = (
+        u_part[...] + dot(made, weight[:, 0 : 2 * LANES], (1, 1)).reshape(us.shape)
+    ).astype(BF16)
+    u_copies = [
+        remote(
+            us.at[around(head, k, heads)], ua.at[head],
+            u_send.at[k], u_recv.at[k], around(head, k, heads), blk,
+        )
         for k in range(1, heads)
     ]
-    start(gh_copies)
+    start(u_copies)
+    ua[head] = us[head]
+    finish(fetched[2:])
+    for copy in g_copies:
+        copy.wait_send()
+    po_copies = [
+        remote(
+            po_ref.at[around(blk, k, blks)], pa.at[blk],
+            po_send.at[k], po_recv.at[k], head, around(blk, k, blks),
+        )
+        for k in range(1, blks)
+    ]
+    start(po_copies)
+    pa[blk] = po_ref[blk]
+
     finish(w2_copies)
     part = w2[0].astype(F32)
     for source in range(1, blks):
@@ -1431,6 +1536,34 @@
         for k in range(1, heads)
     ]
     start(w3_copies)
+
+    finish(u_copies)
+    grad = ua[0].astype(F32)
+    for source in range(1, heads):
+        grad = grad + ua[source].astype(F32)
+    xhat, scale = centre(x_ref[...].astype(F32))
+    dx_ref[...] = dh_ref[...] + centre_back(grad, xhat, scale)
+
+    finish(gq_copies)
+    total = gqa[0].astype(F32)
+    for source in range(1, blks):
+        total = total + gqa[source].astype(F32)
+    gh[head, :, 2 * LANES : 3 * LANES] = total.astype(BF16)
+    for copy in g_copies:
+        copy.wait_recv()
+    total = ga[0].astype(F32)
+    for source in range(1, blks):
+        total = total + ga[source].astype(F32)
+    gh[head, :, 0 : 2 * LANES] = total.astype(BF16)
+    gh_copies = [
+        remote(gh.at[head], gh.at[head], gh_send.at[k], gh_recv.at[k], around(head, k, heads), blk)
+        for k in range(1, heads)
+    ]
+    start(gh_copies)
+    finish(po_copies)
+    parts = pa[...].reshape(share_ref.shape[2], model)
+    mixture = dot(share_ref[0], parts) + dot(share_ref[1], parts)
+    y_ref[...] = (hidden_ref[...] + mixture).astype(BF16)
 
     gain_tile[...] = jnp.zeros_like(gain_tile)
     gain_tile[0:1, 0:rows] = g1_ref[...].astype(F32)
@@ -1471,7 +1604,10 @@
     finish(e_copies)
 
 
-def call_last(x, dh, dq, dkv, xa, wa, w_qkv, g1, grads, rx, win, wout, heads, blks):
+def call_last(
+    x, dh, dq, dkv, xa, wa, w_qkv, g1, grads, rx, win, wout, po, hidden, share,
+    bounds, q, kv, kvt, d_o, lse, delta, heads, blks,
+):
     tokens, model = x.shape
     span = tokens * heads
     rows = w_qkv.shape[0]
@@ -1485,14 +1621,15 @@
     return pl.pallas_call(
         functools.partial(last_kernel, heads, blks),
         out_shape=(
+            jax.ShapeDtypeStruct((tokens, model), BF16),
             jax.ShapeDtypeStruct((tokens, model), F32),
             jax.ShapeDtypeStruct((rows, 3 * model), F32),
             jax.ShapeDtypeStruct((rows, wide), F32),
             jax.ShapeDtypeStruct((2, model, ff // 2), BF16),
             jax.ShapeDtypeStruct((2, ff // 2, model), BF16),
         ),
-        in_specs=hbm_specs(1) + vmem_specs(5) + hbm_specs(2) + vmem_specs(2) + hbm_specs(2),
-        out_specs=tuple(vmem_specs(5)),
+        in_specs=hbm_specs(1) + vmem_specs(5) + hbm_specs(2) + vmem_specs(2) + hbm_specs(2) + vmem_specs(10),
+        out_specs=tuple(vmem_specs(6)),
         scratch_shapes=[
             pltpu.VMEM((tokens, model), BF16),
             pltpu.VMEM((rows, 3 * model), BF16),
@@ -1501,24 +1638,30 @@
             pltpu.VMEM(wout.shape, BF16),
             dma(5),
             pltpu.VMEM((8, LANES), F32),
-            block(4), block(4), block(2, 2), block(), block(),
+            block(4), block(4), block(2, 2), block(), pltpu.VMEM((span // 2, LANES), BF16),
+            pltpu.VMEM((2, span, LANES), F32), pltpu.VMEM((span // 2, LANES), BF16),
+            pltpu.VMEM((2, span, LANES), F32), block(),
             pltpu.VMEM((heads, tokens, model), BF16), pltpu.VMEM((heads, tokens, model), BF16),
-            pltpu.VMEM((blks, rows, 3 * LANES), BF16), pltpu.VMEM((blks, rows, 3 * LANES), BF16),
+            pltpu.VMEM((blks, rows, 2 * LANES), BF16), pltpu.VMEM((blks, rows, 2 * LANES), BF16),
+            pltpu.VMEM((blks, rows, LANES), BF16), pltpu.VMEM((blks, rows, LANES), BF16),
+            pltpu.VMEM((heads, tokens, model), F32), pltpu.VMEM((model, span), BF16),
+            pltpu.VMEM(po.shape, BF16),
             pltpu.VMEM((heads, rows, 3 * LANES), BF16),
             pltpu.VMEM((heads, blks, part, wide), BF16), pltpu.VMEM((blks, part, wide), BF16),
             pltpu.VMEM((blks, part, wide), BF16), pltpu.VMEM((heads, part, wide), BF16),
             pltpu.SemaphoreType.DMA, pltpu.SemaphoreType.DMA, pltpu.SemaphoreType.DMA, pltpu.SemaphoreType.DMA,
             dma(4), dma(4), dma(4), dma(2, 2),
             dma(heads), dma(heads), dma(blks), dma(blks), dma(heads), dma(heads), dma(heads), dma(heads),
-            dma(blks), dma(blks), dma(heads), dma(heads), dma(2), dma(2),
+            dma(blks), dma(blks), dma(heads), dma(heads), dma(2), dma(2), dma(blks), dma(blks), dma(blks), dma(blks),
         ],
         compiler_params=pltpu.CompilerParams(
             collective_id=3, has_side_effects=True, vmem_limit_bytes=24 * MIB
         ),
         name="last",
     )(
-        *in_hbm(x), dh, dq.reshape(2, span, LANES), dkv, xa, wa, *in_hbm(w_qkv, g1.reshape(1, rows)),
-        grads.reshape(blks, heads, part, wide), rx, *in_hbm(win, wout),
+        *in_hbm(x), dh, dq, dkv, xa, wa, *in_hbm(w_qkv, g1.reshape(1, rows)),
+        grads.reshape(blks, heads, part, wide), rx, *in_hbm(win, wout), po, hidden, share,
+        bounds, q, kv, kvt, d_o, lse, delta,
     )
 
 
@@ -1608,19 +1751,21 @@
     model = inputs.shape[1]
     tokens = inputs.shape[0]
     win, wout = expert_in[0], expert_out[0]
-    q, kv, xa, wa, wo, kvt, bounds = call_qkv(
+    q, kv, xa, wa, wo, kvt, bounds, begun = call_qkv(
         inputs, w_qkv, ln1_gain, w_out, w_router, ln2_gain, doc_lengths, heads, blks
     )
-    o, o_low, lse = call_forward(bounds, q, kv, kvt)
-    output, dh, d_o, grads, rx = call_middle(
+    o, o_low, lse = call_forward(bounds, q, kv, kvt, begun)
+    po, hidden, share, dh, d_o, grads, rx = call_middle(
         inputs, o_low.reshape(2, heads, tokens // 2, LANES), wo.reshape(model, model + LANES),
         routes, priority, d_out, win, wout, heads, blks,
     )
-    dq, dkv = call_backward(bounds, q, kv, kvt, d_o, o, lse)
+    d_o = d_o.reshape(2 * heads * tokens // QUERY_TILE, -1, HALF, LANES)
+    dq, dkv, delta = call_backward(bounds, q, kv, kvt, d_o, o, lse)
     ends = call_last(
-        inputs, dh, dq, dkv, xa, wa, w_qkv, ln1_gain, grads, rx, win, wout, heads, blks
-    )
-    output, d_inputs, d_gain_one, d_qkv, d_out_proj, d_gain_two, d_router, d_in, d_out_weight = call_finish(output, *ends)
+        inputs, dh, dq, dkv, xa, wa, w_qkv, ln1_gain, grads, rx, win, wout,
+        po, hidden, share, bounds, q, kv, kvt, d_o, lse, delta, heads, blks,
+    )
+    output, d_inputs, d_gain_one, d_qkv, d_out_proj, d_gain_two, d_router, d_in, d_out_weight = call_finish(*ends)
     return (
         output,
         d_inputs,

time: 129 us -> 122 us (0.946)
  Pallas kernels: 129 us -> 122 us
    pallas_call x1, Pallas kernels: 8.64 us -> 2.03 us  [call_backward(): pl.pallas_call(backward_kernel, out_shape=(jax.ShapeDtypeStruct((tiles, L...]
    pallas_call x1, Pallas kernels: 6.69 us -> 1.6 us  [call_forward(): pl.pallas_call(forward_kernel, out_shape=(jax.ShapeDtypeStruct((tiles, QU...]
    pallas_call x1, Pallas kernels: 39.2 us -> 43.4 us  [call_last(): pl.pallas_call(functools.partial(last_kernel, heads, blks), out_shape=(ja...]
where the time goes in v5:
time: 122 us; the launch traced here: 123 us
  Pallas kernels  122 us (100%)
    pallas_call x1, Pallas kernels, call_last(): pl.pallas_call(functools.partial(last_kernel, heads, blks), out_shape=(ja...  43.4 us
    pallas_call x1, Pallas kernels, call_middle(): pl.pallas_call(functools.partial(middle_kernel, heads, blks), out_shape=(...  39.6 us
    pallas_call x1, Pallas kernels, call_qkv(): pl.pallas_call(functools.partial(qkv_kernel, heads, blks), out_shape=(jax...  31.3 us
    pallas_call x1, Pallas kernels, call_finish(): pl.pallas_call(functools.partial(finish_kernel, experts), out_shape=(jax....  3.75 us

profile of v5, /device:TPU:0, one launch (start us, length us, event | category | flops | bytes accessed | tf_op | source)
XLA Modules:
  0.0 122.5 jit_solution(10968124742041551796)
XLA Ops:
  0.6 31.3 %qkv.1 = (bf16[2,512,128]{2,1,0:T(8,128)(2,1)S(1)}, bf16[8,512,128]{2,1,0:T(8,128)(2,1)S(1)}, bf16[4,128,512]{2,1,0:T(8,128)(2,1)S(1)}, bf16[8,64,384]{2,1,0:T(8...) custom-call(bf16[128,512]{1,0:T(8,128)(2,1)} %x_hbm.5, ...), custom_call_target="tpu_custom_call" | custom-call | tf_op jit(solution)/shard_map/qkv/pallas_call | solution.py:798
  31.9 1.6 %attend.1 = (f32[4,256,128]{2,1,0:T(8,128)S(1)}, bf16[4,2,64,128]{3,2,1,0:T(8,128)(2,1)S(1)}, f32[4,8,256]{2,1,0:T(8,128)S(1)}) custom-call(s32[8,1024]{1,0:T(8,128)S(1)} %get-tuple-element.45.bounds_ref, bf16[2,512,128]{2,1,0:T(8,128)(2,1)S(1)} %get-tuple-element.46.q_ref, bf16[8,512,128]{2,1,0:T(8,128)(2,1)S(1)} %get-tuple-element.47.kv_ref, ...), custom_call_target="tpu_custom_call" | custom-call | tf_op jit(solution)/shard_map/attend/pallas_call | solution.py:875
  33.5 39.6 %experts.1 = (bf16[8,32,512]{2,1,0:T(8,128)(2,1)S(1)}, f32[128,512]{1,0:T(8,128)S(1)}, bf16[2,128,256]{2,1,0:T(8,128)(2,1)S(1)}, f32[128,512]{1,0:T(8,128)S(1)},...) custom-call(bf16[128,512]{1,0:T(8,128)(2,1)} %x_hbm.5, ...), custom_call_target="tpu_custom_call" | custom-call | tf_op jit(solution)/shard_map/experts/pallas_call | solution.py:1237
  73.1 2.0 %attend_back.1 = (f32[4,128,256]{2,1,0:T(8,128)S(1)}, bf16[8,512,128]{2,1,0:T(8,128)(2,1)S(1)}, f32[4,8,256]{2,1,0:T(8,128)S(1)}) custom-call(s32[8,1024]{1,0:T(8,128)S(1)} %get-tuple-element.45.bounds_ref, bf16[2,512,128]{2,1,0:T(8,128)(2,1)S(1)} %get-tuple-element.46.q_ref, bf16[8,512,128]{2,1,0:T(8,128)(2,1)S(1)} %get-tuple-element.47.kv_ref, ...), custom_call_target="tpu_custom_call" | custom-call | tf_op jit(solution)/shard_map/attend_back/pallas_call | solution.py:924
  75.2 43.4 %last.1 = (bf16[128,512]{1,0:T(8,128)(2,1)S(1)}, f32[128,512]{1,0:T(8,128)S(1)}, f32[64,1536]{1,0:T(8,128)S(1)}, f32[64,640]{1,0:T(8,128)S(1)}, bf16[2,512,1024]...) custom-call(bf16[128,512]{1,0:T(8,128)(2,1)} %x_hbm.5, f32[128,512]{1,0:T(8,128)S(1)} %get-tuple-element.52.dh_ref, ...), custom_call_target="tpu_custom_call" | custom-call | tf_op jit(solution)/shard_map/last/pallas_call | solution.py:1621
  118.6 3.7 %finish.1 = (bf16[128,512]{1,0:T(8,128)(2,1)}, f32[128,512]{1,0:T(8,128)}, f32[1,64]{1,0:T(1,128)}, f32[64,1536]{1,0:T(8,128)}, f32[64,512]{1,0:T(8,128)}, /*ind...) custom-call(bf16[128,512]{1,0:T(8,128)(2,1)S(1)} %get-tuple-element.66.y_ref, ...), custom_call_target="tpu_custom_call" | custom-call | tf_op jit(solution)/shard_map/finish/pallas_call | solution.py:1716

commit v6 on v5

--- a/solution.py
+++ b/solution.py
@@ -1397,13 +1397,37 @@
     dq_packed[...] = halves(dq_ref[other_y], own_lanes).astype(BF16)
     q_copy = remote(dq_packed, dq_all, q_send, q_recv, head, pair)
     q_copy.start()
+    for step, there, back, slot in directions:
+
+        @pl.when(there)
+        def _():
+            for side in range(2):
+                near_send_buf[slot + side] = dkv_ref[2 * (z + step) + side]
+
+        @pl.when(jnp.logical_and(there, back))
+        def _():
+            for side in range(2):
+                arrived(far_all.at[slot + side], far_recv.at[slot + side])
+                near_send_buf[slot + side] = (
+                    near_send_buf[slot + side].astype(F32) + far_all[slot + side].astype(F32)
+                ).astype(BF16)
+
+        @pl.when(there)
+        def _():
+            for side in range(2):
+                near_copy(step, slot, side).start()
+
     finish(fetched[:2])
     weight = wa_ref[...].reshape(model, 3 * LANES)
     for piece in range(heads):
         xat[:, piece * tokens : (piece + 1) * tokens] = jnp.transpose(xa_ref[piece])
     even = y == 0
 
-    expert_chunk(0)
+
+    @pl.loop(0, 2)
+    def _(chunk):
+        expert_chunk(chunk)
+
     q_copy.wait()
     landed = dq_all[...].astype(F32)
     landed = jnp.concatenate([landed, pltpu.roll(landed, HALF, 1)], axis=0)
@@ -1421,26 +1445,6 @@
     gqa[blk] = gqs[blk]
     u_part[...] = dot(q_grads, weight[:, 2 * LANES : 3 * LANES], (1, 1)).reshape(u_part.shape)
 
-    for step, there, back, slot in directions:
-
-        @pl.when(there)
-        def _():
-            for side in range(2):
-                near_send_buf[slot + side] = dkv_ref[2 * (z + step) + side]
-
-        @pl.when(jnp.logical_and(there, back))
-        def _():
-            for side in range(2):
-                arrived(far_all.at[slot + side], far_recv.at[slot + side])
-                near_send_buf[slot + side] = (
-                    near_send_buf[slot + side].astype(F32) + far_all[slot + side].astype(F32)
-                ).astype(BF16)
-
-        @pl.when(there)
-        def _():
-            for side in range(2):
-                near_copy(step, slot, side).start()
-
     finish(w1_copies)
     summed = w1[0].astype(F32)
     for source in range(1, heads):
@@ -1456,7 +1460,7 @@
     start(w2_copies)
     w2[blk] = w2s[blk]
 
-    @pl.loop(1, 4)
+    @pl.loop(2, 4)
     def _(chunk):
         expert_chunk(chunk)
 
@@ -1514,17 +1518,6 @@
     start(u_copies)
     ua[head] = us[head]
     finish(fetched[2:])
-    for copy in g_copies:
-        copy.wait_send()
-    po_copies = [
-        remote(
-            po_ref.at[around(blk, k, blks)], pa.at[blk],
-            po_send.at[k], po_recv.at[k], head, around(blk, k, blks),
-        )
-        for k in range(1, blks)
-    ]
-    start(po_copies)
-    pa[blk] = po_ref[blk]
 
     finish(w2_copies)
     part = w2[0].astype(F32)
@@ -1537,20 +1530,13 @@
     ]
     start(w3_copies)
 
-    finish(u_copies)
-    grad = ua[0].astype(F32)
-    for source in range(1, heads):
-        grad = grad + ua[source].astype(F32)
     xhat, scale = centre(x_ref[...].astype(F32))
-    dx_ref[...] = dh_ref[...] + centre_back(grad, xhat, scale)
-
     finish(gq_copies)
     total = gqa[0].astype(F32)
     for source in range(1, blks):
         total = total + gqa[source].astype(F32)
     gh[head, :, 2 * LANES : 3 * LANES] = total.astype(BF16)
-    for copy in g_copies:
-        copy.wait_recv()
+    finish(g_copies)
     total = ga[0].astype(F32)
     for source in range(1, blks):
         total = total + ga[source].astype(F32)
@@ -1560,10 +1546,20 @@
         for k in range(1, heads)
     ]
     start(gh_copies)
-    finish(po_copies)
-    parts = pa[...].reshape(share_ref.shape[2], model)
-    mixture = dot(share_ref[0], parts) + dot(share_ref[1], parts)
-    y_ref[...] = (hidden_ref[...] + mixture).astype(BF16)
+    po_copies = [
+        remote(
+            po_ref.at[around(blk, k, blks)], pa.at[blk],
+            po_send.at[k], po_recv.at[k], head, around(blk, k, blks),
+        )
+        for k in range(1, blks)
+    ]
+    start(po_copies)
+    pa[blk] = po_ref[blk]
+    finish(u_copies)
+    grad = ua[0].astype(F32)
+    for source in range(1, heads):
+        grad = grad + ua[source].astype(F32)
+    dx_ref[...] = dh_ref[...] + centre_back(grad, xhat, scale)
 
     gain_tile[...] = jnp.zeros_like(gain_tile)
     gain_tile[0:1, 0:rows] = g1_ref[...].astype(F32)
@@ -1589,6 +1585,11 @@
     shared_ref[:, model : model + LANES] = jnp.where(
         lane_ids((rows, LANES)) == blks + 1, gain_col, shared[:, model : model + LANES]
     )
+    finish(po_copies)
+    parts = pa[...].reshape(share_ref.shape[2], model)
+    mixture = dot(share_ref[0], parts) + dot(share_ref[1], parts)
+    y_ref[...] = (hidden_ref[...] + mixture).astype(BF16)
+
     for step, there, back, slot in directions:
 
         @pl.when(two_away(step))

time: 122 us -> 119 us (0.975)
  Pallas kernels: 122 us -> 118 us
    pallas_call x1, Pallas kernels: 43.4 us -> 36 us  [call_last(): pl.pallas_call(functools.partial(last_kernel, heads, blks), out_shape=(ja...]
    pallas_call x1, Pallas kernels: 2.03 us -> 6.92 us  [call_backward(): pl.pallas_call(backward_kernel, out_shape=(jax.ShapeDtypeStruct((tiles, L...]
    pallas_call x1, Pallas kernels: 39.6 us -> 35.2 us  [call_middle(): pl.pallas_call(functools.partial(middle_kernel, heads, blks), out_shape=(...]
    pallas_call x1, Pallas kernels: 1.6 us -> 5.37 us  [call_forward(): pl.pallas_call(forward_kernel, out_shape=(jax.ShapeDtypeStruct((tiles, QU...]
where the time goes in v6:
time: 119 us
  Pallas kernels  118 us (99%)
    pallas_call x1, Pallas kernels, call_last(): pl.pallas_call(functools.partial(last_kernel, heads, blks), out_shape=(ja...  36 us
    pallas_call x1, Pallas kernels, call_middle(): pl.pallas_call(functools.partial(middle_kernel, heads, blks), out_shape=(...  35.2 us
    pallas_call x1, Pallas kernels, call_qkv(): pl.pallas_call(functools.partial(qkv_kernel, heads, blks), out_shape=(jax...  31.3 us
    pallas_call x1, Pallas kernels, call_backward(): pl.pallas_call(backward_kernel, out_shape=(jax.ShapeDtypeStruct((tiles, L...  6.92 us
    pallas_call x1, Pallas kernels, call_forward(): pl.pallas_call(forward_kernel, out_shape=(jax.ShapeDtypeStruct((tiles, QU...  5.37 us
    pallas_call x1, Pallas kernels, call_finish(): pl.pallas_call(functools.partial(finish_kernel, experts), out_shape=(jax....  3.75 us

profile of v6, /device:TPU:0, one launch (start us, length us, event | category | flops | bytes accessed | tf_op | source)
XLA Modules:
  0.0 119.3 jit_solution(11873376876975924409)
XLA Ops:
  0.6 31.3 %qkv.1 = (bf16[2,512,128]{2,1,0:T(8,128)(2,1)S(1)}, bf16[8,512,128]{2,1,0:T(8,128)(2,1)S(1)}, bf16[4,128,512]{2,1,0:T(8,128)(2,1)S(1)}, bf16[8,64,384]{2,1,0:T(8...) custom-call(bf16[128,512]{1,0:T(8,128)(2,1)} %x_hbm.5, ...), custom_call_target="tpu_custom_call" | custom-call | tf_op jit(solution)/shard_map/qkv/pallas_call | solution.py:798
  31.9 5.4 %attend.1 = (f32[4,256,128]{2,1,0:T(8,128)S(1)}, bf16[4,2,64,128]{3,2,1,0:T(8,128)(2,1)S(1)}, f32[4,8,256]{2,1,0:T(8,128)S(1)}) custom-call(s32[8,1024]{1,0:T(8,128)S(1)} %get-tuple-element.45.bounds_ref, bf16[2,512,128]{2,1,0:T(8,128)(2,1)S(1)} %get-tuple-element.46.q_ref, bf16[8,512,128]{2,1,0:T(8,128)(2,1)S(1)} %get-tuple-element.47.kv_ref, ...), custom_call_target="tpu_custom_call" | custom-call | tf_op jit(solution)/shard_map/attend/pallas_call | solution.py:875
  37.3 35.2 %experts.1 = (bf16[8,32,512]{2,1,0:T(8,128)(2,1)S(1)}, f32[128,512]{1,0:T(8,128)S(1)}, bf16[2,128,256]{2,1,0:T(8,128)(2,1)S(1)}, f32[128,512]{1,0:T(8,128)S(1)},...) custom-call(bf16[128,512]{1,0:T(8,128)(2,1)} %x_hbm.5, ...), custom_call_target="tpu_custom_call" | custom-call | tf_op jit(solution)/shard_map/experts/pallas_call | solution.py:1237
  72.5 6.9 %attend_back.1 = (f32[4,128,256]{2,1,0:T(8,128)S(1)}, bf16[8,512,128]{2,1,0:T(8,128)(2,1)S(1)}, f32[4,8,256]{2,1,0:T(8,128)S(1)}) custom-call(s32[8,1024]{1,0:T(8,128)S(1)} %get-tuple-element.45.bounds_ref, bf16[2,512,128]{2,1,0:T(8,128)(2,1)S(1)} %get-tuple-element.46.q_ref, bf16[8,512,128]{2,1,0:T(8,128)(2,1)S(1)} %get-tuple-element.47.kv_ref, ...), custom_call_target="tpu_custom_call" | custom-call | tf_op jit(solution)/shard_map/attend_back/pallas_call | solution.py:924
  79.4 36.0 %last.1 = (bf16[128,512]{1,0:T(8,128)(2,1)S(1)}, f32[128,512]{1,0:T(8,128)S(1)}, f32[64,1536]{1,0:T(8,128)S(1)}, f32[64,640]{1,0:T(8,128)S(1)}, bf16[2,512,1024]...) custom-call(bf16[128,512]{1,0:T(8,128)(2,1)} %x_hbm.5, f32[128,512]{1,0:T(8,128)S(1)} %get-tuple-element.52.dh_ref, ...), custom_call_target="tpu_custom_call" | custom-call | tf_op jit(solution)/shard_map/last/pallas_call | solution.py:1622
  115.4 3.7 %finish.1 = (bf16[128,512]{1,0:T(8,128)(2,1)}, f32[128,512]{1,0:T(8,128)}, f32[1,64]{1,0:T(1,128)}, f32[64,1536]{1,0:T(8,128)}, f32[64,512]{1,0:T(8,128)}, /*ind...) custom-call(bf16[128,512]{1,0:T(8,128)(2,1)S(1)} %get-tuple-element.66.y_ref, ...), custom_call_target="tpu_custom_call" | custom-call | tf_op jit(solution)/shard_map/finish/pallas_call | solution.py:1717
